TPU v7x, 128 devices: a whole 4x4x4 slice. The times are simulated.
128 devices in a mesh: dp: 4 (over z), expert: 32 (over y, x, core).
Axes of the slice: x: 4, y: 4, z: 4, core: 2. Of those that a mesh axis runs over, the one named last changes fastest.
Arguments:
- tokens: bfloat16 [16384, 2560], P(('dp', 'expert')), may hold values from -6 to 6
- expert_ids: int32 [16384, 6], P(('dp', 'expert')), may hold values from 0 to 31, as said below
- gate_values: float32 [16384, 6], P(('dp', 'expert')), may hold values from 0.05 to 0.5
- w_gate: bfloat16 [32, 2560, 768], P('expert'), may hold values from -0.125 to 0.125
- w_up: bfloat16 [32, 2560, 768], P('expert'), may hold values from -0.125 to 0.125
- w_down: bfloat16 [32, 768, 2560], P('expert'), may hold values from -0.21875 to 0.21875
Outputs:
- moe_out: bfloat16 [16384, 2560], P(('dp', 'expert'))
Inputs may be any that keep to these rules, and one draw needn't show every extreme that they name: `expert_ids`: within each block of 128 rows (one device's tokens), column 0 of every row holds one of two experts that are the same for all devices of a dp group, each of them in 56 to 72 rows, and no other entry names them; the two experts of different dp groups are different; the entries of a row differ; any other expert is named by at most 33 rows of one device, and in every dp group one such expert is named by exactly 33 rows of each of its devices; in some dp group other than the first, one of the two is named by 72 rows of every device, and that expert is named by exactly 33 rows of every device of the first dp group.
All inputs are finite; a program needn't handle non-finite values.
Results may differ from a plain program's by a relative error of at most 0.0058.
Values may be sent and summed in bfloat16 or wider, within the bound.
A program may use at most 128 MiB of HBM per device.

v0:
```python
import jax
import jax.numpy as jnp
from jax import lax
from jax.sharding import PartitionSpec as P


def expert_apply(row_block, gate_matrix, up_matrix, down_matrix):
    gate_part = jnp.dot(row_block, gate_matrix, preferred_element_type=jnp.float32)
    up_part = jnp.dot(row_block, up_matrix, preferred_element_type=jnp.float32)
    hidden = (jax.nn.silu(gate_part) * up_part).astype(jnp.bfloat16)
    return jnp.dot(hidden, down_matrix, preferred_element_type=jnp.float32).astype(jnp.bfloat16)


def local_experts(received, w_gate, w_up, w_down):
    local_count = w_gate.shape[0]
    sources = received.shape[0] // local_count
    slot_count = received.shape[1]
    features = received.shape[2]
    grouped = received.reshape(sources, local_count, slot_count, features)
    row_block = grouped[:, 0].reshape(-1, features)
    answer = expert_apply(row_block, w_gate[0], w_up[0], w_down[0])
    results = [answer.reshape(sources, slot_count, features)]
    return jnp.stack(results, axis=1).reshape(received.shape)


def dispatch_pairs(source, pair_rows, pair_ids, kept_pairs, slot_bound, w_gate, w_up, w_down):
    source_count, features = source.shape
    experts_all = lax.axis_size("expert") * w_gate.shape[0]
    one_hot = (
        (pair_ids[:, None] == jnp.arange(experts_all, dtype=jnp.int32)[None, :])
        & kept_pairs[:, None]
    ).astype(jnp.int32)
    earlier = jnp.cumsum(one_hot, axis=0) - one_hot
    slot_of = jnp.sum(earlier * one_hot, axis=1)
    padded_source = jnp.concatenate([source, jnp.zeros((1, features), source.dtype)], axis=0)
    buffer_rows = experts_all * slot_bound
    places = pair_ids * slot_bound + slot_of
    places = jnp.where(kept_pairs, places, buffer_rows)
    slot_table = (
        jnp.full((buffer_rows,), source_count, jnp.int32).at[places].set(pair_rows, mode="drop")
    )
    outgoing = padded_source[slot_table].reshape(experts_all, slot_bound, features)
    answered = local_experts(
        lax.all_to_all(outgoing, "expert", split_axis=0, concat_axis=0, tiled=True),
        w_gate,
        w_up,
        w_down,
    )
    returned = lax.all_to_all(answered, "expert", split_axis=0, concat_axis=0, tiled=True)
    flat_back = returned.reshape(buffer_rows, features)
    return flat_back[jnp.minimum(places, buffer_rows - 1)]


def shards(tokens, expert_ids, gate_values, w_gate, w_up, w_down):
    token_count, features = tokens.shape
    topk_width = expert_ids.shape[1]
    local_count = w_gate.shape[0]
    experts_all = lax.axis_size("expert") * local_count
    flat_ids = expert_ids.reshape(-1)
    flat_gates = gate_values.reshape(-1)
    pair_count = flat_ids.shape[0]
    owner_rows = jnp.arange(pair_count, dtype=jnp.int32) // topk_width
    other_bound = min(
        token_count,
        ((topk_width - 1) * token_count + experts_all - 3) // (experts_all - 2) * 3 // 2,
    )
    favoured_bound = token_count * 9 // 16
    kept_pairs = jnp.ones(flat_ids.shape, jnp.bool_)
    slot_bound = max(favoured_bound, other_bound)
    returned = dispatch_pairs(
        tokens, owner_rows, flat_ids, kept_pairs, slot_bound, w_gate, w_up, w_down
    )
    weighted = (flat_gates[:, None] * returned.astype(jnp.float32)).reshape(
        token_count, topk_width, features
    )
    summed = jnp.sum(weighted, axis=1)
    return summed.astype(jnp.bfloat16)


def solution(mesh):
    placed = (
        P(("dp", "expert"), None),
        P(("dp", "expert"), None),
        P(("dp", "expert"), None),
        P("expert", None, None),
        P("expert", None, None),
        P("expert", None, None),
    )
    return jax.shard_map(
        shards, mesh=mesh, in_specs=placed, out_specs=P(("dp", "expert"), None), check_vma=False
    )
```

profile of v0, /device:TPU:0, one launch (start us, length us, event | category | flops | bytes accessed | tf_op | source)
XLA Modules:
  0.0 394.3 jit_solution(10220775935737215812)
XLA Ops:
  0.0 0.8 copy.10
  0.8 0.1 eq.29
  0.9 0.1 eq.25
  1.1 0.7 broadcast_multiply_fusion
  1.8 1.7 reduce-window.6
  3.5 0.3 slice_reduce_fusion
  3.8 0.1 copy.9
  3.9 0.1 mul.42
  4.1 0.1 fusion.8
  4.2 3.4 scatter_custom_fusion
  7.7 1.1 concatenate.3
  8.8 10.7 %gather_fusion = bf16[2304,2560]{1,0:T(8,128)(2,1)} fusion(bf16[129,2560]{1,0:T(8,128)(2,1)S(1)} %concatenate.3, s32[3072]{0:T(1024)S(1)} %pad_clamp_fusion), kind=kCustom, calls=%fused_computation | custom fusion | bytes 23602176 | tf_op jit(solution)/shard_map/gather | solution.py:42
  19.5 0.0 copy-start.2
  19.5 140.2 %all_to_all.10 = bf16[32,72,2560]{2,1,0:T(8,128)(2,1)S(1)} all-to-all(bf16[32,72,2560]{2,1,0:T(8,128)(2,1)} %bitcast.36), channel_id=1, replica_groups=mesh['dp'=4,'expert'=32] {'expert'}, dimensions={0} | all-to-all | bytes 23592960 | tf_op jit(solution)/shard_map/all_to_all | solution.py:44
  159.6 0.0 copy-start
  159.7 4.3 %copy-done = bf16[32,72,2560]{2,1,0:T(8,128)(2,1)} copy-done((bf16[32,72,2560]{2,1,0:T(8,128)(2,1)}, bf16[32,72,2560]{2,1,0:T(8,128)(2,1)S(1)}, u32[]{:S(2)}) %copy-start) | copy-done | bytes 11796504
  163.9 0.0 copy-done.2
  163.9 11.4 %fusion.3 = f32[2304,768]{1,0:T(8,128)} fusion(bf16[2304,2560]{1,0:T(8,128)(2,1)S(1)} %bitcast.38, bf16[1,2560,768]{2,1,0:T(8,128)(2,1)S(1)} %copy-done.2), kind=kOutput, calls=%fused_computation.8 | convolution fusion | flops 9059696640 | bytes 22806528 | tf_op jit(solution)/shard_map/dot_general | solution.py:8
  175.4 31.7 %convolution_convert_fusion = bf16[2304,2560]{1,0:T(8,128)(2,1)} fusion(f32[2304,768]{1,0:T(8,128)} %fusion.3, bf16[2304,2560]{1,0:T(8,128)(2,1)} %bitcast.39, bf16[1,768,2560]{2,1,0:T(8,128)(2,1)} %param.11, bf16[1,2560,768]{2,1,0:T(8,128)(2,1)} %param.10), kind=kOutput, calls=%fused_computation.3 | convolution fusion | flops 18135908352 | bytes 38535168 | tf_op jit(solution)/shard_map/dot_general | solution.py:11
  207.1 0.0 copy-start.1
  207.1 6.2 %all-to-all-start.1 = ((bf16[32,72,2560]{2,1,0:T(8,128)(2,1)}), bf16[32,72,2560]{2,1,0:T(8,128)(2,1)}, u32[]{:S(2)}, u32[]{:S(2)}) async-start(bf16[32,72,2560]{2,1,0:T(8,128)(2,1)} %bitcast.37), calls=%async_computation.1 | async-start | bytes 23592960 | tf_op jit(solution)/shard_map/all_to_all | solution.py:49
  213.3 0.0 copy-done.1
  213.3 0.1 copy.8
  213.4 150.1 %all-to-all-done.1 = bf16[32,72,2560]{2,1,0:T(8,128)(2,1)} async-done(((bf16[32,72,2560]{2,1,0:T(8,128)(2,1)}), bf16[32,72,2560]{2,1,0:T(8,128)(2,1)}, u32[]{:S(2)}, u32[]{:S(2)}) %all-to-all-start.1) | async-done | bytes 11796512 | tf_op jit(solution)/shard_map/all_to_all | solution.py:49
  363.5 14.2 %gather_fusion.1 = bf16[768,2560]{1,0:T(8,128)(2,1)} fusion(bf16[2304,2560]{1,0:T(8,128)(2,1)} %bitcast.7, s32[1024]{0:T(1024)S(1)} %pad_clamp_fusion.1), kind=kCustom, calls=%fused_computation.1 | custom fusion | bytes 7867392 | tf_op jit(solution)/shard_map/gather | solution.py:51
  377.7 7.7 %reshape.85 = f32[128,6,2560]{2,1,0:T(8,128)} reshape(bf16[768,2560]{1,0:T(8,128)(2,1)} %gather_fusion.1) | data formatting | bytes 11796480 | tf_op jit(solution)/shard_map/convert_element_type | solution.py:73
  385.5 8.8 %multiply_reduce_fusion = bf16[128,2560]{1,0:T(8,128)(2,1)} fusion(f32[128,6,2560]{2,1,0:T(8,128)} %reshape.85, f32[128,6]{1,0:T(8,128)S(1)} %copy.8), kind=kLoop, calls=%fused_computation.4 | loop fusion | flops 3604480 | bytes 8522752 | tf_op jit(solution)/shard_map/reduce_sum | solution.py:76
  (7 shorter events, 0.1 us)
Async XLA Ops:
  19.5 144.4 %copy-start.2 = (bf16[1,2560,768]{2,1,0:T(8,128)(2,1)S(1)}, bf16[1,2560,768]{2,1,0:T(8,128)(2,1)}, u32[]{:S(2)}) copy-start(bf16[1,2560,768]{2,1,0:T(8,128)(2,1)} %param.9) | copy-start | bytes 11796484
  159.6 4.3 %copy-start = (bf16[32,72,2560]{2,1,0:T(8,128)(2,1)}, bf16[32,72,2560]{2,1,0:T(8,128)(2,1)S(1)}, u32[]{:S(2)}) copy-start(bf16[32,72,2560]{2,1,0:T(8,128)(2,1)S(1)} %all_to_all.10) | copy-start | bytes 35389444
  207.1 6.2 %copy-start.1 = (f32[128,6]{0,1:T(8,128)S(1)}, f32[128,6]{0,1:T(8,128)}, u32[]{:S(2)}) copy-start(f32[128,6]{0,1:T(8,128)} %param.8) | copy-start | bytes 9220
  207.1 156.4 %all-to-all-start.1 = ((bf16[32,72,2560]{2,1,0:T(8,128)(2,1)}), bf16[32,72,2560]{2,1,0:T(8,128)(2,1)}, u32[]{:S(2)}, u32[]{:S(2)}) async-start(bf16[32,72,2560]{2,1,0:T(8,128)(2,1)} %bitcast.37), calls=%async_computation.1 | async-start | bytes 23592960 | tf_op jit(solution)/shard_map/all_to_all | solution.py:49
where the time goes:
time: 395 us; the launch traced here: 394 us
  waiting for transfers between devices  150 us (38%)
  blocking collectives  140 us (35%)
  matrix products  43.2 us (11%)
  local copies, waits for them, and re-layouts  43.1 us (11%)
  other arithmetic  11.5 us (3%)
  starting transfers between devices  6.17 us (2%)
    all_to_all x1, waiting for transfers between devices, dispatch_pairs(): lax.all_to_all(answered, 'expert', split_axis=0, concat_axis=0, tiled=True)  150 us
    all_to_all x1, blocking collectives, dispatch_pairs(): lax.all_to_all(outgoing, 'expert', split_axis=0, concat_axis=0, tiled=True)  140 us
    dot_general x1, matrix products, expert_apply(): jnp.dot(hidden, down_matrix, preferred_element_type=jnp.float32)  31.7 us
    gather x1, local copies, waits for them, and re-layouts, dispatch_pairs(): return flat_back[jnp.minimum(places, buffer_rows - 1)]  14.2 us
    dot_general x1, matrix products, expert_apply(): jnp.dot(row_block, gate_matrix, preferred_element_type=jnp.float32)  11.4 us
    gather x1, local copies, waits for them, and re-layouts, dispatch_pairs(): padded_source[slot_table].reshape(experts_all, slot_bound, features)  10.7 us
    reduce_sum x1, other arithmetic, shards(): summed = jnp.sum(weighted, axis=1)  8.82 us
  transfers between devices with their start and end apart: 1, of which 1 were waited for; matrix products, arithmetic and copies ran while one was open for 0% of the time, Pallas kernels for 0%

commit v1 on v0

v1 whole, which is shorter than its diff:
```python
import jax
import jax.numpy as jnp
from jax import lax
from jax.sharding import PartitionSpec as P


def expert_apply(row_block, gate_matrix, up_matrix, down_matrix):
    gate_part = jnp.dot(row_block, gate_matrix, preferred_element_type=jnp.float32)
    up_part = jnp.dot(row_block, up_matrix, preferred_element_type=jnp.float32)
    hidden = (jax.nn.silu(gate_part) * up_part).astype(jnp.bfloat16)
    return jnp.dot(hidden, down_matrix, preferred_element_type=jnp.float32).astype(jnp.bfloat16)


def split_bf16(values):
    first = values.astype(jnp.bfloat16)
    rest = values - first.astype(jnp.float32)
    second = rest.astype(jnp.bfloat16)
    third = (rest - second.astype(jnp.float32)).astype(jnp.bfloat16)
    return first, second, third


def shards(tokens, expert_ids, gate_values, w_gate, w_up, w_down):
    token_count, features = tokens.shape
    topk_width = expert_ids.shape[1]
    local_count = w_gate.shape[0]
    experts_all = lax.axis_size("expert") * local_count
    other_bound = min(
        token_count,
        ((topk_width - 1) * token_count + experts_all - 3) // (experts_all - 2) * 3 // 2,
    )
    favoured_bound = token_count * 9 // 16
    slot_bound = max(favoured_bound, other_bound)
    buffer_rows = experts_all * slot_bound

    flat_ids = expert_ids.reshape(-1)
    one_hot = (flat_ids[:, None] == jnp.arange(experts_all, dtype=jnp.int32)[None, :]).astype(
        jnp.int32
    )
    earlier = jnp.cumsum(one_hot, axis=0) - one_hot
    slot_of = jnp.sum(earlier * one_hot, axis=1)
    places = (flat_ids * slot_bound + slot_of).reshape(token_count, topk_width)

    hit = places[:, :, None] == jnp.arange(buffer_rows, dtype=jnp.int32)[None, None, :]
    pick = jnp.any(hit, axis=1).astype(jnp.bfloat16)
    outgoing = jnp.einsum(
        "tr,td->rd", pick, tokens, preferred_element_type=jnp.float32
    ).astype(jnp.bfloat16)

    received = lax.all_to_all(
        outgoing.reshape(experts_all, slot_bound, features),
        "expert",
        split_axis=0,
        concat_axis=0,
        tiled=True,
    )
    answered = expert_apply(
        received.reshape(buffer_rows, features), w_gate[0], w_up[0], w_down[0]
    )
    returned = lax.all_to_all(
        answered.reshape(experts_all, slot_bound, features),
        "expert",
        split_axis=0,
        concat_axis=0,
        tiled=True,
    ).reshape(buffer_rows, features)

    weights = jnp.sum(jnp.where(hit, gate_values[:, :, None], 0.0), axis=1)
    summed = None
    for part in split_bf16(weights):
        term = jnp.dot(part, returned, preferred_element_type=jnp.float32)
        summed = term if summed is None else summed + term
    return summed.astype(jnp.bfloat16)


def solution(mesh):
    placed = (
        P(("dp", "expert"), None),
        P(("dp", "expert"), None),
        P(("dp", "expert"), None),
        P("expert", None, None),
        P("expert", None, None),
        P("expert", None, None),
    )
    return jax.shard_map(
        shards, mesh=mesh, in_specs=placed, out_specs=P(("dp", "expert"), None), check_vma=False
    )
```

time: 395 us -> 373 us (0.944)
  local copies, waits for them, and re-layouts: 43.1 us -> 5.86 us
  matrix products: 43.2 us -> 66 us
  other arithmetic: 11.5 us -> 5.09 us
    gather x2 -> x0, local copies, waits for them, and re-layouts: 24.9 us -> none  [the longest x1 14.2 us: dispatch_pairs(): return flat_back[jnp.minimum(places, buffer_rows - 1)]]
    dot_general x0 -> x4, matrix products: none -> 22.8 us  [the longest x3 19.3 us: shards(): term = jnp.dot(part, returned, preferred_element_type=jnp.float32)]
    reduce_sum x2, other arithmetic: 8.93 us -> 1.18 us  [the longest x1 1.07 us: shards(): weights = jnp.sum(jnp.where(hit, gate_values[:, :, None], 0.0), axis=1)]
    convert_element_type x1 -> x0, local copies, waits for them, and re-layouts: 7.73 us -> none  [shards(): returned.astype(jnp.float32)]
where the time goes in v1:
time: 373 us; the launch traced here: 372 us
  waiting for transfers between devices  149 us (40%)
  blocking collectives  140 us (38%)
  matrix products  66 us (18%)
  starting transfers between devices  6.22 us (2%)
  local copies, waits for them, and re-layouts  5.86 us (2%)
  other arithmetic  5.09 us (1%)
    all_to_all x1, waiting for transfers between devices, shards(): lax.all_to_all(answered.reshape(experts_all, slot_bound, features), 'expe...  149 us
    all_to_all x1, blocking collectives, shards(): lax.all_to_all(outgoing.reshape(experts_all, slot_bound, features), 'expe...  140 us
    dot_general x1, matrix products, expert_apply(): jnp.dot(hidden, down_matrix, preferred_element_type=jnp.float32)  31.7 us
    dot_general x3, matrix products, shards(): term = jnp.dot(part, returned, preferred_element_type=jnp.float32)  19.3 us
    dot_general x1, matrix products, expert_apply(): jnp.dot(row_block, gate_matrix, preferred_element_type=jnp.float32)  11.4 us
  transfers between devices with their start and end apart: 1, of which 1 were waited for; matrix products, arithmetic and copies ran while one was open for 0% of the time, Pallas kernels for 0%

profile of v1, /device:TPU:0, one launch (start us, length us, event | category | flops | bytes accessed | tf_op | source)
XLA Modules:
  0.0 372.4 jit_solution(5481896021074570551)
XLA Ops:
  0.0 0.0 copy-start
  0.0 0.9 copy.21
  0.9 0.1 eq.42
  1.0 0.1 eq.38
  1.2 1.7 reduce-window.6
  2.9 0.3 slice_reduce_fusion
  3.2 0.1 fusion.14
  3.3 0.1 reduce_sum.21
  3.4 0.1 copy.24
  3.5 0.7 multiply_add_fusion
  4.2 1.4 fusion
  5.6 0.0 copy-done
  5.7 3.5 convolution_convert_fusion.1
  9.2 0.0 copy-start.4
  9.2 140.0 %all_to_all.10 = bf16[32,72,2560]{2,1,0:T(8,128)(2,1)S(1)} all-to-all(bf16[32,72,2560]{2,1,0:T(8,128)(2,1)S(1)} %bitcast.41), channel_id=1, replica_groups=mesh['dp'=4,'expert'=32] {'expert'}, dimensions={0} | all-to-all | bytes 23592960 | tf_op jit(solution)/shard_map/all_to_all | solution.py:49
  149.1 0.0 copy-start.2
  149.2 4.3 %copy-done.2 = bf16[32,72,2560]{2,1,0:T(8,128)(2,1)} copy-done((bf16[32,72,2560]{2,1,0:T(8,128)(2,1)}, bf16[32,72,2560]{2,1,0:T(8,128)(2,1)S(1)}, u32[]{:S(2)}) %copy-start.2) | copy-done | bytes 11796504
  153.4 0.0 copy-done.4
  153.4 11.4 %fusion.4 = f32[2304,768]{1,0:T(8,128)} fusion(bf16[2304,2560]{1,0:T(8,128)(2,1)S(1)} %bitcast.43, bf16[1,2560,768]{2,1,0:T(8,128)(2,1)S(1)} %copy-done.4), kind=kOutput, calls=%fused_computation.8 | convolution fusion | flops 9059696640 | bytes 22806528 | tf_op jit(solution)/shard_map/dot_general | solution.py:8
  164.9 31.7 %convolution_convert_fusion = bf16[2304,2560]{1,0:T(8,128)(2,1)} fusion(f32[2304,768]{1,0:T(8,128)} %fusion.4, bf16[2304,2560]{1,0:T(8,128)(2,1)} %bitcast.44, bf16[1,768,2560]{2,1,0:T(8,128)(2,1)} %param.11, bf16[1,2560,768]{2,1,0:T(8,128)(2,1)} %param.10), kind=kOutput, calls=%fused_computation | convolution fusion | flops 18135908352 | bytes 38535168 | tf_op jit(solution)/shard_map/dot_general | solution.py:11
  196.6 0.0 copy-start.3
  196.6 6.2 %all-to-all-start.1 = ((bf16[32,72,2560]{2,1,0:T(8,128)(2,1)}), bf16[32,72,2560]{2,1,0:T(8,128)(2,1)}, u32[]{:S(2)}, u32[]{:S(2)}) async-start(bf16[32,72,2560]{2,1,0:T(8,128)(2,1)} %bitcast.42), calls=%async_computation.1 | async-start | bytes 23592960 | tf_op jit(solution)/shard_map/all_to_all | solution.py:59
  202.8 0.0 copy-done.3
  202.8 1.1 select_reduce_fusion
  203.9 149.1 %all-to-all-done.1 = bf16[32,72,2560]{2,1,0:T(8,128)(2,1)} async-done(((bf16[32,72,2560]{2,1,0:T(8,128)(2,1)}), bf16[32,72,2560]{2,1,0:T(8,128)(2,1)}, u32[]{:S(2)}, u32[]{:S(2)}) %all-to-all-start.1) | async-done | bytes 11796512 | tf_op jit(solution)/shard_map/all_to_all | solution.py:59
  353.1 6.1 %fusion.9 = f32[128,2560]{1,0:T(8,128)S(1)} fusion(bf16[2304,2560]{1,0:T(8,128)(2,1)} %bitcast.7, f32[128,2304]{1,0:T(8,128)S(1)} %select_reduce_fusion), kind=kOutput, calls=%fused_computation.17 | convolution fusion | flops 1510244352 | bytes 14286848 | tf_op jit(solution)/shard_map/dot_general | solution.py:70
  359.1 0.0 copy-start.1
  359.2 6.2 %convolution_add_fusion.1 = f32[128,2560]{1,0:T(8,128)S(1)} fusion(f32[128,2560]{1,0:T(8,128)S(1)} %fusion.9, bf16[2304,2560]{1,0:T(8,128)(2,1)} %bitcast.7, f32[128,2304]{1,0:T(8,128)S(1)} %select_reduce_fusion), kind=kOutput, calls=%fused_computation.11 | convolution fusion | flops 1511456768 | bytes 15597568 | tf_op jit(solution)/shard_map/dot_general | solution.py:70
  365.4 7.0 %fusion.6 = bf16[128,2560]{1,0:T(8,128)(2,1)} fusion(f32[128,2560]{1,0:T(8,128)S(1)} %convolution_add_fusion.1, bf16[2304,2560]{1,0:T(8,128)(2,1)} %bitcast.7, f32[128,2304]{1,0:T(8,128)S(1)} %select_reduce_fusion), kind=kOutput, calls=%fused_computation.12 | convolution fusion | flops 1512669184 | bytes 14942208 | tf_op jit(solution)/shard_map/dot_general | solution.py:70
  372.4 0.0 copy-done.1
  (2 shorter events, 0.0 us)
Async XLA Ops:
  0.0 5.6 %copy-start = (bf16[128,2560]{1,0:T(8,128)(2,1)S(1)}, bf16[128,2560]{1,0:T(8,128)(2,1)}, u32[]{:S(2)}) copy-start(bf16[128,2560]{1,0:T(8,128)(2,1)} %param.6) | copy-start | bytes 1966084
  9.2 144.2 %copy-start.4 = (bf16[1,2560,768]{2,1,0:T(8,128)(2,1)S(1)}, bf16[1,2560,768]{2,1,0:T(8,128)(2,1)}, u32[]{:S(2)}) copy-start(bf16[1,2560,768]{2,1,0:T(8,128)(2,1)} %param.9) | copy-start | bytes 11796484
  149.1 4.3 %copy-start.2 = (bf16[32,72,2560]{2,1,0:T(8,128)(2,1)}, bf16[32,72,2560]{2,1,0:T(8,128)(2,1)S(1)}, u32[]{:S(2)}) copy-start(bf16[32,72,2560]{2,1,0:T(8,128)(2,1)S(1)} %all_to_all.10) | copy-start | bytes 35389444
  196.6 6.2 %copy-start.3 = (f32[128,6]{0,1:T(8,128)S(1)}, f32[128,6]{0,1:T(8,128)}, u32[]{:S(2)}) copy-start(f32[128,6]{0,1:T(8,128)} %param.8) | copy-start | bytes 9220
  196.6 156.5 %all-to-all-start.1 = ((bf16[32,72,2560]{2,1,0:T(8,128)(2,1)}), bf16[32,72,2560]{2,1,0:T(8,128)(2,1)}, u32[]{:S(2)}, u32[]{:S(2)}) async-start(bf16[32,72,2560]{2,1,0:T(8,128)(2,1)} %bitcast.42), calls=%async_computation.1 | async-start | bytes 23592960 | tf_op jit(solution)/shard_map/all_to_all | solution.py:59
  359.1 13.3 %copy-start.1 = (bf16[128,2560]{1,0:T(8,128)(2,1)S(1)}, bf16[128,2560]{1,0:T(8,128)(2,1)}, u32[]{:S(2)}) copy-start(bf16[128,2560]{1,0:T(8,128)(2,1)} %param.6) | copy-start | bytes 1966084

commit v2 on v1

--- a/solution.py
+++ b/solution.py
@@ -46,29 +46,36 @@
         "tr,td->rd", pick, tokens, preferred_element_type=jnp.float32
     ).astype(jnp.bfloat16)
 
-    received = lax.all_to_all(
-        outgoing.reshape(experts_all, slot_bound, features),
-        "expert",
-        split_axis=0,
-        concat_axis=0,
-        tiled=True,
-    )
-    answered = expert_apply(
-        received.reshape(buffer_rows, features), w_gate[0], w_up[0], w_down[0]
-    )
-    returned = lax.all_to_all(
-        answered.reshape(experts_all, slot_bound, features),
-        "expert",
-        split_axis=0,
-        concat_axis=0,
-        tiled=True,
-    ).reshape(buffer_rows, features)
+    chunks = 2
+    chunk_slots = slot_bound // chunks
+    staged = outgoing.reshape(experts_all, slot_bound, features)
+    answers = []
+    for chunk in range(chunks):
+        received = lax.all_to_all(
+            staged[:, chunk * chunk_slots:(chunk + 1) * chunk_slots],
+            "expert",
+            split_axis=0,
+            concat_axis=0,
+            tiled=True,
+        )
+        answered = expert_apply(
+            received.reshape(-1, features), w_gate[0], w_up[0], w_down[0]
+        )
+        answers.append(
+            lax.all_to_all(
+                answered.reshape(experts_all, chunk_slots, features),
+                "expert",
+                split_axis=0,
+                concat_axis=0,
+                tiled=True,
+            )
+        )
+    returned = jnp.concatenate(answers, axis=1).reshape(buffer_rows, features)
 
     weights = jnp.sum(jnp.where(hit, gate_values[:, :, None], 0.0), axis=1)
-    summed = None
-    for part in split_bf16(weights):
-        term = jnp.dot(part, returned, preferred_element_type=jnp.float32)
-        summed = term if summed is None else summed + term
+    stacked = jnp.concatenate(split_bf16(weights), axis=0)
+    terms = jnp.dot(stacked, returned, preferred_element_type=jnp.float32)
+    summed = jnp.sum(terms.reshape(3, token_count, features), axis=0)
     return summed.astype(jnp.bfloat16)
 
 

time: 373 us -> 371 us (level)
  blocking collectives: 140 us -> 83.6 us
  local copies, waits for them, and re-layouts: 5.86 us -> 37.8 us
  starting transfers between devices: 6.22 us -> 15.4 us
  other arithmetic: 5.09 us -> 12.8 us
    all_to_all x1, blocking collectives: 140 us -> 83.6 us  [shards(): lax.all_to_all(staged[:, chunk * chunk_slots:(chunk + 1) * chunk_slots],...]
    reshape x0 -> x4, local copies, waits for them, and re-layouts: none -> 32.4 us  [the longest x2 16.4 us: shards(): received.reshape(-1, features)]
    dot_general x3 -> x1, matrix products: 19.3 us -> 5.61 us  [shards(): terms = jnp.dot(stacked, returned, preferred_element_type=jnp.float32)]
    dot_general x1 -> x2, matrix products: 11.4 us -> 20.8 us  [expert_apply(): jnp.dot(row_block, gate_matrix, preferred_element_type=jnp.float32)]
    all_to_all x1 -> x3, starting transfers between devices: 6.22 us -> 15.4 us  [the longest x2 10.3 us: shards(): lax.all_to_all(answered.reshape(experts_all, chunk_slots, features), 'exp...]
    concatenate x0 -> x2, other arithmetic: none -> 7.51 us  [the longest x1 7.39 us: shards(): returned = jnp.concatenate(answers, axis=1).reshape(buffer_rows, features)]
    dot_general x1 -> x2, matrix products: 31.7 us -> 37.7 us  [expert_apply(): jnp.dot(hidden, down_matrix, preferred_element_type=jnp.float32)]
    unnamed x11 -> x7, local copies, waits for them, and re-layouts: 5.15 us -> 0.87 us
  transfers between devices with their start and end apart: 1 -> 3, of which waited for: 1 -> 3; matrix products, arithmetic and copies ran while one was open for 0% -> 25% of each run, Pallas kernels for 0% -> 0%
where the time goes in v2:
time: 371 us; the launch traced here: 369 us
  waiting for transfers between devices  152 us (41%)
  blocking collectives  83.6 us (23%)
  matrix products  67.6 us (18%)
  local copies, waits for them, and re-layouts  37.8 us (10%)
  starting transfers between devices  15.4 us (4%)
  other arithmetic  12.8 us (3%)
    all_to_all x2, waiting for transfers between devices, shards(): lax.all_to_all(answered.reshape(experts_all, chunk_slots, features), 'exp...  116 us
    all_to_all x1, blocking collectives, shards(): lax.all_to_all(staged[:, chunk * chunk_slots:(chunk + 1) * chunk_slots],...  83.6 us
    dot_general x2, matrix products, expert_apply(): jnp.dot(hidden, down_matrix, preferred_element_type=jnp.float32)  37.7 us
    all_to_all x1, waiting for transfers between devices, shards(): lax.all_to_all(staged[:, chunk * chunk_slots:(chunk + 1) * chunk_slots],...  36.1 us
    dot_general x2, matrix products, expert_apply(): jnp.dot(row_block, gate_matrix, preferred_element_type=jnp.float32)  20.8 us
    reshape x2, local copies, waits for them, and re-layouts, shards(): received.reshape(-1, features)  16.4 us
    reshape x2, local copies, waits for them, and re-layouts, shards(): answered.reshape(experts_all, chunk_slots, features)  16 us
    all_to_all x2, starting transfers between devices, shards(): lax.all_to_all(answered.reshape(experts_all, chunk_slots, features), 'exp...  10.3 us
  transfers between devices with their start and end apart: 3, of which 3 were waited for; matrix products, arithmetic and copies ran while one was open for 25% of the time, Pallas kernels for 0%

profile of v2, /device:TPU:0, one launch (start us, length us, event | category | flops | bytes accessed | tf_op | source)
XLA Modules:
  0.0 369.4 jit_solution(14728625679430244610)
XLA Ops:
  0.0 0.9 copy.21
  0.9 0.1 eq.42
  1.0 0.1 eq.38
  1.2 1.7 reduce-window.6
  2.9 0.3 slice_reduce_fusion
  3.2 0.1 fusion.22
  3.3 0.1 reduce_sum.30
  3.4 0.1 copy.24
  3.5 0.7 multiply_add_fusion
  4.2 1.4 fusion
  5.7 3.5 convolution_convert_fusion
  9.2 3.8 %fusion.26 = (bf16[32,36,2560]{2,1,0:T(8,128)(2,1)S(1)}, bf16[32,36,2560]{2,1,0:T(8,128)(2,1)}) fusion(bf16[32,72,2560]{2,1,0:T(8,128)(2,1)S(1)} %bitcast.56), kind=kLoop, calls=%fused_computation.36 | loop fusion | bytes 23592960 | tf_op jit(solution)/shard_map/slice | solution.py:55
  13.0 83.6 %all_to_all.20 = bf16[32,36,2560]{2,1,0:T(8,128)(2,1)} all-to-all(bf16[32,36,2560]{2,1,0:T(8,128)(2,1)S(1)} %get-tuple-element.5), channel_id=1, replica_groups=mesh['dp'=4,'expert'=32] {'expert'}, dimensions={0} | all-to-all | bytes 11796480 | tf_op jit(solution)/shard_map/all_to_all | solution.py:54
  96.6 5.1 %all-to-all-start.2 = ((bf16[32,36,2560]{2,1,0:T(8,128)(2,1)}), bf16[32,36,2560]{2,1,0:T(8,128)(2,1)}, u32[]{:S(2)}, u32[]{:S(2)}) async-start(bf16[32,36,2560]{2,1,0:T(8,128)(2,1)} %get-tuple-element.6), calls=%async_computation.2 | async-start | bytes 13107200 | tf_op jit(solution)/shard_map/all_to_all | solution.py:54
  101.7 8.2 %reshape.47 = bf16[1152,2560]{1,0:T(8,128)(2,1)} reshape(bf16[32,36,2560]{2,1,0:T(8,128)(2,1)} %all_to_all.20) | data formatting | bytes 11796480 | tf_op jit(solution)/shard_map/reshape | solution.py:62
  109.9 10.3 %fusion.7 = f32[1152,768]{1,0:T(8,128)} fusion(bf16[1152,2560]{1,0:T(8,128)(2,1)} %reshape.47, bf16[1,2560,768]{2,1,0:T(8,128)(2,1)} %param.9), kind=kOutput, calls=%fused_computation.15 | convolution fusion | flops 4529848320 | bytes 13369344 | tf_op jit(solution)/shard_map/dot_general | solution.py:8
  120.3 18.9 %convolution_convert_fusion.2 = bf16[1152,2560]{1,0:T(8,128)(2,1)} fusion(bf16[1,768,2560]{2,1,0:T(8,128)(2,1)} %param.11, bf16[1152,2560]{1,0:T(8,128)(2,1)} %reshape.47, bf16[1,2560,768]{2,1,0:T(8,128)(2,1)} %param.10, f32[1152,768]{1,0:T(8,128)} %fusion.7), kind=kOutput, calls=%fused_computation.3 | convolution fusion | flops 9067954176 | bytes 23199744 | tf_op jit(solution)/shard_map/dot_general | solution.py:11
  139.2 8.0 %reshape.48 = bf16[32,36,2560]{2,1,0:T(8,128)(2,1)} reshape(bf16[1152,2560]{1,0:T(8,128)(2,1)} %convolution_convert_fusion.2) | data formatting | bytes 11796480 | tf_op jit(solution)/shard_map/reshape | solution.py:66
  147.1 36.1 %all-to-all-done.2 = bf16[32,36,2560]{2,1,0:T(8,128)(2,1)} async-done(((bf16[32,36,2560]{2,1,0:T(8,128)(2,1)}), bf16[32,36,2560]{2,1,0:T(8,128)(2,1)}, u32[]{:S(2)}, u32[]{:S(2)}) %all-to-all-start.2) | async-done | bytes 5898272 | tf_op jit(solution)/shard_map/all_to_all | solution.py:54
  183.2 5.1 %all-to-all-start.1 = ((bf16[32,36,2560]{2,1,0:T(8,128)(2,1)}), bf16[32,36,2560]{2,1,0:T(8,128)(2,1)}, u32[]{:S(2)}, u32[]{:S(2)}) async-start(bf16[32,36,2560]{2,1,0:T(8,128)(2,1)} %reshape.48), calls=%async_computation.1 | async-start | bytes 13107200 | tf_op jit(solution)/shard_map/all_to_all | solution.py:65
  188.3 8.2 %reshape.49 = bf16[1152,2560]{1,0:T(8,128)(2,1)} reshape(bf16[32,36,2560]{2,1,0:T(8,128)(2,1)} %all-to-all-done.2) | data formatting | bytes 11796480 | tf_op jit(solution)/shard_map/reshape | solution.py:62
  196.6 10.4 %fusion.5 = f32[1152,768]{1,0:T(8,128)} fusion(bf16[1152,2560]{1,0:T(8,128)(2,1)} %reshape.49, bf16[1,2560,768]{2,1,0:T(8,128)(2,1)} %param.9), kind=kOutput, calls=%fused_computation.13 | convolution fusion | flops 4529848320 | bytes 13369344 | tf_op jit(solution)/shard_map/dot_general | solution.py:8
  207.0 18.8 %convolution_convert_fusion.1 = bf16[1152,2560]{1,0:T(8,128)(2,1)} fusion(bf16[1,768,2560]{2,1,0:T(8,128)(2,1)} %param.11, bf16[1152,2560]{1,0:T(8,128)(2,1)} %reshape.49, bf16[1,2560,768]{2,1,0:T(8,128)(2,1)} %param.10, f32[1152,768]{1,0:T(8,128)} %fusion.5), kind=kOutput, calls=%fused_computation.2 | convolution fusion | flops 9067954176 | bytes 23199744 | tf_op jit(solution)/shard_map/dot_general | solution.py:11
  225.8 8.0 %reshape.50 = bf16[32,36,2560]{2,1,0:T(8,128)(2,1)} reshape(bf16[1152,2560]{1,0:T(8,128)(2,1)} %convolution_convert_fusion.1) | data formatting | bytes 11796480 | tf_op jit(solution)/shard_map/reshape | solution.py:66
  233.8 36.0 %all-to-all-done.1 = bf16[32,36,2560]{2,1,0:T(8,128)(2,1)} async-done(((bf16[32,36,2560]{2,1,0:T(8,128)(2,1)}), bf16[32,36,2560]{2,1,0:T(8,128)(2,1)}, u32[]{:S(2)}, u32[]{:S(2)}) %all-to-all-start.1) | async-done | bytes 5898272 | tf_op jit(solution)/shard_map/all_to_all | solution.py:65
  269.8 5.2 %all-to-all-start.3 = ((bf16[32,36,2560]{2,1,0:T(8,128)(2,1)}), bf16[32,36,2560]{2,1,0:T(8,128)(2,1)}, u32[]{:S(2)}, u32[]{:S(2)}) async-start(bf16[32,36,2560]{2,1,0:T(8,128)(2,1)} %reshape.50), calls=%async_computation.3 | async-start | bytes 13107200 | tf_op jit(solution)/shard_map/all_to_all | solution.py:65
  275.0 1.1 select_reduce_fusion
  276.0 0.2 fusion.27
  276.2 0.1 pad_maximum_fusion.1
  276.3 80.0 %all-to-all-done.3 = bf16[32,36,2560]{2,1,0:T(8,128)(2,1)} async-done(((bf16[32,36,2560]{2,1,0:T(8,128)(2,1)}), bf16[32,36,2560]{2,1,0:T(8,128)(2,1)}, u32[]{:S(2)}, u32[]{:S(2)}) %all-to-all-start.3) | async-done | bytes 5898272 | tf_op jit(solution)/shard_map/all_to_all | solution.py:65
  356.4 7.4 %pad_maximum_fusion = bf16[32,72,2560]{2,1,0:T(8,128)(2,1)S(1)} fusion(bf16[32,36,2560]{2,1,0:T(8,128)(2,1)} %all-to-all-done.3, bf16[32,36,2560]{2,1,0:T(8,128)(2,1)} %all-to-all-done.1), kind=kLoop, calls=%fused_computation.1 | loop fusion | flops 23592960 | bytes 23592960 | tf_op jit(solution)/shard_map/concatenate | solution.py:73
  363.8 5.6 %convolution_reduce_fusion = bf16[128,2560]{1,0:T(8,128)(2,1)} fusion(bf16[3,128,2304]{2,1,0:T(8,128)(2,1)S(1)} %bitcast.58, bf16[2304,2560,1]{1,0,2:T(8,128)(2,1)S(1)} %bitcast.57), kind=kOutput, calls=%fused_computation.20 | convolution fusion | flops 4530503680 | bytes 14221312 | tf_op jit(solution)/shard_map/dot_general | solution.py:77
  (8 shorter events, 0.0 us)
Async XLA Ops:
  0.0 5.6 %copy-start = (bf16[128,2560]{1,0:T(8,128)(2,1)S(1)}, bf16[128,2560]{1,0:T(8,128)(2,1)}, u32[]{:S(2)}) copy-start(bf16[128,2560]{1,0:T(8,128)(2,1)} %param.6) | copy-start | bytes 1966084
  96.6 86.6 %all-to-all-start.2 = ((bf16[32,36,2560]{2,1,0:T(8,128)(2,1)}), bf16[32,36,2560]{2,1,0:T(8,128)(2,1)}, u32[]{:S(2)}, u32[]{:S(2)}) async-start(bf16[32,36,2560]{2,1,0:T(8,128)(2,1)} %get-tuple-element.6), calls=%async_computation.2 | async-start | bytes 13107200 | tf_op jit(solution)/shard_map/all_to_all | solution.py:54
  183.2 86.6 %all-to-all-start.1 = ((bf16[32,36,2560]{2,1,0:T(8,128)(2,1)}), bf16[32,36,2560]{2,1,0:T(8,128)(2,1)}, u32[]{:S(2)}, u32[]{:S(2)}) async-start(bf16[32,36,2560]{2,1,0:T(8,128)(2,1)} %reshape.48), calls=%async_computation.1 | async-start | bytes 13107200 | tf_op jit(solution)/shard_map/all_to_all | solution.py:65
  233.8 41.2 %copy-start.2 = (f32[128,6]{0,1:T(8,128)S(1)}, f32[128,6]{0,1:T(8,128)}, u32[]{:S(2)}) copy-start(f32[128,6]{0,1:T(8,128)} %param.8) | copy-start | bytes 9220
  269.8 86.6 %all-to-all-start.3 = ((bf16[32,36,2560]{2,1,0:T(8,128)(2,1)}), bf16[32,36,2560]{2,1,0:T(8,128)(2,1)}, u32[]{:S(2)}, u32[]{:S(2)}) async-start(bf16[32,36,2560]{2,1,0:T(8,128)(2,1)} %reshape.50), calls=%async_computation.3 | async-start | bytes 13107200 | tf_op jit(solution)/shard_map/all_to_all | solution.py:65
  363.8 5.6 %copy-start.1 = (bf16[128,2560]{1,0:T(8,128)(2,1)S(1)}, bf16[128,2560]{1,0:T(8,128)(2,1)}, u32[]{:S(2)}) copy-start(bf16[128,2560]{1,0:T(8,128)(2,1)} %param.6) | copy-start | bytes 1966084

commit v3 on v1

--- a/solution.py
+++ b/solution.py
@@ -1,7 +1,68 @@
+import functools
+
 import jax
 import jax.numpy as jnp
 from jax import lax
+from jax.experimental import pallas as pl
+from jax.experimental.pallas import tpu as pltpu
 from jax.sharding import PartitionSpec as P
+
+MESH = pl.DeviceIdType.MESH
+
+
+def exchange_kernel(n, x_ref, y_ref, send_sem, recv_sem, local_sem):
+    me = lax.axis_index("expert")
+    barrier = pltpu.get_barrier_semaphore()
+
+    def greet(k, carry):
+        pl.semaphore_signal(
+            barrier, inc=1, device_id={"expert": lax.rem(me + k, n)}, device_id_type=MESH
+        )
+        return carry
+
+    lax.fori_loop(1, n, greet, 0)
+    pl.semaphore_wait(barrier, n - 1)
+    local = pltpu.make_async_copy(x_ref.at[me], y_ref.at[me], local_sem)
+    local.start()
+
+    def remote(k):
+        target = lax.rem(me + k, n)
+        return pltpu.make_async_remote_copy(
+            src_ref=x_ref.at[target],
+            dst_ref=y_ref.at[me],
+            send_sem=send_sem.at[k],
+            recv_sem=recv_sem.at[k],
+            device_id={"expert": target},
+            device_id_type=MESH,
+        )
+
+    def start(k, carry):
+        remote(k).start()
+        return carry
+
+    def finish(k, carry):
+        remote(k).wait()
+        return carry
+
+    lax.fori_loop(1, n, start, 0)
+    lax.fori_loop(1, n, finish, 0)
+    local.wait()
+
+
+def exchange(blocks, collective_id):
+    n = lax.axis_size("expert")
+    return pl.pallas_call(
+        functools.partial(exchange_kernel, n),
+        out_shape=jax.ShapeDtypeStruct(blocks.shape, blocks.dtype),
+        in_specs=[pl.BlockSpec(memory_space=pl.ANY)],
+        out_specs=pl.BlockSpec(memory_space=pl.ANY),
+        scratch_shapes=[
+            pltpu.SemaphoreType.DMA((n,)),
+            pltpu.SemaphoreType.DMA((n,)),
+            pltpu.SemaphoreType.DMA,
+        ],
+        compiler_params=pltpu.CompilerParams(collective_id=collective_id, has_side_effects=True),
+    )(blocks)
 
 
 def expert_apply(row_block, gate_matrix, up_matrix, down_matrix):
@@ -12,11 +73,11 @@
 
 
 def split_bf16(values):
-    first = values.astype(jnp.bfloat16)
-    rest = values - first.astype(jnp.float32)
-    second = rest.astype(jnp.bfloat16)
-    third = (rest - second.astype(jnp.float32)).astype(jnp.bfloat16)
-    return first, second, third
+    first = lax.reduce_precision(values, exponent_bits=8, mantissa_bits=7)
+    rest = values - first
+    second = lax.reduce_precision(rest, exponent_bits=8, mantissa_bits=7)
+    third = rest - second
+    return tuple(part.astype(jnp.bfloat16) for part in (first, second, third))
 
 
 def shards(tokens, expert_ids, gate_values, w_gate, w_up, w_down):
@@ -46,29 +107,18 @@
         "tr,td->rd", pick, tokens, preferred_element_type=jnp.float32
     ).astype(jnp.bfloat16)
 
-    received = lax.all_to_all(
-        outgoing.reshape(experts_all, slot_bound, features),
-        "expert",
-        split_axis=0,
-        concat_axis=0,
-        tiled=True,
-    )
+    received = exchange(outgoing.reshape(experts_all, slot_bound, features), 0)
     answered = expert_apply(
         received.reshape(buffer_rows, features), w_gate[0], w_up[0], w_down[0]
     )
-    returned = lax.all_to_all(
-        answered.reshape(experts_all, slot_bound, features),
-        "expert",
-        split_axis=0,
-        concat_axis=0,
-        tiled=True,
-    ).reshape(buffer_rows, features)
+    returned = exchange(answered.reshape(experts_all, slot_bound, features), 1).reshape(
+        buffer_rows, features
+    )
 
     weights = jnp.sum(jnp.where(hit, gate_values[:, :, None], 0.0), axis=1)
-    summed = None
-    for part in split_bf16(weights):
-        term = jnp.dot(part, returned, preferred_element_type=jnp.float32)
-        summed = term if summed is None else summed + term
+    stacked = jnp.concatenate(split_bf16(weights), axis=0)
+    terms = jnp.dot(stacked, returned, preferred_element_type=jnp.float32)
+    summed = jnp.sum(terms.reshape(3, token_count, features), axis=0)
     return summed.astype(jnp.bfloat16)
 
 

time: 373 us -> 510 us (1.37)
  the two profiles are of different devices: /device:TPU:0 before, /device:TPU:41 now
where the time goes in v3:
time: 510 us
  Pallas kernels  439 us (86%)
  matrix products  63.1 us (12%)
  other arithmetic  6.23 us (1%)
    pallas_call x2, Pallas kernels, exchange(): pl.pallas_call(functools.partial(exchange_kernel, n), out_shape=jax.Shape...  439 us
    dot_general x1, matrix products, expert_apply(): jnp.dot(hidden, down_matrix, preferred_element_type=jnp.float32)  31.7 us
    dot_general x1, matrix products, expert_apply(): jnp.dot(row_block, gate_matrix, preferred_element_type=jnp.float32)  15.3 us

profile of v3, /device:TPU:41, one launch (start us, length us, event | category | flops | bytes accessed | tf_op | source)
XLA Modules:
  0.0 509.9 jit_solution(10631795403624015504)
XLA Ops:
  0.0 0.0 copy-start
  0.0 0.9 copy.21
  0.9 0.1 eq.42
  1.0 0.1 eq.38
  1.2 1.7 reduce-window.6
  2.9 0.3 slice_reduce_fusion
  3.2 0.1 fusion.10
  3.3 0.1 reduce_sum.30
  3.4 0.1 copy.24
  3.5 0.7 multiply_add_fusion
  4.2 1.4 fusion
  5.6 1.9 select_reduce_fusion
  7.5 0.2 reduce-precision_convert_fusion.1
  7.7 0.1 pad_maximum_fusion
  7.9 0.0 copy-done
  7.9 6.0 %convolution_convert_fusion.1 = bf16[2304,2560]{1,0:T(8,128)(2,1)} fusion(pred[128,2304]{1,0:T(8,128)(4,1)S(1)} %fusion, bf16[128,2560]{1,0:T(8,128)(2,1)S(1)} %copy-done), kind=kOutput, calls=%fused_computation.1 | convolution fusion | flops 1515847680 | bytes 12746752 | tf_op jit(solution)/shard_map/tr,td->rd/dot_general | solution.py:106
  13.9 218.6 %shard_map.64 = bf16[32,72,2560]{2,1,0:T(8,128)(2,1)} custom-call(bf16[32,72,2560]{2,1,0:T(8,128)(2,1)} %bitcast.43), custom_call_target="tpu_custom_call" | custom-call | tf_op jit(solution)/shard_map/pallas_call | solution.py:54
  232.6 15.3 %fusion.4 = f32[2304,768]{1,0:T(8,128)} fusion(bf16[2304,2560]{1,0:T(8,128)(2,1)} %bitcast.44, bf16[1,2560,768]{2,1,0:T(8,128)(2,1)} %param.9), kind=kOutput, calls=%fused_computation.8 | convolution fusion | flops 9059696640 | bytes 22806528 | tf_op jit(solution)/shard_map/dot_general | solution.py:69
  247.8 31.7 %convolution_convert_fusion = bf16[2304,2560]{1,0:T(8,128)(2,1)} fusion(f32[2304,768]{1,0:T(8,128)} %fusion.4, bf16[2304,2560]{1,0:T(8,128)(2,1)} %bitcast.45, bf16[1,768,2560]{2,1,0:T(8,128)(2,1)} %param.11, bf16[1,2560,768]{2,1,0:T(8,128)(2,1)} %param.10), kind=kOutput, calls=%fused_computation | convolution fusion | flops 18135908352 | bytes 38535168 | tf_op jit(solution)/shard_map/dot_general | solution.py:72
  279.5 220.3 %shard_map.65 = bf16[32,72,2560]{2,1,0:T(8,128)(2,1)} custom-call(bf16[32,72,2560]{2,1,0:T(8,128)(2,1)} %bitcast.46), custom_call_target="tpu_custom_call" | custom-call | tf_op jit(solution)/shard_map/pallas_call | solution.py:54
  499.8 0.0 copy-start.1
  499.8 10.1 %convolution_reduce_fusion = bf16[128,2560]{1,0:T(8,128)(2,1)} fusion(bf16[3,128,2304]{2,1,0:T(8,128)(2,1)S(1)} %bitcast.48, bf16[2304,2560,1]{1,0,2:T(8,128)(2,1)} %bitcast.47), kind=kOutput, calls=%fused_computation.12 | convolution fusion | flops 4530503680 | bytes 14221312 | tf_op jit(solution)/shard_map/dot_general | solution.py:120
  509.9 0.0 copy-done.1
  (2 shorter events, 0.0 us)
Async XLA Ops:
  0.0 7.9 %copy-start = (bf16[128,2560]{1,0:T(8,128)(2,1)S(1)}, bf16[128,2560]{1,0:T(8,128)(2,1)}, u32[]{:S(2)}) copy-start(bf16[128,2560]{1,0:T(8,128)(2,1)} %param.6) | copy-start | bytes 1966084
  499.8 10.1 %copy-start.1 = (bf16[128,2560]{1,0:T(8,128)(2,1)S(1)}, bf16[128,2560]{1,0:T(8,128)(2,1)}, u32[]{:S(2)}) copy-start(bf16[128,2560]{1,0:T(8,128)(2,1)} %param.6) | copy-start | bytes 1966084

commit v4 on v3

--- a/solution.py
+++ b/solution.py
@@ -101,24 +101,34 @@
     slot_of = jnp.sum(earlier * one_hot, axis=1)
     places = (flat_ids * slot_bound + slot_of).reshape(token_count, topk_width)
 
-    hit = places[:, :, None] == jnp.arange(buffer_rows, dtype=jnp.int32)[None, None, :]
-    pick = jnp.any(hit, axis=1).astype(jnp.bfloat16)
-    outgoing = jnp.einsum(
-        "tr,td->rd", pick, tokens, preferred_element_type=jnp.float32
-    ).astype(jnp.bfloat16)
-
-    received = exchange(outgoing.reshape(experts_all, slot_bound, features), 0)
-    answered = expert_apply(
-        received.reshape(buffer_rows, features), w_gate[0], w_up[0], w_down[0]
-    )
-    returned = exchange(answered.reshape(experts_all, slot_bound, features), 1).reshape(
-        buffer_rows, features
-    )
-
-    weights = jnp.sum(jnp.where(hit, gate_values[:, :, None], 0.0), axis=1)
-    stacked = jnp.concatenate(split_bf16(weights), axis=0)
-    terms = jnp.dot(stacked, returned, preferred_element_type=jnp.float32)
-    summed = jnp.sum(terms.reshape(3, token_count, features), axis=0)
+    chunk_sizes = (slot_bound // 2, slot_bound - slot_bound // 2)
+    weight_parts = split_bf16(gate_values)
+    summed = None
+    begin = 0
+    for size in chunk_sizes:
+        inside = (slot_of >= begin) & (slot_of < begin + size)
+        local_place = jnp.where(inside, flat_ids * size + slot_of - begin, -1)
+        hit = (
+            local_place.reshape(token_count, topk_width)[:, :, None]
+            == jnp.arange(experts_all * size, dtype=jnp.int32)[None, None, :]
+        ).reshape(token_count, topk_width, experts_all, size)
+        begin += size
+        pick = jnp.any(hit, axis=1).astype(jnp.bfloat16)
+        outgoing = jnp.einsum(
+            "tes,td->esd", pick, tokens, preferred_element_type=jnp.float32
+        ).astype(jnp.bfloat16)
+        received = lax.all_to_all(outgoing, "expert", split_axis=0, concat_axis=0, tiled=True)
+        answered = expert_apply(received, w_gate[0], w_up[0], w_down[0])
+        returned = lax.all_to_all(answered, "expert", split_axis=0, concat_axis=0, tiled=True)
+        stacked = jnp.stack(
+            [
+                jnp.sum(jnp.where(hit, part.astype(jnp.float32)[:, :, None, None], 0.0), axis=1)
+                for part in weight_parts
+            ]
+        ).astype(jnp.bfloat16)
+        terms = jnp.einsum("ptes,esd->ptd", stacked, returned, preferred_element_type=jnp.float32)
+        term = jnp.sum(terms, axis=0)
+        summed = term if summed is None else summed + term
     return summed.astype(jnp.bfloat16)
 
 

time: 510 us -> 366 us (0.72)
  the two profiles are of different devices: /device:TPU:41 before, /device:TPU:0 now
where the time goes in v4:
time: 366 us; the launch traced here: 365 us
  waiting for transfers between devices  251 us (69%)
  matrix products  82 us (22%)
  starting transfers between devices  22.9 us (6%)
  other arithmetic  6.61 us (2%)
    all_to_all x2, waiting for transfers between devices, shards(): lax.all_to_all(outgoing, 'expert', split_axis=0, concat_axis=0, tiled=True)  128 us
    all_to_all x2, waiting for transfers between devices, shards(): lax.all_to_all(answered, 'expert', split_axis=0, concat_axis=0, tiled=True)  123 us
    dot_general x2, matrix products, expert_apply(): jnp.dot(hidden, down_matrix, preferred_element_type=jnp.float32)  41.6 us
    dot_general x2, matrix products, expert_apply(): up_part = jnp.dot(row_block, up_matrix, preferred_element_type=jnp.float32)  19.9 us
    all_to_all x2, starting transfers between devices, shards(): lax.all_to_all(outgoing, 'expert', split_axis=0, concat_axis=0, tiled=True)  12.6 us
    dot_general x2, matrix products, shards(): jnp.einsum('ptes,esd->ptd', stacked, returned, preferred_element_type=jnp...  11.4 us
    all_to_all x2, starting transfers between devices, shards(): lax.all_to_all(answered, 'expert', split_axis=0, concat_axis=0, tiled=True)  10.3 us
    dot_general x2, matrix products, shards(): jnp.einsum('tes,td->esd', pick, tokens, preferred_element_type=jnp.float32)  9.1 us
  transfers between devices with their start and end apart: 4, of which 4 were waited for; matrix products, arithmetic and copies ran while one was open for 20% of the time, Pallas kernels for 0%

profile of v4, /device:TPU:0, one launch (start us, length us, event | category | flops | bytes accessed | tf_op | source)
XLA Modules:
  0.0 365.4 jit_solution(3833259620116138067)
XLA Ops:
  0.0 0.9 copy.20
  0.9 0.1 eq.63
  1.0 0.1 eq.67
  1.1 0.7 broadcast_multiply_fusion
  1.8 1.7 reduce-window.6
  3.6 0.3 slice_reduce_fusion
  3.9 0.1 fusion.62
  4.0 0.1 reduce_sum.84
  4.1 0.1 copy.24
  4.3 0.1 copy.25
  4.4 0.9 compare_reduce_fusion
  5.3 4.6 %convolution_convert_fusion.3 = bf16[32,36,2560]{2,1,0:T(8,128)(2,1)} fusion(bf16[128,2560]{1,0:T(8,128)(2,1)S(1)} %copy-done, pred[128,32,36]{0,1,2:T(8,128)(4,1)S(1)} %get-tuple-element.12), kind=kOutput, calls=%fused_computation.15 | convolution fusion | flops 757923840 | bytes 6701056 | tf_op jit(solution)/shard_map/tes,td->esd/dot_general | solution.py:117
  9.9 7.5 %all-to-all-start = ((bf16[32,36,2560]{2,1,0:T(8,128)(2,1)}), bf16[32,36,2560]{2,1,0:T(8,128)(2,1)}, u32[]{:S(2)}, u32[]{:S(2)}) async-start(bf16[32,36,2560]{2,1,0:T(8,128)(2,1)} %convolution_convert_fusion.3), calls=%async_computation | async-start | bytes 13107200 | tf_op jit(solution)/shard_map/all_to_all | solution.py:120
  17.4 4.5 %convolution_convert_fusion.1 = bf16[32,36,2560]{2,1,0:T(8,128)(2,1)} fusion(bf16[128,2560]{1,0:T(8,128)(2,1)S(1)} %copy-done, pred[128,32,36]{0,1,2:T(8,128)(4,1)S(1)} %get-tuple-element.11), kind=kOutput, calls=%fused_computation.13 | convolution fusion | flops 757923840 | bytes 6701056 | tf_op jit(solution)/shard_map/tes,td->esd/dot_general | solution.py:117
  21.9 77.1 %all-to-all-done = bf16[32,36,2560]{2,1,0:T(8,128)(2,1)} async-done(((bf16[32,36,2560]{2,1,0:T(8,128)(2,1)}), bf16[32,36,2560]{2,1,0:T(8,128)(2,1)}, u32[]{:S(2)}, u32[]{:S(2)}) %all-to-all-start) | async-done | bytes 5898272 | tf_op jit(solution)/shard_map/all_to_all | solution.py:120
  99.0 5.1 %all-to-all-start.2 = ((bf16[32,36,2560]{2,1,0:T(8,128)(2,1)}), bf16[32,36,2560]{2,1,0:T(8,128)(2,1)}, u32[]{:S(2)}, u32[]{:S(2)}) async-start(bf16[32,36,2560]{2,1,0:T(8,128)(2,1)} %convolution_convert_fusion.1), calls=%async_computation.2 | async-start | bytes 13107200 | tf_op jit(solution)/shard_map/all_to_all | solution.py:120
  104.1 9.9 %fusion.14 = f32[32,36,768]{2,1,0:T(8,128)} fusion(bf16[32,36,2560]{2,1,0:T(8,128)(2,1)} %all-to-all-done, bf16[1,2560,768]{2,1,0:T(8,128)(2,1)} %param.10), kind=kOutput, calls=%fused_computation.22 | convolution fusion | flops 4529848320 | bytes 13369344 | tf_op jit(solution)/shard_map/dot_general | solution.py:70
  114.1 20.8 %convolution_convert_fusion.2 = bf16[32,36,2560]{2,1,0:T(8,128)(2,1)} fusion(bf16[1,768,2560]{2,1,0:T(8,128)(2,1)} %param.11, f32[32,36,768]{2,1,0:T(8,128)} %fusion.14, bf16[32,36,2560]{2,1,0:T(8,128)(2,1)} %all-to-all-done, bf16[1,2560,768]{2,1,0:T(8,128)(2,1)} %param.9), kind=kOutput, calls=%fused_computation.14 | convolution fusion | flops 9067954176 | bytes 23199744 | tf_op jit(solution)/shard_map/dot_general | solution.py:72
  134.8 50.8 %all-to-all-done.2 = bf16[32,36,2560]{2,1,0:T(8,128)(2,1)} async-done(((bf16[32,36,2560]{2,1,0:T(8,128)(2,1)}), bf16[32,36,2560]{2,1,0:T(8,128)(2,1)}, u32[]{:S(2)}, u32[]{:S(2)}) %all-to-all-start.2) | async-done | bytes 5898272 | tf_op jit(solution)/shard_map/all_to_all | solution.py:120
  185.6 5.1 %all-to-all-start.1 = ((bf16[32,36,2560]{2,1,0:T(8,128)(2,1)}), bf16[32,36,2560]{2,1,0:T(8,128)(2,1)}, u32[]{:S(2)}, u32[]{:S(2)}) async-start(bf16[32,36,2560]{2,1,0:T(8,128)(2,1)} %convolution_convert_fusion.2), calls=%async_computation.1 | async-start | bytes 13107200 | tf_op jit(solution)/shard_map/all_to_all | solution.py:122
  190.7 9.9 %fusion.12 = f32[32,36,768]{2,1,0:T(8,128)} fusion(bf16[32,36,2560]{2,1,0:T(8,128)(2,1)} %all-to-all-done.2, bf16[1,2560,768]{2,1,0:T(8,128)(2,1)} %param.10), kind=kOutput, calls=%fused_computation.20 | convolution fusion | flops 4529848320 | bytes 13369344 | tf_op jit(solution)/shard_map/dot_general | solution.py:70
  200.7 20.8 %convolution_convert_fusion = bf16[32,36,2560]{2,1,0:T(8,128)(2,1)} fusion(bf16[1,768,2560]{2,1,0:T(8,128)(2,1)} %param.11, f32[32,36,768]{2,1,0:T(8,128)} %fusion.12, bf16[32,36,2560]{2,1,0:T(8,128)(2,1)} %all-to-all-done.2, bf16[1,2560,768]{2,1,0:T(8,128)(2,1)} %param.9), kind=kOutput, calls=%fused_computation.12 | convolution fusion | flops 9067954176 | bytes 23199744 | tf_op jit(solution)/shard_map/dot_general | solution.py:72
  221.5 50.7 %all-to-all-done.1 = bf16[32,36,2560]{2,1,0:T(8,128)(2,1)} async-done(((bf16[32,36,2560]{2,1,0:T(8,128)(2,1)}), bf16[32,36,2560]{2,1,0:T(8,128)(2,1)}, u32[]{:S(2)}, u32[]{:S(2)}) %all-to-all-start.1) | async-done | bytes 5898272 | tf_op jit(solution)/shard_map/all_to_all | solution.py:122
  272.2 5.2 %all-to-all-start.3 = ((bf16[32,36,2560]{2,1,0:T(8,128)(2,1)}), bf16[32,36,2560]{2,1,0:T(8,128)(2,1)}, u32[]{:S(2)}, u32[]{:S(2)}) async-start(bf16[32,36,2560]{2,1,0:T(8,128)(2,1)} %convolution_convert_fusion), calls=%async_computation.3 | async-start | bytes 13107200 | tf_op jit(solution)/shard_map/all_to_all | solution.py:122
  277.4 2.2 fusion.23
  279.5 0.2 fusion.56
  279.8 0.2 fusion.54
  280.0 0.2 fusion.58
  280.3 5.7 %fusion.33 = f32[128,2560]{1,0:T(8,128)S(1)} fusion(bf16[32,36,2560]{2,1,0:T(8,128)(2,1)} %all-to-all-done.1, bf16[1,128,32,36]{1,3,2,0:T(8,128)(2,1)S(1)} %get-tuple-element.20, bf16[1,128,32,36]{1,3,2,0:T(8,128)(2,1)S(1)} %get-tuple-element.19, bf16[1,128,32,36]{1,3,2,0:T(8,128)(2,1)S(1)} %get-tuple-element.18), kind=kOutput, calls=%fused_computation.37 | convolution fusion | flops 2266464256 | bytes 8093696 | tf_op jit(solution)/shard_map/ptes,esd->ptd/dot_general | solution.py:129
  286.0 72.8 %all-to-all-done.3 = bf16[32,36,2560]{2,1,0:T(8,128)(2,1)} async-done(((bf16[32,36,2560]{2,1,0:T(8,128)(2,1)}), bf16[32,36,2560]{2,1,0:T(8,128)(2,1)}, u32[]{:S(2)}, u32[]{:S(2)}) %all-to-all-start.3) | async-done | bytes 5898272 | tf_op jit(solution)/shard_map/all_to_all | solution.py:122
  358.7 5.7 %fusion.30 = f32[128,2560]{1,0:T(8,128)S(1)} fusion(bf16[32,36,2560]{2,1,0:T(8,128)(2,1)} %all-to-all-done.3, bf16[1,128,32,36]{1,3,2,0:T(8,128)(2,1)S(1)} %get-tuple-element.23, bf16[1,128,32,36]{1,3,2,0:T(8,128)(2,1)S(1)} %get-tuple-element.22, bf16[1,128,32,36]{1,3,2,0:T(8,128)(2,1)S(1)} %get-tuple-element.21), kind=kOutput, calls=%fused_computation.36 | convolution fusion | flops 2266464256 | bytes 8093696 | tf_op jit(solution)/shard_map/ptes,esd->ptd/dot_general | solution.py:129
  364.5 1.0 add_convert_fusion
  (12 shorter events, 0.1 us)
Async XLA Ops:
  0.0 5.3 %copy-start = (bf16[128,2560]{1,0:T(8,128)(2,1)S(1)}, bf16[128,2560]{1,0:T(8,128)(2,1)}, u32[]{:S(2)}) copy-start(bf16[128,2560]{1,0:T(8,128)(2,1)} %param.6) | copy-start | bytes 1966084
  9.9 89.2 %all-to-all-start = ((bf16[32,36,2560]{2,1,0:T(8,128)(2,1)}), bf16[32,36,2560]{2,1,0:T(8,128)(2,1)}, u32[]{:S(2)}, u32[]{:S(2)}) async-start(bf16[32,36,2560]{2,1,0:T(8,128)(2,1)} %convolution_convert_fusion.3), calls=%async_computation | async-start | bytes 13107200 | tf_op jit(solution)/shard_map/all_to_all | solution.py:120
  99.0 86.6 %all-to-all-start.2 = ((bf16[32,36,2560]{2,1,0:T(8,128)(2,1)}), bf16[32,36,2560]{2,1,0:T(8,128)(2,1)}, u32[]{:S(2)}, u32[]{:S(2)}) async-start(bf16[32,36,2560]{2,1,0:T(8,128)(2,1)} %convolution_convert_fusion.1), calls=%async_computation.2 | async-start | bytes 13107200 | tf_op jit(solution)/shard_map/all_to_all | solution.py:120
  185.6 86.6 %all-to-all-start.1 = ((bf16[32,36,2560]{2,1,0:T(8,128)(2,1)}), bf16[32,36,2560]{2,1,0:T(8,128)(2,1)}, u32[]{:S(2)}, u32[]{:S(2)}) async-start(bf16[32,36,2560]{2,1,0:T(8,128)(2,1)} %convolution_convert_fusion.2), calls=%async_computation.1 | async-start | bytes 13107200 | tf_op jit(solution)/shard_map/all_to_all | solution.py:122
  221.5 55.9 %copy-start.2 = (f32[128,6]{0,1:T(8,128)S(1)}, f32[128,6]{0,1:T(8,128)}, u32[]{:S(2)}) copy-start(f32[128,6]{0,1:T(8,128)} %param.8) | copy-start | bytes 9220
  272.2 86.6 %all-to-all-start.3 = ((bf16[32,36,2560]{2,1,0:T(8,128)(2,1)}), bf16[32,36,2560]{2,1,0:T(8,128)(2,1)}, u32[]{:S(2)}, u32[]{:S(2)}) async-start(bf16[32,36,2560]{2,1,0:T(8,128)(2,1)} %convolution_convert_fusion), calls=%async_computation.3 | async-start | bytes 13107200 | tf_op jit(solution)/shard_map/all_to_all | solution.py:122
  358.7 6.7 %copy-start.1 = (bf16[128,2560]{1,0:T(8,128)(2,1)S(1)}, bf16[128,2560]{1,0:T(8,128)(2,1)}, u32[]{:S(2)}) copy-start(bf16[128,2560]{1,0:T(8,128)(2,1)} %param.6) | copy-start | bytes 1966084

commit v5 on v4

--- a/solution.py
+++ b/solution.py
@@ -101,28 +101,29 @@
     slot_of = jnp.sum(earlier * one_hot, axis=1)
     places = (flat_ids * slot_bound + slot_of).reshape(token_count, topk_width)
 
-    chunk_sizes = (slot_bound // 2, slot_bound - slot_bound // 2)
+    hit = (
+        places[:, :, None] == jnp.arange(buffer_rows, dtype=jnp.int32)[None, None, :]
+    ).reshape(token_count, topk_width, experts_all, slot_bound)
+    pick = jnp.any(hit, axis=1).astype(jnp.bfloat16)
+    outgoing = jnp.einsum(
+        "tes,td->esd", pick, tokens, preferred_element_type=jnp.float32
+    ).astype(jnp.bfloat16)
+    received = lax.all_to_all(outgoing, "expert", split_axis=0, concat_axis=0, tiled=True)
+
+    small = slot_bound // 9
     weight_parts = split_bf16(gate_values)
     summed = None
-    begin = 0
-    for size in chunk_sizes:
-        inside = (slot_of >= begin) & (slot_of < begin + size)
-        local_place = jnp.where(inside, flat_ids * size + slot_of - begin, -1)
-        hit = (
-            local_place.reshape(token_count, topk_width)[:, :, None]
-            == jnp.arange(experts_all * size, dtype=jnp.int32)[None, None, :]
-        ).reshape(token_count, topk_width, experts_all, size)
-        begin += size
-        pick = jnp.any(hit, axis=1).astype(jnp.bfloat16)
-        outgoing = jnp.einsum(
-            "tes,td->esd", pick, tokens, preferred_element_type=jnp.float32
-        ).astype(jnp.bfloat16)
-        received = lax.all_to_all(outgoing, "expert", split_axis=0, concat_axis=0, tiled=True)
-        answered = expert_apply(received, w_gate[0], w_up[0], w_down[0])
+    for begin, end in ((0, small), (small, slot_bound)):
+        answered = expert_apply(received[:, begin:end], w_gate[0], w_up[0], w_down[0])
         returned = lax.all_to_all(answered, "expert", split_axis=0, concat_axis=0, tiled=True)
         stacked = jnp.stack(
             [
-                jnp.sum(jnp.where(hit, part.astype(jnp.float32)[:, :, None, None], 0.0), axis=1)
+                jnp.sum(
+                    jnp.where(
+                        hit[:, :, :, begin:end], part.astype(jnp.float32)[:, :, None, None], 0.0
+                    ),
+                    axis=1,
+                )
                 for part in weight_parts
             ]
         ).astype(jnp.bfloat16)

time: 366 us -> 359 us (0.981)
  blocking collectives: 0 us -> 140 us
  waiting for transfers between devices: 251 us -> 127 us
  matrix products: 82 us -> 61.4 us
  starting transfers between devices: 22.9 us -> 13.5 us
  local copies, waits for them, and re-layouts: 2.48 us -> 8.36 us
    all_to_all x0 -> x1, blocking collectives: none -> 140 us  [shards(): lax.all_to_all(outgoing, 'expert', split_axis=0, concat_axis=0, tiled=True)]
    all_to_all x2 -> x0, waiting for transfers between devices: 128 us -> none  [shards(): lax.all_to_all(outgoing, 'expert', split_axis=0, concat_axis=0, tiled=True)]
    all_to_all x2 -> x0, starting transfers between devices: 12.6 us -> none  [shards(): lax.all_to_all(outgoing, 'expert', split_axis=0, concat_axis=0, tiled=True)]
    dot_general x2, matrix products: 41.6 us -> 31 us  [expert_apply(): jnp.dot(hidden, down_matrix, preferred_element_type=jnp.float32)]
    dot_general x2 -> x1, matrix products: 9.1 us -> 3.37 us  [shards(): jnp.einsum('tes,td->esd', pick, tokens, preferred_element_type=jnp.float32)]
    unnamed x7 -> x15, local copies, waits for them, and re-layouts: 0.87 us -> 5.83 us
    dot_general x2, matrix products: 19.9 us -> 15.1 us  [expert_apply(): up_part = jnp.dot(row_block, up_matrix, preferred_element_type=jnp.float32)]
  transfers between devices with their start and end apart: 4 -> 2, of which waited for: 4 -> 1; matrix products, arithmetic and copies ran while one was open for 20% -> 14% of each run, Pallas kernels for 0% -> 0%
where the time goes in v5:
time: 359 us
  blocking collectives  140 us (39%)
  waiting for transfers between devices  127 us (35%)
  matrix products  61.4 us (17%)
  starting transfers between devices  13.5 us (4%)
  other arithmetic  8.59 us (2%)
  local copies, waits for them, and re-layouts  8.36 us (2%)
    all_to_all x1, blocking collectives, shards(): lax.all_to_all(outgoing, 'expert', split_axis=0, concat_axis=0, tiled=True)  140 us
    all_to_all x2, waiting for transfers between devices, shards(): lax.all_to_all(answered, 'expert', split_axis=0, concat_axis=0, tiled=True)  127 us
    dot_general x2, matrix products, expert_apply(): jnp.dot(hidden, down_matrix, preferred_element_type=jnp.float32)  31 us
    dot_general x2, matrix products, expert_apply(): up_part = jnp.dot(row_block, up_matrix, preferred_element_type=jnp.float32)  15.1 us
    all_to_all x2, starting transfers between devices, shards(): lax.all_to_all(answered, 'expert', split_axis=0, concat_axis=0, tiled=True)  13.5 us
    dot_general x2, matrix products, shards(): jnp.einsum('ptes,esd->ptd', stacked, returned, preferred_element_type=jnp...  10.7 us
  transfers between devices with their start and end apart: 2, of which 1 were waited for; matrix products, arithmetic and copies ran while one was open for 14% of the time, Pallas kernels for 0%

profile of v5, /device:TPU:0, one launch (start us, length us, event | category | flops | bytes accessed | tf_op | source)
XLA Modules:
  0.0 358.8 jit_solution(12508211301092923291)
XLA Ops:
  0.0 0.0 copy-start
  0.0 0.9 copy.51
  0.9 0.1 eq.49
  1.0 0.1 eq.45
  1.2 1.7 reduce-window.6
  2.9 0.3 slice_reduce_fusion
  3.2 0.1 fusion.57
  3.3 0.1 reduce_sum.84
  3.4 0.1 copy.54
  3.5 0.7 multiply_add_fusion.1
  4.2 1.5 broadcast_compare_fusion
  5.7 3.4 convolution_convert_fusion
  9.1 0.0 copy-start.6
  9.1 140.0 %all_to_all.15 = bf16[32,72,2560]{2,1,0:T(8,128)(2,1)S(1)} all-to-all(bf16[32,72,2560]{2,1,0:T(8,128)(2,1)S(1)} %convolution_convert_fusion), channel_id=1, replica_groups=mesh['dp'=4,'expert'=32] {'expert'}, dimensions={0} | all-to-all | bytes 23592960 | tf_op jit(solution)/shard_map/all_to_all | solution.py:111
  149.1 1.2 fusion.16
  150.3 3.8 %copy-done.4 = bf16[1,2560,768]{2,1,0:T(8,128)(2,1)S(1)} copy-done((bf16[1,2560,768]{2,1,0:T(8,128)(2,1)S(1)}, bf16[1,2560,768]{2,1,0:T(8,128)(2,1)}, u32[]{:S(2)}) %copy-start.4) | copy-done | bytes 3932184
  154.1 1.3 fusion.39
  155.4 1.2 copy-done.5
  156.6 1.2 fusion.18
  157.7 0.0 copy-done.2
  157.7 1.8 copy.59
  159.5 6.0 %all-to-all-start.1 = ((bf16[32,8,2560]{2,1,0:T(8,128)(2,1)}), bf16[32,8,2560]{2,1,0:T(8,128)(2,1)}, u32[]{:S(2)}, u32[]{:S(2)}) async-start(bf16[32,8,2560]{2,1,0:T(8,128)(2,1)} %copy.59), calls=%async_computation.1 | async-start | bytes 2621440 | tf_op jit(solution)/shard_map/all_to_all | solution.py:118
  165.6 13.9 %fusion.2 = f32[32,64,768]{2,1,0:T(8,128)} fusion(bf16[32,72,2560]{2,1,0:T(8,128)(2,1)} %copy-done.2, bf16[1,2560,768]{2,1,0:T(8,128)(2,1)} %param.10), kind=kOutput, calls=%fused_computation.2 | convolution fusion | flops 8053063680 | bytes 20709376 | tf_op jit(solution)/shard_map/dot_general | solution.py:70
  179.5 29.8 %convolution_convert_fusion.1 = bf16[32,64,2560]{2,1,0:T(8,128)(2,1)} fusion(bf16[1,768,2560]{2,1,0:T(8,128)(2,1)} %param.11, f32[32,64,768]{2,1,0:T(8,128)} %fusion.2, bf16[1,2560,768]{2,1,0:T(8,128)(2,1)} %param.9, bf16[32,72,2560]{2,1,0:T(8,128)(2,1)} %copy-done.2), kind=kOutput, calls=%fused_computation.7 | convolution fusion | flops 16120807424 | bytes 35127296 | tf_op jit(solution)/shard_map/dot_general | solution.py:72
  209.2 0.0 all-to-all-done.1
  209.3 7.5 %all-to-all-start.2 = ((bf16[32,64,2560]{2,1,0:T(8,128)(2,1)}), bf16[32,64,2560]{2,1,0:T(8,128)(2,1)}, u32[]{:S(2)}, u32[]{:S(2)}) async-start(bf16[32,64,2560]{2,1,0:T(8,128)(2,1)} %convolution_convert_fusion.1), calls=%async_computation.2 | async-start | bytes 20971520 | tf_op jit(solution)/shard_map/all_to_all | solution.py:118
  216.8 0.2 select_reduce_fusion.5
  217.0 3.3 select_reduce_fusion.2
  220.3 2.2 fusion.25
  222.5 126.8 %all-to-all-done.2 = bf16[32,64,2560]{2,1,0:T(8,128)(2,1)} async-done(((bf16[32,64,2560]{2,1,0:T(8,128)(2,1)}), bf16[32,64,2560]{2,1,0:T(8,128)(2,1)}, u32[]{:S(2)}, u32[]{:S(2)}) %all-to-all-start.2) | async-done | bytes 10485792 | tf_op jit(solution)/shard_map/all_to_all | solution.py:118
  349.3 8.5 %fusion.26 = f32[128,2560]{1,0:T(8,128)S(1)} fusion(bf16[32,64,2560]{2,1,0:T(8,128)(2,1)} %all-to-all-done.2, bf16[1,128,32,64]{1,3,2,0:T(8,128)(2,1)} %bitcast.90, bf16[1,128,32,64]{1,3,2,0:T(8,128)(2,1)S(1)} %bitcast.89, bf16[1,128,32,64]{1,3,2,0:T(8,128)(2,1)S(1)} %bitcast.88), kind=kOutput, calls=%fused_computation.26 | convolution fusion | flops 4028760064 | bytes 13369344 | tf_op jit(solution)/shard_map/ptes,esd->ptd/dot_general | solution.py:130
  357.8 1.0 add_convert_fusion
  (15 shorter events, 0.1 us)
Async XLA Ops:
  0.0 5.7 %copy-start = (bf16[128,2560]{1,0:T(8,128)(2,1)S(1)}, bf16[128,2560]{1,0:T(8,128)(2,1)}, u32[]{:S(2)}) copy-start(bf16[128,2560]{1,0:T(8,128)(2,1)} %param.6) | copy-start | bytes 1966084
  9.1 140.0 %copy-start.6 = (bf16[1,2560,768]{2,1,0:T(8,128)(2,1)S(1)}, bf16[1,2560,768]{2,1,0:T(8,128)(2,1)}, u32[]{:S(2)}) copy-start(bf16[1,2560,768]{2,1,0:T(8,128)(2,1)} %param.9) | copy-start | bytes 11796484
  149.1 8.7 %copy-start.2 = (bf16[32,72,2560]{2,1,0:T(8,128)(2,1)}, bf16[32,72,2560]{2,1,0:T(8,128)(2,1)S(1)}, u32[]{:S(2)}) copy-start(bf16[32,72,2560]{2,1,0:T(8,128)(2,1)S(1)} %all_to_all.15) | copy-start | bytes 35389444
  149.1 5.0 %copy-start.4 = (bf16[1,2560,768]{2,1,0:T(8,128)(2,1)S(1)}, bf16[1,2560,768]{2,1,0:T(8,128)(2,1)}, u32[]{:S(2)}) copy-start(bf16[1,2560,768]{2,1,0:T(8,128)(2,1)} %param.10) | copy-start | bytes 11796484
  154.1 2.4 copy-start.5
  159.5 49.7 %all-to-all-start.1 = ((bf16[32,8,2560]{2,1,0:T(8,128)(2,1)}), bf16[32,8,2560]{2,1,0:T(8,128)(2,1)}, u32[]{:S(2)}, u32[]{:S(2)}) async-start(bf16[32,8,2560]{2,1,0:T(8,128)(2,1)} %copy.59), calls=%async_computation.1 | async-start | bytes 2621440 | tf_op jit(solution)/shard_map/all_to_all | solution.py:118
  209.2 7.5 %copy-start.3 = (f32[128,6]{0,1:T(8,128)S(1)}, f32[128,6]{0,1:T(8,128)}, u32[]{:S(2)}) copy-start(f32[128,6]{0,1:T(8,128)} %param.8) | copy-start | bytes 9220
  209.3 140.0 %all-to-all-start.2 = ((bf16[32,64,2560]{2,1,0:T(8,128)(2,1)}), bf16[32,64,2560]{2,1,0:T(8,128)(2,1)}, u32[]{:S(2)}, u32[]{:S(2)}) async-start(bf16[32,64,2560]{2,1,0:T(8,128)(2,1)} %convolution_convert_fusion.1), calls=%async_computation.2 | async-start | bytes 20971520 | tf_op jit(solution)/shard_map/all_to_all | solution.py:118
  349.3 9.5 %copy-start.1 = (bf16[128,2560]{1,0:T(8,128)(2,1)S(1)}, bf16[128,2560]{1,0:T(8,128)(2,1)}, u32[]{:S(2)}) copy-start(bf16[128,2560]{1,0:T(8,128)(2,1)} %param.6) | copy-start | bytes 1966084

commit v6 on v5

--- a/solution.py
+++ b/solution.py
@@ -72,6 +72,37 @@
     return jnp.dot(hidden, down_matrix, preferred_element_type=jnp.float32).astype(jnp.bfloat16)
 
 
+def ffn_kernel(x_ref, gate_ref, up_ref, down_ref, out_ref):
+    sources, slots, features = x_ref.shape
+    rows = x_ref[...].reshape(sources * slots, features)
+    out_ref[...] = expert_apply(rows, gate_ref[...], up_ref[...], down_ref[...]).reshape(
+        sources, slots, features
+    )
+
+
+def expert_blocks(received, gate_matrix, up_matrix, down_matrix, slots, per_step):
+    sources, _, features = received.shape
+    hidden = gate_matrix.shape[1]
+    return pl.pallas_call(
+        ffn_kernel,
+        out_shape=jax.ShapeDtypeStruct((sources, slots, features), received.dtype),
+        grid=(sources // per_step,),
+        in_specs=[
+            pl.BlockSpec((per_step, slots, features), lambda i: (i, 0, 0)),
+            pl.BlockSpec((features, hidden), lambda i: (0, 0)),
+            pl.BlockSpec((features, hidden), lambda i: (0, 0)),
+            pl.BlockSpec((hidden, features), lambda i: (0, 0)),
+        ],
+        out_specs=pl.BlockSpec((per_step, slots, features), lambda i: (i, 0, 0)),
+        compiler_params=pltpu.CompilerParams(vmem_limit_bytes=60 * 1024 * 1024),
+        cost_estimate=pl.CostEstimate(
+            flops=6 * sources * slots * features * hidden,
+            transcendentals=sources * slots * hidden,
+            bytes_accessed=2 * (2 * sources * slots * features + 3 * features * hidden),
+        ),
+    )(received, gate_matrix, up_matrix, down_matrix)
+
+
 def split_bf16(values):
     first = lax.reduce_precision(values, exponent_bits=8, mantissa_bits=7)
     rest = values - first
@@ -110,11 +141,14 @@
     ).astype(jnp.bfloat16)
     received = lax.all_to_all(outgoing, "expert", split_axis=0, concat_axis=0, tiled=True)
 
-    small = slot_bound // 9
+    large = slot_bound - slot_bound // 9
     weight_parts = split_bf16(gate_values)
     summed = None
-    for begin, end in ((0, small), (small, slot_bound)):
-        answered = expert_apply(received[:, begin:end], w_gate[0], w_up[0], w_down[0])
+    for begin, end in ((large, slot_bound), (0, large)):
+        if begin == 0:
+            answered = expert_blocks(received, w_gate[0], w_up[0], w_down[0], end, 4)
+        else:
+            answered = expert_apply(received[:, begin:end], w_gate[0], w_up[0], w_down[0])
         returned = lax.all_to_all(answered, "expert", split_axis=0, concat_axis=0, tiled=True)
         stacked = jnp.stack(
             [

time: 359 us -> 348 us (0.969)
  matrix products: 61.4 us -> 17.7 us
  Pallas kernels: 0 us -> 31.8 us
    pallas_call x0 -> x1, Pallas kernels: none -> 31.8 us  [expert_blocks(): pl.pallas_call(ffn_kernel, out_shape=jax.ShapeDtypeStruct((sources, slots...]
    dot_general x2 -> x1, matrix products: 31 us -> 1.18 us  [expert_apply(): jnp.dot(hidden, down_matrix, preferred_element_type=jnp.float32)]
    dot_general x2 -> x1, matrix products: 15.1 us -> 1.26 us  [expert_apply(): up_part = jnp.dot(row_block, up_matrix, preferred_element_type=jnp.float32)]
  transfers between devices with their start and end apart: 2 -> 2, of which waited for: 1 -> 1; matrix products, arithmetic and copies ran while one was open for 14% -> 2% of each run, Pallas kernels for 0% -> 9%
where the time goes in v6:
time: 348 us; the launch traced here: 347 us
  blocking collectives  140 us (40%)
  waiting for transfers between devices  127 us (36%)
  Pallas kernels  31.8 us (9%)
  matrix products  17.7 us (5%)
  starting transfers between devices  13.6 us (4%)
  other arithmetic  8.58 us (2%)
  local copies, waits for them, and re-layouts  8.35 us (2%)
    all_to_all x1, blocking collectives, shards(): lax.all_to_all(outgoing, 'expert', split_axis=0, concat_axis=0, tiled=True)  140 us
    all_to_all x2, waiting for transfers between devices, shards(): lax.all_to_all(answered, 'expert', split_axis=0, concat_axis=0, tiled=True)  127 us
    pallas_call x1, Pallas kernels, expert_blocks(): pl.pallas_call(ffn_kernel, out_shape=jax.ShapeDtypeStruct((sources, slots...  31.8 us
    all_to_all x2, starting transfers between devices, shards(): lax.all_to_all(answered, 'expert', split_axis=0, concat_axis=0, tiled=True)  13.6 us
    dot_general x2, matrix products, shards(): jnp.einsum('ptes,esd->ptd', stacked, returned, preferred_element_type=jnp...  10.7 us
  transfers between devices with their start and end apart: 2, of which 1 were waited for; matrix products, arithmetic and copies ran while one was open for 2% of the time, Pallas kernels for 9%

profile of v6, /device:TPU:0, one launch (start us, length us, event | category | flops | bytes accessed | tf_op | source)
XLA Modules:
  0.0 347.1 jit_solution(18007533231144008511)
XLA Ops:
  0.0 0.0 copy-start
  0.0 0.9 copy.51
  0.9 0.1 eq.49
  1.0 0.1 eq.45
  1.2 1.7 reduce-window.6
  2.9 0.3 slice_reduce_fusion
  3.2 0.1 fusion.42
  3.3 0.1 reduce_sum.84
  3.4 0.1 copy.54
  3.5 0.7 multiply_add_fusion.1
  4.2 1.5 broadcast_compare_fusion
  5.7 0.0 copy-done
  5.7 3.4 convolution_convert_fusion
  9.1 0.0 copy-start.6
  9.1 140.0 %all_to_all.15.x_ref = bf16[32,72,2560]{2,1,0:T(8,128)(2,1)S(1)} all-to-all(bf16[32,72,2560]{2,1,0:T(8,128)(2,1)S(1)} %convolution_convert_fusion), channel_id=1, replica_groups=mesh['dp'=4,'expert'=32] {'expert'}, dimensions={0} | all-to-all | bytes 23592960 | tf_op jit(solution)/shard_map/all_to_all | solution.py:142
  149.1 1.2 fusion.9
  150.3 3.8 %copy-done.5 = bf16[1,2560,768]{2,1,0:T(8,128)(2,1)S(1)} copy-done((bf16[1,2560,768]{2,1,0:T(8,128)(2,1)S(1)}, bf16[1,2560,768]{2,1,0:T(8,128)(2,1)}, u32[]{:S(2)}) %copy-start.5) | copy-done | bytes 3932184
  154.1 1.3 fusion.28
  155.4 1.2 copy-done.4
  156.6 1.2 fusion.11
  157.7 0.0 copy-done.2
  157.7 1.8 copy.59
  159.5 5.9 %all-to-all-start.1 = ((bf16[32,8,2560]{2,1,0:T(8,128)(2,1)}), bf16[32,8,2560]{2,1,0:T(8,128)(2,1)}, u32[]{:S(2)}, u32[]{:S(2)}) async-start(bf16[32,8,2560]{2,1,0:T(8,128)(2,1)} %copy.59), calls=%async_computation.1 | async-start | bytes 2621440 | tf_op jit(solution)/shard_map/all_to_all | solution.py:152
  165.4 31.8 %shard_map.64 = bf16[32,64,2560]{2,1,0:T(8,128)(2,1)} custom-call(bf16[32,72,2560]{2,1,0:T(8,128)(2,1)} %copy-done.2, bf16[2560,768]{1,0:T(8,128)(2,1)} %bitcast.85, bf16[2560,768]{1,0:T(8,128)(2,1)} %bitcast.84, bf16[768,2560]{1,0:T(8,128)(2,1)} %bitcast.83), custom_call_target="tpu_custom_call" | custom-call | flops 24159191040 | bytes 32768000 | tf_op jit(solution)/shard_map/pallas_call | solution.py:86
  197.2 0.0 all-to-all-done.1
  197.2 7.7 %all-to-all-start.2 = ((bf16[32,64,2560]{2,1,0:T(8,128)(2,1)}), bf16[32,64,2560]{2,1,0:T(8,128)(2,1)}, u32[]{:S(2)}, u32[]{:S(2)}) async-start(bf16[32,64,2560]{2,1,0:T(8,128)(2,1)} %shard_map.64), calls=%async_computation.2 | async-start | bytes 20971520 | tf_op jit(solution)/shard_map/all_to_all | solution.py:152
  205.0 0.2 select_reduce_fusion.5
  205.2 3.3 select_reduce_fusion.2
  208.5 2.2 fusion.14
  210.7 126.8 %all-to-all-done.2 = bf16[32,64,2560]{2,1,0:T(8,128)(2,1)} async-done(((bf16[32,64,2560]{2,1,0:T(8,128)(2,1)}), bf16[32,64,2560]{2,1,0:T(8,128)(2,1)}, u32[]{:S(2)}, u32[]{:S(2)}) %all-to-all-start.2) | async-done | bytes 10485792 | tf_op jit(solution)/shard_map/all_to_all | solution.py:152
  337.5 8.5 %fusion.15 = f32[128,2560]{1,0:T(8,128)S(1)} fusion(bf16[32,64,2560]{2,1,0:T(8,128)(2,1)} %all-to-all-done.2, bf16[1,128,32,64]{1,3,2,0:T(8,128)(2,1)} %bitcast.80, bf16[1,128,32,64]{1,3,2,0:T(8,128)(2,1)S(1)} %bitcast.79, bf16[1,128,32,64]{1,3,2,0:T(8,128)(2,1)S(1)} %bitcast.78), kind=kOutput, calls=%fused_computation.17 | convolution fusion | flops 4028760064 | bytes 13369344 | tf_op jit(solution)/shard_map/ptes,esd->ptd/dot_general | solution.py:164
  346.0 1.0 add_convert_fusion
  (14 shorter events, 0.1 us)
Async XLA Ops:
  0.0 5.7 %copy-start = (bf16[128,2560]{1,0:T(8,128)(2,1)S(1)}, bf16[128,2560]{1,0:T(8,128)(2,1)}, u32[]{:S(2)}) copy-start(bf16[128,2560]{1,0:T(8,128)(2,1)} %param.6) | copy-start | bytes 1966084
  9.1 140.0 %copy-start.6 = (bf16[1,2560,768]{2,1,0:T(8,128)(2,1)S(1)}, bf16[1,2560,768]{2,1,0:T(8,128)(2,1)}, u32[]{:S(2)}) copy-start(bf16[1,2560,768]{2,1,0:T(8,128)(2,1)} %param.9) | copy-start | bytes 11796484
  149.1 8.7 %copy-start.2 = (bf16[32,72,2560]{2,1,0:T(8,128)(2,1)}, bf16[32,72,2560]{2,1,0:T(8,128)(2,1)S(1)}, u32[]{:S(2)}) copy-start(bf16[32,72,2560]{2,1,0:T(8,128)(2,1)S(1)} %all_to_all.15.x_ref) | copy-start | bytes 35389444
  149.1 5.0 %copy-start.5 = (bf16[1,2560,768]{2,1,0:T(8,128)(2,1)S(1)}, bf16[1,2560,768]{2,1,0:T(8,128)(2,1)}, u32[]{:S(2)}) copy-start(bf16[1,2560,768]{2,1,0:T(8,128)(2,1)} %param.10) | copy-start | bytes 11796484
  154.1 2.4 copy-start.4
  159.5 37.7 %all-to-all-start.1 = ((bf16[32,8,2560]{2,1,0:T(8,128)(2,1)}), bf16[32,8,2560]{2,1,0:T(8,128)(2,1)}, u32[]{:S(2)}, u32[]{:S(2)}) async-start(bf16[32,8,2560]{2,1,0:T(8,128)(2,1)} %copy.59), calls=%async_computation.1 | async-start | bytes 2621440 | tf_op jit(solution)/shard_map/all_to_all | solution.py:152
  197.2 7.8 %copy-start.3 = (f32[128,6]{0,1:T(8,128)S(1)}, f32[128,6]{0,1:T(8,128)}, u32[]{:S(2)}) copy-start(f32[128,6]{0,1:T(8,128)} %param.8) | copy-start | bytes 9220
  197.2 140.3 %all-to-all-start.2 = ((bf16[32,64,2560]{2,1,0:T(8,128)(2,1)}), bf16[32,64,2560]{2,1,0:T(8,128)(2,1)}, u32[]{:S(2)}, u32[]{:S(2)}) async-start(bf16[32,64,2560]{2,1,0:T(8,128)(2,1)} %shard_map.64), calls=%async_computation.2 | async-start | bytes 20971520 | tf_op jit(solution)/shard_map/all_to_all | solution.py:152
  337.5 9.5 %copy-start.1 = (bf16[128,2560]{1,0:T(8,128)(2,1)S(1)}, bf16[128,2560]{1,0:T(8,128)(2,1)}, u32[]{:S(2)}) copy-start(bf16[128,2560]{1,0:T(8,128)(2,1)} %param.6) | copy-start | bytes 1966084

commit v7 on v6

--- a/solution.py
+++ b/solution.py
@@ -72,7 +72,8 @@
     return jnp.dot(hidden, down_matrix, preferred_element_type=jnp.float32).astype(jnp.bfloat16)
 
 
-def ffn_kernel(x_ref, gate_ref, up_ref, down_ref, out_ref):
+def ffn_kernel(x_ref, gate_ref, up_ref, down_ref, *refs):
+    out_ref = refs[-1]
     sources, slots, features = x_ref.shape
     rows = x_ref[...].reshape(sources * slots, features)
     out_ref[...] = expert_apply(rows, gate_ref[...], up_ref[...], down_ref[...]).reshape(
@@ -80,27 +81,29 @@
     )
 
 
-def expert_blocks(received, gate_matrix, up_matrix, down_matrix, slots, per_step):
-    sources, _, features = received.shape
+def expert_blocks(received, gate_matrix, up_matrix, down_matrix, per_step, into, slot_block):
+    sources, slots, features = received.shape
     hidden = gate_matrix.shape[1]
     return pl.pallas_call(
         ffn_kernel,
-        out_shape=jax.ShapeDtypeStruct((sources, slots, features), received.dtype),
+        out_shape=jax.ShapeDtypeStruct(into.shape, into.dtype),
         grid=(sources // per_step,),
         in_specs=[
             pl.BlockSpec((per_step, slots, features), lambda i: (i, 0, 0)),
             pl.BlockSpec((features, hidden), lambda i: (0, 0)),
             pl.BlockSpec((features, hidden), lambda i: (0, 0)),
             pl.BlockSpec((hidden, features), lambda i: (0, 0)),
+            pl.BlockSpec(memory_space=pl.ANY),
         ],
-        out_specs=pl.BlockSpec((per_step, slots, features), lambda i: (i, 0, 0)),
+        out_specs=pl.BlockSpec((per_step, slots, features), lambda i: (i, slot_block, 0)),
+        input_output_aliases={4: 0},
         compiler_params=pltpu.CompilerParams(vmem_limit_bytes=60 * 1024 * 1024),
         cost_estimate=pl.CostEstimate(
             flops=6 * sources * slots * features * hidden,
             transcendentals=sources * slots * hidden,
             bytes_accessed=2 * (2 * sources * slots * features + 3 * features * hidden),
         ),
-    )(received, gate_matrix, up_matrix, down_matrix)
+    )(received, gate_matrix, up_matrix, down_matrix, into)
 
 
 def split_bf16(values):
@@ -136,34 +139,26 @@
         places[:, :, None] == jnp.arange(buffer_rows, dtype=jnp.int32)[None, None, :]
     ).reshape(token_count, topk_width, experts_all, slot_bound)
     pick = jnp.any(hit, axis=1).astype(jnp.bfloat16)
-    outgoing = jnp.einsum(
-        "tes,td->esd", pick, tokens, preferred_element_type=jnp.float32
+    small = slot_bound // 9
+    answered = jnp.zeros((experts_all, slot_bound, features), jnp.bfloat16)
+    for begin, end in ((0, slot_bound - small), (slot_bound - small, slot_bound)):
+        outgoing = jnp.einsum(
+            "tes,td->esd", pick[:, :, begin:end], tokens, preferred_element_type=jnp.float32
+        ).astype(jnp.bfloat16)
+        received = lax.all_to_all(outgoing, "expert", split_axis=0, concat_axis=0, tiled=True)
+        answered = expert_blocks(
+            received, w_gate[0], w_up[0], w_down[0], 4, answered, begin // (end - begin)
+        )
+    returned = lax.all_to_all(answered, "expert", split_axis=0, concat_axis=0, tiled=True)
+
+    stacked = jnp.stack(
+        [
+            jnp.sum(jnp.where(hit, part.astype(jnp.float32)[:, :, None, None], 0.0), axis=1)
+            for part in split_bf16(gate_values)
+        ]
     ).astype(jnp.bfloat16)
-    received = lax.all_to_all(outgoing, "expert", split_axis=0, concat_axis=0, tiled=True)
-
-    large = slot_bound - slot_bound // 9
-    weight_parts = split_bf16(gate_values)
-    summed = None
-    for begin, end in ((large, slot_bound), (0, large)):
-        if begin == 0:
-            answered = expert_blocks(received, w_gate[0], w_up[0], w_down[0], end, 4)
-        else:
-            answered = expert_apply(received[:, begin:end], w_gate[0], w_up[0], w_down[0])
-        returned = lax.all_to_all(answered, "expert", split_axis=0, concat_axis=0, tiled=True)
-        stacked = jnp.stack(
-            [
-                jnp.sum(
-                    jnp.where(
-                        hit[:, :, :, begin:end], part.astype(jnp.float32)[:, :, None, None], 0.0
-                    ),
-                    axis=1,
-                )
-                for part in weight_parts
-            ]
-        ).astype(jnp.bfloat16)
-        terms = jnp.einsum("ptes,esd->ptd", stacked, returned, preferred_element_type=jnp.float32)
-        term = jnp.sum(terms, axis=0)
-        summed = term if summed is None else summed + term
+    terms = jnp.einsum("ptes,esd->ptd", stacked, returned, preferred_element_type=jnp.float32)
+    summed = jnp.sum(terms, axis=0)
     return summed.astype(jnp.bfloat16)
 
 

time: 348 us -> 384 us (1.10)
  waiting for transfers between devices: 127 us -> 279 us
  blocking collectives: 140 us -> 0 us
  Pallas kernels: 31.8 us -> 54.2 us
  starting transfers between devices: 13.6 us -> 19.3 us
    all_to_all x1 -> x0, blocking collectives: 140 us -> none  [shards(): lax.all_to_all(outgoing, 'expert', split_axis=0, concat_axis=0, tiled=True)]
    all_to_all x0 -> x2, waiting for transfers between devices: none -> 131 us  [shards(): lax.all_to_all(outgoing, 'expert', split_axis=0, concat_axis=0, tiled=True)]
    pallas_call x1 -> x2, Pallas kernels: 31.8 us -> 54.2 us  [expert_blocks(): pl.pallas_call(ffn_kernel, out_shape=jax.ShapeDtypeStruct(into.shape, int...]
    all_to_all x2 -> x1, waiting for transfers between devices: 127 us -> 148 us  [shards(): lax.all_to_all(answered, 'expert', split_axis=0, concat_axis=0, tiled=True)]
    all_to_all x0 -> x2, starting transfers between devices: none -> 11.5 us  [shards(): lax.all_to_all(outgoing, 'expert', split_axis=0, concat_axis=0, tiled=True)]
    all_to_all x2 -> x1, starting transfers between devices: 13.6 us -> 7.81 us  [shards(): lax.all_to_all(answered, 'expert', split_axis=0, concat_axis=0, tiled=True)]
    broadcast_in_dim x0 -> x1, local copies, waits for them, and re-layouts: none -> 5.17 us  [shards(): answered = jnp.zeros((experts_all, slot_bound, features), jnp.bfloat16)]
    unnamed x15 -> x7, local copies, waits for them, and re-layouts: 5.83 us -> 1.97 us
  transfers between devices with their start and end apart: 2 -> 3, of which waited for: 1 -> 2; matrix products, arithmetic and copies ran while one was open for 2% -> 2% of each run, Pallas kernels for 9% -> 8%
where the time goes in v7:
time: 384 us
  waiting for transfers between devices  279 us (73%)
  Pallas kernels  54.2 us (14%)
  starting transfers between devices  19.3 us (5%)
  matrix products  17.1 us (4%)
  local copies, waits for them, and re-layouts  7.85 us (2%)
  other arithmetic  5.85 us (2%)
    all_to_all x1, waiting for transfers between devices, shards(): lax.all_to_all(answered, 'expert', split_axis=0, concat_axis=0, tiled=True)  148 us
    all_to_all x2, waiting for transfers between devices, shards(): lax.all_to_all(outgoing, 'expert', split_axis=0, concat_axis=0, tiled=True)  131 us
    pallas_call x2, Pallas kernels, expert_blocks(): pl.pallas_call(ffn_kernel, out_shape=jax.ShapeDtypeStruct(into.shape, int...  54.2 us
    all_to_all x2, starting transfers between devices, shards(): lax.all_to_all(outgoing, 'expert', split_axis=0, concat_axis=0, tiled=True)  11.5 us
    dot_general x1, matrix products, shards(): jnp.einsum('ptes,esd->ptd', stacked, returned, preferred_element_type=jnp...  10.1 us
    all_to_all x1, starting transfers between devices, shards(): lax.all_to_all(answered, 'expert', split_axis=0, concat_axis=0, tiled=True)  7.81 us
  transfers between devices with their start and end apart: 3, of which 2 were waited for; matrix products, arithmetic and copies ran while one was open for 2% of the time, Pallas kernels for 8%

profile of v7, /device:TPU:0, one launch (start us, length us, event | category | flops | bytes accessed | tf_op | source)
XLA Modules:
  0.0 383.6 jit_solution(13017955327310480782)
XLA Ops:
  0.0 0.0 copy-start
  0.0 0.9 copy.27
  0.9 0.1 eq.49
  1.0 0.1 eq.45
  1.2 1.7 reduce-window.6
  2.9 0.3 slice_reduce_fusion
  3.2 0.1 fusion.24
  3.3 0.1 reduce_sum.48
  3.5 0.1 copy.30
  3.5 0.7 multiply_add_fusion.1
  4.2 1.1 compare_reduce_fusion
  5.3 0.0 copy-done
  5.3 5.4 %convolution_convert_fusion = bf16[32,64,2560]{2,1,0:T(8,128)(2,1)} fusion(pred[128,32,72]{0,2,1:T(8,128)(4,1)S(1)} %compare_reduce_fusion, bf16[128,2560]{1,0:T(8,128)(2,1)S(1)} %copy-done), kind=kOutput, calls=%fused_computation.6 | convolution fusion | flops 1347420160 | bytes 11403264 | tf_op jit(solution)/shard_map/tes,td->esd/dot_general | solution.py:145
  10.7 7.5 %all-to-all-start.1 = ((bf16[32,64,2560]{2,1,0:T(8,128)(2,1)}), bf16[32,64,2560]{2,1,0:T(8,128)(2,1)}, u32[]{:S(2)}, u32[]{:S(2)}) async-start(bf16[32,64,2560]{2,1,0:T(8,128)(2,1)} %convolution_convert_fusion), calls=%async_computation.1 | async-start | bytes 20971520 | tf_op jit(solution)/shard_map/all_to_all | solution.py:148
  18.3 1.6 convolution_convert_fusion.1
  19.9 131.1 %all-to-all-done.1.x_ref = bf16[32,64,2560]{2,1,0:T(8,128)(2,1)} async-done(((bf16[32,64,2560]{2,1,0:T(8,128)(2,1)}), bf16[32,64,2560]{2,1,0:T(8,128)(2,1)}, u32[]{:S(2)}, u32[]{:S(2)}) %all-to-all-start.1) | async-done | bytes 10485792 | tf_op jit(solution)/shard_map/all_to_all | solution.py:148
  151.0 3.9 %all-to-all-start = ((bf16[32,8,2560]{2,1,0:T(8,128)(2,1)}), bf16[32,8,2560]{2,1,0:T(8,128)(2,1)S(1)}, u32[]{:S(2)}, u32[]{:S(2)}) async-start(bf16[32,8,2560]{2,1,0:T(8,128)(2,1)} %convolution_convert_fusion.1), calls=%async_computation | async-start | bytes 2621440 | tf_op jit(solution)/shard_map/all_to_all | solution.py:148
  155.0 5.2 %broadcast_in_dim.36.refs_0_ = bf16[32,72,2560]{2,1,0:T(8,128)(2,1)} broadcast(bf16[]{:T(256)} %constant.14.clone.1), dimensions={} | broadcast | bytes 11796482 | tf_op jit(solution)/shard_map/broadcast_in_dim | solution.py:143
  160.1 31.8 %shard_map.64.refs_0_ = bf16[32,72,2560]{2,1,0:T(8,128)(2,1)} custom-call(bf16[32,64,2560]{2,1,0:T(8,128)(2,1)} %all-to-all-done.1.x_ref, bf16[2560,768]{1,0:T(8,128)(2,1)} %bitcast.49, bf16[2560,768]{1,0:T(8,128)(2,1)} %bitcast.51, bf16[768,2560]{1,0:T(8,128)(2,1)} %bitcast.53, ...), custom_call_target="tpu_custom_call", output_to_operand_aliasing={{}: (4, {})} | custom-call | flops 24159191040 | bytes 32768000 | tf_op jit(solution)/shard_map/pallas_call | solution.py:87
  191.9 0.0 all-to-all-done.x_ref
  191.9 0.0 copy-start.1
  191.9 1.1 copy-done.1
  193.0 22.4 %shard_map.65 = bf16[32,72,2560]{2,1,0:T(8,128)(2,1)} custom-call(bf16[32,8,2560]{2,1,0:T(8,128)(2,1)} %copy-done.1, bf16[2560,768]{1,0:T(8,128)(2,1)} %bitcast.50, bf16[2560,768]{1,0:T(8,128)(2,1)} %bitcast.52, bf16[768,2560]{1,0:T(8,128)(2,1)} %bitcast.54, bf16[32,72,2560]{2,1,0:T(8,128)(2,1)} %shard_map.64.refs_0_), custom_call_target="tpu_custom_call", output_to_operand_aliasing={{}: (4, {})} | custom-call | flops 3019898880 | bytes 14417920 | tf_op jit(solution)/shard_map/pallas_call | solution.py:87
  215.4 0.0 copy-start.2
  215.4 7.8 %all-to-all-start.2 = ((bf16[32,72,2560]{2,1,0:T(8,128)(2,1)}), bf16[32,72,2560]{2,1,0:T(8,128)(2,1)}, u32[]{:S(2)}, u32[]{:S(2)}) async-start(bf16[32,72,2560]{2,1,0:T(8,128)(2,1)} %shard_map.65), calls=%async_computation.2 | async-start | bytes 23592960 | tf_op jit(solution)/shard_map/all_to_all | solution.py:152
  223.3 0.0 copy-done.2
  223.3 2.2 fusion.2
  225.4 148.1 %all-to-all-done.2 = bf16[32,72,2560]{2,1,0:T(8,128)(2,1)} async-done(((bf16[32,72,2560]{2,1,0:T(8,128)(2,1)}), bf16[32,72,2560]{2,1,0:T(8,128)(2,1)}, u32[]{:S(2)}, u32[]{:S(2)}) %all-to-all-start.2) | async-done | bytes 11796512 | tf_op jit(solution)/shard_map/all_to_all | solution.py:152
  373.5 10.1 %fusion.13 = bf16[128,2560]{1,0:T(8,128)(2,1)} fusion(bf16[32,72,2560]{2,1,0:T(8,128)(2,1)} %all-to-all-done.2, bf16[1,128,32,72]{1,3,2,0:T(8,128)(2,1)S(1)} %bitcast.56, bf16[1,128,32,72]{1,3,2,0:T(8,128)(2,1)S(1)} %bitcast.57, bf16[1,128,32,72]{1,3,2,0:T(8,128)(2,1)S(1)} %bitcast.55), kind=kOutput, calls=%fused_computation.17 | convolution fusion | flops 4532273152 | bytes 14221312 | tf_op jit(solution)/shard_map/ptes,esd->ptd/dot_general | solution.py:160
  (4 shorter events, 0.0 us)
Async XLA Ops:
  0.0 5.3 %copy-start = (bf16[128,2560]{1,0:T(8,128)(2,1)S(1)}, bf16[128,2560]{1,0:T(8,128)(2,1)}, u32[]{:S(2)}) copy-start(bf16[128,2560]{1,0:T(8,128)(2,1)} %param.6) | copy-start | bytes 1966084
  10.7 140.3 %all-to-all-start.1 = ((bf16[32,64,2560]{2,1,0:T(8,128)(2,1)}), bf16[32,64,2560]{2,1,0:T(8,128)(2,1)}, u32[]{:S(2)}, u32[]{:S(2)}) async-start(bf16[32,64,2560]{2,1,0:T(8,128)(2,1)} %convolution_convert_fusion), calls=%async_computation.1 | async-start | bytes 20971520 | tf_op jit(solution)/shard_map/all_to_all | solution.py:148
  151.0 40.9 %all-to-all-start = ((bf16[32,8,2560]{2,1,0:T(8,128)(2,1)}), bf16[32,8,2560]{2,1,0:T(8,128)(2,1)S(1)}, u32[]{:S(2)}, u32[]{:S(2)}) async-start(bf16[32,8,2560]{2,1,0:T(8,128)(2,1)} %convolution_convert_fusion.1), calls=%async_computation | async-start | bytes 2621440 | tf_op jit(solution)/shard_map/all_to_all | solution.py:148
  191.9 1.1 copy-start.1
  215.4 7.8 %copy-start.2 = (f32[128,6]{0,1:T(8,128)S(1)}, f32[128,6]{0,1:T(8,128)}, u32[]{:S(2)}) copy-start(f32[128,6]{0,1:T(8,128)} %param.8) | copy-start | bytes 9220
  215.4 158.1 %all-to-all-start.2 = ((bf16[32,72,2560]{2,1,0:T(8,128)(2,1)}), bf16[32,72,2560]{2,1,0:T(8,128)(2,1)}, u32[]{:S(2)}, u32[]{:S(2)}) async-start(bf16[32,72,2560]{2,1,0:T(8,128)(2,1)} %shard_map.65), calls=%async_computation.2 | async-start | bytes 23592960 | tf_op jit(solution)/shard_map/all_to_all | solution.py:152

commit v8 on v6

--- a/solution.py
+++ b/solution.py
@@ -80,7 +80,7 @@
     )
 
 
-def expert_blocks(received, gate_matrix, up_matrix, down_matrix, slots, per_step):
+def expert_blocks(received, gate_matrix, up_matrix, down_matrix, slots, per_step, slot_block):
     sources, _, features = received.shape
     hidden = gate_matrix.shape[1]
     return pl.pallas_call(
@@ -88,7 +88,7 @@
         out_shape=jax.ShapeDtypeStruct((sources, slots, features), received.dtype),
         grid=(sources // per_step,),
         in_specs=[
-            pl.BlockSpec((per_step, slots, features), lambda i: (i, 0, 0)),
+            pl.BlockSpec((per_step, slots, features), lambda i: (i, slot_block, 0)),
             pl.BlockSpec((features, hidden), lambda i: (0, 0)),
             pl.BlockSpec((features, hidden), lambda i: (0, 0)),
             pl.BlockSpec((hidden, features), lambda i: (0, 0)),
@@ -105,10 +105,8 @@
 
 def split_bf16(values):
     first = lax.reduce_precision(values, exponent_bits=8, mantissa_bits=7)
-    rest = values - first
-    second = lax.reduce_precision(rest, exponent_bits=8, mantissa_bits=7)
-    third = rest - second
-    return tuple(part.astype(jnp.bfloat16) for part in (first, second, third))
+    second = values - first
+    return tuple(part.astype(jnp.bfloat16) for part in (first, second))
 
 
 def shards(tokens, expert_ids, gate_values, w_gate, w_up, w_down):
@@ -145,10 +143,11 @@
     weight_parts = split_bf16(gate_values)
     summed = None
     for begin, end in ((large, slot_bound), (0, large)):
-        if begin == 0:
-            answered = expert_blocks(received, w_gate[0], w_up[0], w_down[0], end, 4)
-        else:
-            answered = expert_apply(received[:, begin:end], w_gate[0], w_up[0], w_down[0])
+        size = end - begin
+        per_step = 4 if begin == 0 else experts_all
+        answered = expert_blocks(
+            received, w_gate[0], w_up[0], w_down[0], size, per_step, begin // size
+        )
         returned = lax.all_to_all(answered, "expert", split_axis=0, concat_axis=0, tiled=True)
         stacked = jnp.stack(
             [

time: 348 us -> 344 us (0.989)
  Pallas kernels: 31.8 us -> 40.9 us
  local copies, waits for them, and re-layouts: 8.35 us -> 1.59 us
  matrix products: 17.7 us -> 12.4 us
    pallas_call x1 -> x2, Pallas kernels: 31.8 us -> 40.9 us  [expert_blocks(): pl.pallas_call(ffn_kernel, out_shape=jax.ShapeDtypeStruct((sources, slots...]
    unnamed x15 -> x5, local copies, waits for them, and re-layouts: 5.83 us -> 0.86 us
    dot_general x3 -> x0, matrix products: 3.68 us -> none  [the longest x1 1.26 us: expert_apply(): up_part = jnp.dot(row_block, up_matrix, preferred_element_type=jnp.float32)]
  transfers between devices with their start and end apart: 2 -> 2, of which waited for: 1 -> 1; matrix products, arithmetic and copies ran while one was open for 2% -> 1% of each run, Pallas kernels for 9% -> 9%
where the time goes in v8:
time: 344 us
  blocking collectives  140 us (41%)
  waiting for transfers between devices  129 us (38%)
  Pallas kernels  40.9 us (12%)
  starting transfers between devices  13.6 us (4%)
  matrix products  12.4 us (4%)
  other arithmetic  6.51 us (2%)
    all_to_all x1, blocking collectives, shards(): lax.all_to_all(outgoing, 'expert', split_axis=0, concat_axis=0, tiled=True)  140 us
    all_to_all x2, waiting for transfers between devices, shards(): lax.all_to_all(answered, 'expert', split_axis=0, concat_axis=0, tiled=True)  129 us
    pallas_call x2, Pallas kernels, expert_blocks(): pl.pallas_call(ffn_kernel, out_shape=jax.ShapeDtypeStruct((sources, slots...  40.9 us
    all_to_all x2, starting transfers between devices, shards(): lax.all_to_all(answered, 'expert', split_axis=0, concat_axis=0, tiled=True)  13.6 us
    dot_general x2, matrix products, shards(): jnp.einsum('ptes,esd->ptd', stacked, returned, preferred_element_type=jnp...  8.98 us
  transfers between devices with their start and end apart: 2, of which 1 were waited for; matrix products, arithmetic and copies ran while one was open for 1% of the time, Pallas kernels for 9%

profile of v8, /device:TPU:0, one launch (start us, length us, event | category | flops | bytes accessed | tf_op | source)
XLA Modules:
  0.0 344.0 jit_solution(4506898200397642600)
XLA Ops:
  0.0 0.0 copy-start
  0.0 0.9 copy.32
  0.9 0.1 eq.49
  1.0 0.1 eq.45
  1.2 1.7 reduce-window.6
  2.9 0.3 slice_reduce_fusion
  3.2 0.1 fusion.20
  3.3 0.1 reduce_sum.66
  3.4 0.1 copy.35
  3.5 0.7 multiply_add_fusion.1
  4.2 1.5 broadcast_compare_fusion
  5.7 0.0 copy-done
  5.7 3.4 convolution_convert_fusion
  9.1 139.8 %all_to_all.15.x_ref = bf16[32,72,2560]{2,1,0:T(8,128)(2,1)} all-to-all(bf16[32,72,2560]{2,1,0:T(8,128)(2,1)S(1)} %convolution_convert_fusion), channel_id=1, replica_groups=mesh['dp'=4,'expert'=32] {'expert'}, dimensions={0} | all-to-all | bytes 23592960 | tf_op jit(solution)/shard_map/all_to_all | solution.py:140
  148.9 9.1 %shard_map.64 = bf16[32,8,2560]{2,1,0:T(8,128)(2,1)} custom-call(bf16[32,72,2560]{2,1,0:T(8,128)(2,1)} %all_to_all.15.x_ref, bf16[2560,768]{1,0:T(8,128)(2,1)} %bitcast.57, bf16[2560,768]{1,0:T(8,128)(2,1)} %bitcast.59, bf16[768,2560]{1,0:T(8,128)(2,1)} %bitcast.61), custom_call_target="tpu_custom_call" | custom-call | flops 3019898880 | bytes 14417920 | tf_op jit(solution)/shard_map/pallas_call | solution.py:86
  158.0 5.9 %all-to-all-start.1 = ((bf16[32,8,2560]{2,1,0:T(8,128)(2,1)}), bf16[32,8,2560]{2,1,0:T(8,128)(2,1)}, u32[]{:S(2)}, u32[]{:S(2)}) async-start(bf16[32,8,2560]{2,1,0:T(8,128)(2,1)} %shard_map.64), calls=%async_computation.1 | async-start | bytes 2621440 | tf_op jit(solution)/shard_map/all_to_all | solution.py:151
  163.9 31.8 %shard_map.65 = bf16[32,64,2560]{2,1,0:T(8,128)(2,1)} custom-call(bf16[32,72,2560]{2,1,0:T(8,128)(2,1)} %all_to_all.15.x_ref, bf16[2560,768]{1,0:T(8,128)(2,1)} %bitcast.58, bf16[2560,768]{1,0:T(8,128)(2,1)} %bitcast.60, bf16[768,2560]{1,0:T(8,128)(2,1)} %bitcast.62), custom_call_target="tpu_custom_call" | custom-call | flops 24159191040 | bytes 32768000 | tf_op jit(solution)/shard_map/pallas_call | solution.py:86
  195.7 0.0 copy-start.1
  195.7 0.0 all-to-all-done.1
  195.7 7.7 %all-to-all-start.2 = ((bf16[32,64,2560]{2,1,0:T(8,128)(2,1)}), bf16[32,64,2560]{2,1,0:T(8,128)(2,1)}, u32[]{:S(2)}, u32[]{:S(2)}) async-start(bf16[32,64,2560]{2,1,0:T(8,128)(2,1)} %shard_map.65), calls=%async_computation.2 | async-start | bytes 20971520 | tf_op jit(solution)/shard_map/all_to_all | solution.py:151
  203.4 0.0 copy-done.1
  203.4 0.2 select_reduce_fusion.3
  203.6 1.3 select_reduce_fusion.1
  204.9 2.0 fusion.5
  206.9 129.0 %all-to-all-done.2 = bf16[32,64,2560]{2,1,0:T(8,128)(2,1)} async-done(((bf16[32,64,2560]{2,1,0:T(8,128)(2,1)}), bf16[32,64,2560]{2,1,0:T(8,128)(2,1)}, u32[]{:S(2)}, u32[]{:S(2)}) %all-to-all-start.2) | async-done | bytes 10485792 | tf_op jit(solution)/shard_map/all_to_all | solution.py:151
  336.0 6.9 %fusion.6 = f32[128,2560]{1,0:T(8,128)S(1)} fusion(bf16[32,64,2560]{2,1,0:T(8,128)(2,1)} %all-to-all-done.2, bf16[1,128,32,64]{1,3,2,0:T(8,128)(2,1)S(1)} %bitcast.64, bf16[1,128,32,64]{1,3,2,0:T(8,128)(2,1)S(1)} %bitcast.63), kind=kOutput, calls=%fused_computation.9 | convolution fusion | flops 2685206528 | bytes 12845056 | tf_op jit(solution)/shard_map/ptes,esd->ptd/dot_general | solution.py:163
  342.9 1.0 add_convert_fusion
  (5 shorter events, 0.1 us)
Async XLA Ops:
  0.0 5.7 %copy-start = (bf16[128,2560]{1,0:T(8,128)(2,1)S(1)}, bf16[128,2560]{1,0:T(8,128)(2,1)}, u32[]{:S(2)}) copy-start(bf16[128,2560]{1,0:T(8,128)(2,1)} %param.6) | copy-start | bytes 1966084
  158.0 37.7 %all-to-all-start.1 = ((bf16[32,8,2560]{2,1,0:T(8,128)(2,1)}), bf16[32,8,2560]{2,1,0:T(8,128)(2,1)}, u32[]{:S(2)}, u32[]{:S(2)}) async-start(bf16[32,8,2560]{2,1,0:T(8,128)(2,1)} %shard_map.64), calls=%async_computation.1 | async-start | bytes 2621440 | tf_op jit(solution)/shard_map/all_to_all | solution.py:151
  195.7 7.8 %copy-start.1 = (f32[128,6]{0,1:T(8,128)S(1)}, f32[128,6]{0,1:T(8,128)}, u32[]{:S(2)}) copy-start(f32[128,6]{0,1:T(8,128)} %param.8) | copy-start | bytes 9220
  195.7 140.3 %all-to-all-start.2 = ((bf16[32,64,2560]{2,1,0:T(8,128)(2,1)}), bf16[32,64,2560]{2,1,0:T(8,128)(2,1)}, u32[]{:S(2)}, u32[]{:S(2)}) async-start(bf16[32,64,2560]{2,1,0:T(8,128)(2,1)} %shard_map.65), calls=%async_computation.2 | async-start | bytes 20971520 | tf_op jit(solution)/shard_map/all_to_all | solution.py:151

commit v9 on v5

--- a/solution.py
+++ b/solution.py
@@ -10,26 +10,26 @@
 MESH = pl.DeviceIdType.MESH
 
 
-def exchange_kernel(n, x_ref, y_ref, send_sem, recv_sem, local_sem):
+def expert_apply(row_block, gate_matrix, up_matrix, down_matrix):
+    gate_part = jnp.dot(row_block, gate_matrix, preferred_element_type=jnp.float32)
+    up_part = jnp.dot(row_block, up_matrix, preferred_element_type=jnp.float32)
+    hidden = (jax.nn.silu(gate_part) * up_part).astype(jnp.bfloat16)
+    return jnp.dot(hidden, down_matrix, preferred_element_type=jnp.float32).astype(jnp.bfloat16)
+
+
+def ffn_kernel(
+    n, small_ref, large_ref, gate_ref, up_ref, down_ref, large_out, small_out,
+    held, send_sem, recv_sem, local_sem,
+):
+    step = pl.program_id(0)
     me = lax.axis_index("expert")
-    barrier = pltpu.get_barrier_semaphore()
-
-    def greet(k, carry):
-        pl.semaphore_signal(
-            barrier, inc=1, device_id={"expert": lax.rem(me + k, n)}, device_id_type=MESH
-        )
-        return carry
-
-    lax.fori_loop(1, n, greet, 0)
-    pl.semaphore_wait(barrier, n - 1)
-    local = pltpu.make_async_copy(x_ref.at[me], y_ref.at[me], local_sem)
-    local.start()
+    local = pltpu.make_async_copy(held.at[me], small_out.at[me], local_sem)
 
     def remote(k):
         target = lax.rem(me + k, n)
         return pltpu.make_async_remote_copy(
-            src_ref=x_ref.at[target],
-            dst_ref=y_ref.at[me],
+            src_ref=held.at[target],
+            dst_ref=small_out.at[me],
             send_sem=send_sem.at[k],
             recv_sem=recv_sem.at[k],
             device_id={"expert": target},
@@ -44,40 +44,82 @@
         remote(k).wait()
         return carry
 
-    lax.fori_loop(1, n, start, 0)
-    lax.fori_loop(1, n, finish, 0)
-    local.wait()
+    @pl.when(step == 0)
+    def _():
+        barrier = pltpu.get_barrier_semaphore()
+
+        def greet(k, carry):
+            pl.semaphore_signal(
+                barrier, inc=1, device_id={"expert": lax.rem(me + k, n)}, device_id_type=MESH
+            )
+            return carry
+
+        lax.fori_loop(1, n, greet, 0)
+        pl.semaphore_wait(barrier, n - 1)
+        sources, slots, features = small_ref.shape
+        rows = small_ref[...].reshape(sources * slots, features)
+        held[...] = expert_apply(rows, gate_ref[...], up_ref[...], down_ref[...]).reshape(
+            sources, slots, features
+        )
+        local.start()
+        lax.fori_loop(1, n, start, 0)
+
+    sources, slots, features = large_ref.shape
+    rows = large_ref[...].reshape(sources * slots, features)
+    large_out[...] = expert_apply(rows, gate_ref[...], up_ref[...], down_ref[...]).reshape(
+        sources, slots, features
+    )
+
+    @pl.when(step == pl.num_programs(0) - 1)
+    def _():
+        lax.fori_loop(1, n, finish, 0)
+        local.wait()
 
 
-def exchange(blocks, collective_id):
+def expert_blocks(received, gate_matrix, up_matrix, down_matrix, large, per_step):
     n = lax.axis_size("expert")
+    sources, slot_bound, features = received.shape
+    small = slot_bound - large
+    hidden = gate_matrix.shape[1]
     return pl.pallas_call(
-        functools.partial(exchange_kernel, n),
-        out_shape=jax.ShapeDtypeStruct(blocks.shape, blocks.dtype),
-        in_specs=[pl.BlockSpec(memory_space=pl.ANY)],
-        out_specs=pl.BlockSpec(memory_space=pl.ANY),
+        functools.partial(ffn_kernel, n),
+        out_shape=(
+            jax.ShapeDtypeStruct((sources, large, features), received.dtype),
+            jax.ShapeDtypeStruct((sources, small, features), received.dtype),
+        ),
+        grid=(sources // per_step,),
+        in_specs=[
+            pl.BlockSpec((sources, small, features), lambda i: (0, large // small, 0)),
+            pl.BlockSpec((per_step, large, features), lambda i: (i, 0, 0)),
+            pl.BlockSpec((features, hidden), lambda i: (0, 0)),
+            pl.BlockSpec((features, hidden), lambda i: (0, 0)),
+            pl.BlockSpec((hidden, features), lambda i: (0, 0)),
+        ],
+        out_specs=(
+            pl.BlockSpec((per_step, large, features), lambda i: (i, 0, 0)),
+            pl.BlockSpec(memory_space=pl.ANY),
+        ),
         scratch_shapes=[
+            pltpu.VMEM((sources, small, features), received.dtype),
             pltpu.SemaphoreType.DMA((n,)),
             pltpu.SemaphoreType.DMA((n,)),
             pltpu.SemaphoreType.DMA,
         ],
-        compiler_params=pltpu.CompilerParams(collective_id=collective_id, has_side_effects=True),
-    )(blocks)
-
-
-def expert_apply(row_block, gate_matrix, up_matrix, down_matrix):
-    gate_part = jnp.dot(row_block, gate_matrix, preferred_element_type=jnp.float32)
-    up_part = jnp.dot(row_block, up_matrix, preferred_element_type=jnp.float32)
-    hidden = (jax.nn.silu(gate_part) * up_part).astype(jnp.bfloat16)
-    return jnp.dot(hidden, down_matrix, preferred_element_type=jnp.float32).astype(jnp.bfloat16)
+        compiler_params=pltpu.CompilerParams(
+            collective_id=0, has_side_effects=True, vmem_limit_bytes=60 * 1024 * 1024
+        ),
+        cost_estimate=pl.CostEstimate(
+            flops=6 * sources * slot_bound * features * hidden,
+            transcendentals=sources * slot_bound * hidden,
+            bytes_accessed=2 * (2 * sources * slot_bound * features + 3 * features * hidden),
+        ),
+    )(received, received, gate_matrix, up_matrix, down_matrix)
 
 
 def split_bf16(values):
     first = lax.reduce_precision(values, exponent_bits=8, mantissa_bits=7)
-    rest = values - first
-    second = lax.reduce_precision(rest, exponent_bits=8, mantissa_bits=7)
-    third = rest - second
-    return tuple(part.astype(jnp.bfloat16) for part in (first, second, third))
+    second = values - first
+    return tuple(part.astype(jnp.bfloat16) for part in (first, second))
 
 
 def shards(tokens, expert_ids, gate_values, w_gate, w_up, w_down):
@@ -110,12 +152,12 @@
     ).astype(jnp.bfloat16)
     received = lax.all_to_all(outgoing, "expert", split_axis=0, concat_axis=0, tiled=True)
 
-    small = slot_bound // 9
+    large = slot_bound - slot_bound // 9
+    answered, returned_small = expert_blocks(received, w_gate[0], w_up[0], w_down[0], large, 4)
+    returned_large = lax.all_to_all(answered, "expert", split_axis=0, concat_axis=0, tiled=True)
     weight_parts = split_bf16(gate_values)
     summed = None
-    for begin, end in ((0, small), (small, slot_bound)):
-        answered = expert_apply(received[:, begin:end], w_gate[0], w_up[0], w_down[0])
-        returned = lax.all_to_all(answered, "expert", split_axis=0, concat_axis=0, tiled=True)
+    for begin, end, returned in ((large, slot_bound, returned_small), (0, large, returned_large)):
         stacked = jnp.stack(
             [
                 jnp.sum(

time: 359 us -> 336 us (0.936)
  matrix products: 61.4 us -> 12.4 us
  Pallas kernels: 0 us -> 40.8 us
  starting transfers between devices: 13.5 us -> 5.18 us
  local copies, waits for them, and re-layouts: 8.36 us -> 1.6 us
    dot_general x5 -> x0, matrix products: 47.3 us -> none  [the longest x2 31 us: expert_apply(): jnp.dot(hidden, down_matrix, preferred_element_type=jnp.float32)]
    pallas_call x0 -> x1, Pallas kernels: none -> 40.8 us  [expert_blocks(): pl.pallas_call(functools.partial(ffn_kernel, n), out_shape=(jax.ShapeDtyp...]
    all_to_all x2 -> x1, starting transfers between devices: 13.5 us -> 5.18 us  [shards(): lax.all_to_all(answered, 'expert', split_axis=0, concat_axis=0, tiled=True)]
    unnamed x15 -> x5, local copies, waits for them, and re-layouts: 5.83 us -> 0.87 us
    all_to_all x2 -> x1, waiting for transfers between devices: 127 us -> 129 us  [shards(): lax.all_to_all(answered, 'expert', split_axis=0, concat_axis=0, tiled=True)]
  transfers between devices with their start and end apart: 2 -> 1, of which waited for: 1 -> 1; matrix products, arithmetic and copies ran while one was open for 14% -> 1% of each run, Pallas kernels for 0% -> 0%
where the time goes in v9:
time: 336 us; the launch traced here: 335 us
  blocking collectives  140 us (42%)
  waiting for transfers between devices  129 us (38%)
  Pallas kernels  40.8 us (12%)
  matrix products  12.4 us (4%)
  other arithmetic  6.51 us (2%)
  starting transfers between devices  5.18 us (2%)
    all_to_all x1, blocking collectives, shards(): lax.all_to_all(outgoing, 'expert', split_axis=0, concat_axis=0, tiled=True)  140 us
    all_to_all x1, waiting for transfers between devices, shards(): lax.all_to_all(answered, 'expert', split_axis=0, concat_axis=0, tiled=True)  129 us
    pallas_call x1, Pallas kernels, expert_blocks(): pl.pallas_call(functools.partial(ffn_kernel, n), out_shape=(jax.ShapeDtyp...  40.8 us
    dot_general x2, matrix products, shards(): jnp.einsum('ptes,esd->ptd', stacked, returned, preferred_element_type=jnp...  8.98 us
  transfers between devices with their start and end apart: 1, of which 1 were waited for; matrix products, arithmetic and copies ran while one was open for 1% of the time, Pallas kernels for 0%

profile of v9, /device:TPU:0, one launch (start us, length us, event | category | flops | bytes accessed | tf_op | source)
XLA Modules:
  0.0 335.5 jit_solution(17796773747559295347)
XLA Ops:
  0.0 0.0 copy-start
  0.0 0.9 copy.32
  0.9 0.1 eq.49
  1.0 0.1 eq.45
  1.2 1.7 reduce-window.6
  2.9 0.3 slice_reduce_fusion
  3.2 0.1 fusion.20
  3.3 0.1 reduce_sum.66
  3.4 0.1 copy.35
  3.5 0.7 multiply_add_fusion.1
  4.2 1.5 broadcast_compare_fusion
  5.7 0.0 copy-done
  5.7 3.4 %convolution_convert_fusion = bf16[32,72,2560]{2,1,0:T(8,128)(2,1)S(1)} fusion(pred[128,32,72]{0,2,1:T(8,128)(4,1)S(1)} %get-tuple-element.14, bf16[128,2560]{1,0:T(8,128)(2,1)S(1)} %copy-done), kind=kOutput, calls=%fused_computation.2 | convolution fusion | flops 1515847680 | bytes 12746752 | tf_op jit(solution)/shard_map/tes,td->esd/dot_general | solution.py:150
  9.1 139.8 %all_to_all.10.small_ref.large_ref = bf16[32,72,2560]{2,1,0:T(8,128)(2,1)} all-to-all(bf16[32,72,2560]{2,1,0:T(8,128)(2,1)S(1)} %convolution_convert_fusion), channel_id=1, replica_groups=mesh['dp'=4,'expert'=32] {'expert'}, dimensions={0} | all-to-all | bytes 23592960 | tf_op jit(solution)/shard_map/all_to_all | solution.py:153
  148.9 40.8 %shard_map.64 = (bf16[32,64,2560]{2,1,0:T(8,128)(2,1)}, bf16[32,8,2560]{2,1,0:T(8,128)(2,1)}) custom-call(bf16[32,72,2560]{2,1,0:T(8,128)(2,1)} %all_to_all.10.small_ref.large_ref, bf16[32,72,2560]{2,1,0:T(8,128)(2,1)} %all_to_all.10.small_ref.large_ref, bf16[2560,768]{1,0:T(8,128)(2,1)} %bitcast.60, bf16[2560,768]{1,0:T(8,128)(2,1)} %bitcast.61, ...), custom_call_target="tpu_custom_call" | custom-call | flops 27179089920 | bytes 35389440 | tf_op jit(solution)/shard_map/pallas_call | solution.py:84
  189.7 0.0 copy-start.1
  189.7 5.2 %all-to-all-start.1 = ((bf16[32,64,2560]{2,1,0:T(8,128)(2,1)}), bf16[32,64,2560]{2,1,0:T(8,128)(2,1)}, u32[]{:S(2)}, u32[]{:S(2)}) async-start(bf16[32,64,2560]{2,1,0:T(8,128)(2,1)} %get-tuple-element.8), calls=%async_computation.1 | async-start | bytes 20971520 | tf_op jit(solution)/shard_map/all_to_all | solution.py:157
  194.9 0.0 copy-done.1
  194.9 0.2 select_reduce_fusion.3
  195.1 1.3 select_reduce_fusion.1
  196.4 2.0 fusion.5
  198.4 129.1 %all-to-all-done.1 = bf16[32,64,2560]{2,1,0:T(8,128)(2,1)} async-done(((bf16[32,64,2560]{2,1,0:T(8,128)(2,1)}), bf16[32,64,2560]{2,1,0:T(8,128)(2,1)}, u32[]{:S(2)}, u32[]{:S(2)}) %all-to-all-start.1) | async-done | bytes 10485792 | tf_op jit(solution)/shard_map/all_to_all | solution.py:157
  327.5 6.9 %fusion.6 = f32[128,2560]{1,0:T(8,128)S(1)} fusion(bf16[32,64,2560]{2,1,0:T(8,128)(2,1)} %all-to-all-done.1, bf16[1,128,32,64]{1,3,2,0:T(8,128)(2,1)S(1)} %bitcast.58, bf16[1,128,32,64]{1,3,2,0:T(8,128)(2,1)S(1)} %bitcast.57), kind=kOutput, calls=%fused_computation.9 | convolution fusion | flops 2685206528 | bytes 12845056 | tf_op jit(solution)/shard_map/ptes,esd->ptd/dot_general | solution.py:172
  334.5 1.0 add_convert_fusion
  (5 shorter events, 0.1 us)
Async XLA Ops:
  0.0 5.7 %copy-start = (bf16[128,2560]{1,0:T(8,128)(2,1)S(1)}, bf16[128,2560]{1,0:T(8,128)(2,1)}, u32[]{:S(2)}) copy-start(bf16[128,2560]{1,0:T(8,128)(2,1)} %param.6) | copy-start | bytes 1966084
  189.7 5.2 %copy-start.1 = (f32[128,6]{0,1:T(8,128)S(1)}, f32[128,6]{0,1:T(8,128)}, u32[]{:S(2)}) copy-start(f32[128,6]{0,1:T(8,128)} %param.8) | copy-start | bytes 9220
  189.7 137.8 %all-to-all-start.1 = ((bf16[32,64,2560]{2,1,0:T(8,128)(2,1)}), bf16[32,64,2560]{2,1,0:T(8,128)(2,1)}, u32[]{:S(2)}, u32[]{:S(2)}) async-start(bf16[32,64,2560]{2,1,0:T(8,128)(2,1)} %get-tuple-element.8), calls=%async_computation.1 | async-start | bytes 20971520 | tf_op jit(solution)/shard_map/all_to_all | solution.py:157

commit v10 on v9

--- a/solution.py
+++ b/solution.py
@@ -116,6 +116,36 @@
     )(received, received, gate_matrix, up_matrix, down_matrix)
 
 
+def combine_kernel(weights_ref, returned_ref, partial_ref, out_ref):
+    total = partial_ref[...]
+    for part in range(weights_ref.shape[0]):
+        total = total + jnp.dot(
+            weights_ref[part], returned_ref[...], preferred_element_type=jnp.float32
+        )
+    out_ref[...] = total.astype(out_ref.dtype)
+
+
+def combine(weights, returned, partial, columns):
+    parts, tokens, rows = weights.shape
+    features = returned.shape[1]
+    return pl.pallas_call(
+        combine_kernel,
+        out_shape=jax.ShapeDtypeStruct((tokens, features), jnp.bfloat16),
+        grid=(features // columns,),
+        in_specs=[
+            pl.BlockSpec((parts, tokens, rows), lambda j: (0, 0, 0)),
+            pl.BlockSpec((rows, columns), lambda j: (0, j)),
+            pl.BlockSpec((tokens, columns), lambda j: (0, j)),
+        ],
+        out_specs=pl.BlockSpec((tokens, columns), lambda j: (0, j)),
+        cost_estimate=pl.CostEstimate(
+            flops=2 * parts * tokens * rows * features,
+            transcendentals=0,
+            bytes_accessed=2 * rows * features + 6 * tokens * features,
+        ),
+    )(weights, returned, partial)
+
+
 def split_bf16(values):
     first = lax.reduce_precision(values, exponent_bits=8, mantissa_bits=7)
     second = values - first
@@ -156,9 +186,8 @@
     answered, returned_small = expert_blocks(received, w_gate[0], w_up[0], w_down[0], large, 4)
     returned_large = lax.all_to_all(answered, "expert", split_axis=0, concat_axis=0, tiled=True)
     weight_parts = split_bf16(gate_values)
-    summed = None
-    for begin, end, returned in ((large, slot_bound, returned_small), (0, large, returned_large)):
-        stacked = jnp.stack(
+    stacked = [
+        jnp.stack(
             [
                 jnp.sum(
                     jnp.where(
@@ -169,10 +198,18 @@
                 for part in weight_parts
             ]
         ).astype(jnp.bfloat16)
-        terms = jnp.einsum("ptes,esd->ptd", stacked, returned, preferred_element_type=jnp.float32)
-        term = jnp.sum(terms, axis=0)
-        summed = term if summed is None else summed + term
-    return summed.astype(jnp.bfloat16)
+        for begin, end in ((large, slot_bound), (0, large))
+    ]
+    small_terms = jnp.einsum(
+        "ptes,esd->ptd", stacked[0], returned_small, preferred_element_type=jnp.float32
+    )
+    parts = len(weight_parts)
+    return combine(
+        stacked[1].reshape(parts, token_count, experts_all * large),
+        returned_large.reshape(experts_all * large, features),
+        jnp.sum(small_terms, axis=0),
+        512,
+    )
 
 
 def solution(mesh):

time: 336 us -> 336 us (level)
  Pallas kernels: 40.8 us -> 49 us
  matrix products: 12.4 us -> 6.49 us
  waiting for transfers between devices: 129 us -> 125 us
    pallas_call x0 -> x1, Pallas kernels: none -> 8.2 us  [combine(): pl.pallas_call(combine_kernel, out_shape=jax.ShapeDtypeStruct((tokens, fe...]
    dot_general x2 -> x1, matrix products: 8.98 us -> 3.12 us  [shards(): jnp.einsum('ptes,esd->ptd', stacked[0], returned_small, preferred_element...]
    all_to_all x1, waiting for transfers between devices: 129 us -> 125 us  [shards(): lax.all_to_all(answered, 'expert', split_axis=0, concat_axis=0, tiled=True)]
  transfers between devices with their start and end apart: 1 -> 1, of which waited for: 1 -> 1; matrix products, arithmetic and copies ran while one was open for 1% -> 2% of each run, Pallas kernels for 0% -> 0%
where the time goes in v10:
time: 336 us
  blocking collectives  140 us (42%)
  waiting for transfers between devices  125 us (37%)
  Pallas kernels  49 us (15%)
  other arithmetic  7.61 us (2%)
  matrix products  6.49 us (2%)
  starting transfers between devices  5 us (1%)
    all_to_all x1, blocking collectives, shards(): lax.all_to_all(outgoing, 'expert', split_axis=0, concat_axis=0, tiled=True)  140 us
    all_to_all x1, waiting for transfers between devices, shards(): lax.all_to_all(answered, 'expert', split_axis=0, concat_axis=0, tiled=True)  125 us
    pallas_call x1, Pallas kernels, expert_blocks(): pl.pallas_call(functools.partial(ffn_kernel, n), out_shape=(jax.ShapeDtyp...  40.8 us
    pallas_call x1, Pallas kernels, combine(): pl.pallas_call(combine_kernel, out_shape=jax.ShapeDtypeStruct((tokens, fe...  8.2 us
  transfers between devices with their start and end apart: 1, of which 1 were waited for; matrix products, arithmetic and copies ran while one was open for 2% of the time, Pallas kernels for 0%

profile of v10, /device:TPU:0, one launch (start us, length us, event | category | flops | bytes accessed | tf_op | source)
XLA Modules:
  0.0 335.7 jit_solution(8443879388093343098)
XLA Ops:
  0.0 0.0 copy-start
  0.0 0.9 copy.36
  0.9 0.1 eq.49
  1.0 0.1 eq.45
  1.2 1.7 reduce-window.6
  2.9 0.3 slice_reduce_fusion
  3.2 0.1 fusion.9
  3.3 0.1 reduce_sum.57
  3.4 0.1 copy.39
  3.5 0.7 multiply_add_fusion.1
  4.2 1.5 fusion.17
  5.7 0.0 copy-done
  5.7 3.4 %convolution_convert_fusion = bf16[32,72,2560]{2,1,0:T(8,128)(2,1)S(1)} fusion(pred[128,32,72]{0,2,1:T(8,128)(4,1)S(1)} %get-tuple-element.13, bf16[128,2560]{1,0:T(8,128)(2,1)S(1)} %copy-done), kind=kOutput, calls=%fused_computation | convolution fusion | flops 1515847680 | bytes 12746752 | tf_op jit(solution)/shard_map/tes,td->esd/dot_general | solution.py:180
  9.1 139.8 %all_to_all.10.small_ref.large_ref = bf16[32,72,2560]{2,1,0:T(8,128)(2,1)} all-to-all(bf16[32,72,2560]{2,1,0:T(8,128)(2,1)S(1)} %convolution_convert_fusion), channel_id=1, replica_groups=mesh['dp'=4,'expert'=32] {'expert'}, dimensions={0} | all-to-all | bytes 23592960 | tf_op jit(solution)/shard_map/all_to_all | solution.py:183
  148.9 40.8 %shard_map.64 = (bf16[32,64,2560]{2,1,0:T(8,128)(2,1)}, bf16[32,8,2560]{2,1,0:T(8,128)(2,1)}) custom-call(bf16[32,72,2560]{2,1,0:T(8,128)(2,1)} %all_to_all.10.small_ref.large_ref, bf16[32,72,2560]{2,1,0:T(8,128)(2,1)} %all_to_all.10.small_ref.large_ref, bf16[2560,768]{1,0:T(8,128)(2,1)} %bitcast.45, bf16[2560,768]{1,0:T(8,128)(2,1)} %bitcast.46, ...), custom_call_target="tpu_custom_call" | custom-call | flops 27179089920 | bytes 35389440 | tf_op jit(solution)/shard_map/pallas_call | solution.py:84
  189.7 0.0 copy-start.1
  189.7 5.0 %all-to-all-start.1 = ((bf16[32,64,2560]{2,1,0:T(8,128)(2,1)}), bf16[32,64,2560]{2,1,0:T(8,128)(2,1)}, u32[]{:S(2)}, u32[]{:S(2)}) async-start(bf16[32,64,2560]{2,1,0:T(8,128)(2,1)} %get-tuple-element.7), calls=%async_computation.1 | async-start | bytes 20971520 | tf_op jit(solution)/shard_map/all_to_all | solution.py:187
  194.7 0.0 copy-done.1
  194.7 1.3 select_reduce_fusion.1
  196.0 1.0 copy.40
  197.0 0.2 copy.41
  197.2 0.2 select_reduce_fusion.3
  197.4 2.1 pad_maximum_fusion.weights_ref
  199.5 3.1 fusion.partial_ref
  202.7 124.9 %all-to-all-done.1 = bf16[32,64,2560]{2,1,0:T(8,128)(2,1)} async-done(((bf16[32,64,2560]{2,1,0:T(8,128)(2,1)}), bf16[32,64,2560]{2,1,0:T(8,128)(2,1)}, u32[]{:S(2)}, u32[]{:S(2)}) %all-to-all-start.1) | async-done | bytes 10485792 | tf_op jit(solution)/shard_map/all_to_all | solution.py:187
  327.5 8.2 %shard_map.65 = bf16[128,2560]{1,0:T(8,128)(2,1)} custom-call(bf16[2,128,2048]{2,1,0:T(8,128)(2,1)} %pad_maximum_fusion.weights_ref, bf16[2048,2560]{1,0:T(8,128)(2,1)} %bitcast.7.returned_ref, f32[128,2560]{1,0:T(8,128)} %fusion.partial_ref), custom_call_target="tpu_custom_call" | custom-call | flops 2684354560 | bytes 12451840 | tf_op jit(solution)/shard_map/pallas_call | solution.py:131
  (5 shorter events, 0.1 us)
Async XLA Ops:
  0.0 5.7 %copy-start = (bf16[128,2560]{1,0:T(8,128)(2,1)S(1)}, bf16[128,2560]{1,0:T(8,128)(2,1)}, u32[]{:S(2)}) copy-start(bf16[128,2560]{1,0:T(8,128)(2,1)} %param.6) | copy-start | bytes 1966084
  189.7 5.0 %copy-start.1 = (f32[128,6]{0,1:T(8,128)S(1)}, f32[128,6]{0,1:T(8,128)}, u32[]{:S(2)}) copy-start(f32[128,6]{0,1:T(8,128)} %param.8) | copy-start | bytes 9220
  189.7 137.8 %all-to-all-start.1 = ((bf16[32,64,2560]{2,1,0:T(8,128)(2,1)}), bf16[32,64,2560]{2,1,0:T(8,128)(2,1)}, u32[]{:S(2)}, u32[]{:S(2)}) async-start(bf16[32,64,2560]{2,1,0:T(8,128)(2,1)} %get-tuple-element.7), calls=%async_computation.1 | async-start | bytes 20971520 | tf_op jit(solution)/shard_map/all_to_all | solution.py:187

commit v11 on v9

--- a/solution.py
+++ b/solution.py
@@ -137,10 +137,13 @@
 
     flat_ids = expert_ids.reshape(-1)
     one_hot = (flat_ids[:, None] == jnp.arange(experts_all, dtype=jnp.int32)[None, :]).astype(
-        jnp.int32
+        jnp.bfloat16
     )
-    earlier = jnp.cumsum(one_hot, axis=0) - one_hot
-    slot_of = jnp.sum(earlier * one_hot, axis=1)
+    pair_count = flat_ids.shape[0]
+    pair_index = jnp.arange(pair_count, dtype=jnp.int32)
+    before = (pair_index[:, None] > pair_index[None, :]).astype(jnp.bfloat16)
+    earlier = jnp.dot(before, one_hot, preferred_element_type=jnp.float32)
+    slot_of = jnp.sum(earlier * one_hot.astype(jnp.float32), axis=1).astype(jnp.int32)
     places = (flat_ids * slot_bound + slot_of).reshape(token_count, topk_width)
 
     hit = (

time: 336 us -> 334 us (level)
  no operation moved by 1% of the time
where the time goes in v11:
time: 334 us
  blocking collectives  140 us (42%)
  waiting for transfers between devices  130 us (39%)
  Pallas kernels  40.8 us (12%)
  matrix products  11.3 us (3%)
  starting transfers between devices  5.18 us (2%)
  other arithmetic  4.63 us (1%)
    all_to_all x1, blocking collectives, shards(): lax.all_to_all(outgoing, 'expert', split_axis=0, concat_axis=0, tiled=True)  140 us
    all_to_all x1, waiting for transfers between devices, shards(): lax.all_to_all(answered, 'expert', split_axis=0, concat_axis=0, tiled=True)  130 us
    pallas_call x1, Pallas kernels, expert_blocks(): pl.pallas_call(functools.partial(ffn_kernel, n), out_shape=(jax.ShapeDtyp...  40.8 us
    dot_general x2, matrix products, shards(): jnp.einsum('ptes,esd->ptd', stacked, returned, preferred_element_type=jnp...  7.56 us
  transfers between devices with their start and end apart: 1, of which 1 were waited for; matrix products, arithmetic and copies ran while one was open for 1% of the time, Pallas kernels for 0%

profile of v11, /device:TPU:0, one launch (start us, length us, event | category | flops | bytes accessed | tf_op | source)
XLA Modules:
  0.0 333.5 jit_solution(14261881005706933855)
XLA Ops:
  0.0 0.0 copy-start
  0.0 0.9 copy.28
  0.9 0.1 eq.35
  1.0 0.4 fusion.13
  1.4 0.1 convert_element_type.41
  1.5 0.1 copy.29
  1.6 0.7 multiply_add_fusion.1
  2.3 1.5 broadcast_compare_fusion
  3.8 0.0 copy-done
  3.8 3.4 %convolution_convert_fusion = bf16[32,72,2560]{2,1,0:T(8,128)(2,1)S(1)} fusion(pred[128,32,72]{0,2,1:T(8,128)(4,1)S(1)} %get-tuple-element.14, bf16[128,2560]{1,0:T(8,128)(2,1)S(1)} %copy-done), kind=kOutput, calls=%fused_computation.2 | convolution fusion | flops 1515847680 | bytes 12746752 | tf_op jit(solution)/shard_map/tes,td->esd/dot_general | solution.py:153
  7.2 139.8 %all_to_all.10.small_ref.large_ref = bf16[32,72,2560]{2,1,0:T(8,128)(2,1)} all-to-all(bf16[32,72,2560]{2,1,0:T(8,128)(2,1)S(1)} %convolution_convert_fusion), channel_id=1, replica_groups=mesh['dp'=4,'expert'=32] {'expert'}, dimensions={0} | all-to-all | bytes 23592960 | tf_op jit(solution)/shard_map/all_to_all | solution.py:156
  147.0 40.8 %shard_map.64 = (bf16[32,64,2560]{2,1,0:T(8,128)(2,1)}, bf16[32,8,2560]{2,1,0:T(8,128)(2,1)}) custom-call(bf16[32,72,2560]{2,1,0:T(8,128)(2,1)} %all_to_all.10.small_ref.large_ref, bf16[32,72,2560]{2,1,0:T(8,128)(2,1)} %all_to_all.10.small_ref.large_ref, bf16[2560,768]{1,0:T(8,128)(2,1)} %bitcast.39, bf16[2560,768]{1,0:T(8,128)(2,1)} %bitcast.40, ...), custom_call_target="tpu_custom_call" | custom-call | flops 27179089920 | bytes 35389440 | tf_op jit(solution)/shard_map/pallas_call | solution.py:84
  187.8 0.0 copy-start.2
  187.8 5.2 %all-to-all-start.1 = ((bf16[32,64,2560]{2,1,0:T(8,128)(2,1)}), bf16[32,64,2560]{2,1,0:T(8,128)(2,1)}, u32[]{:S(2)}, u32[]{:S(2)}) async-start(bf16[32,64,2560]{2,1,0:T(8,128)(2,1)} %get-tuple-element.8), calls=%async_computation.1 | async-start | bytes 20971520 | tf_op jit(solution)/shard_map/all_to_all | solution.py:160
  193.0 0.0 copy-done.2
  193.0 0.0 copy-start.1
  193.0 0.2 select_reduce_fusion.3
  193.2 1.3 select_reduce_fusion.1
  194.5 0.0 copy-done.1
  194.5 0.6 fusion.6
  195.1 130.5 %all-to-all-done.1 = bf16[32,64,2560]{2,1,0:T(8,128)(2,1)} async-done(((bf16[32,64,2560]{2,1,0:T(8,128)(2,1)}), bf16[32,64,2560]{2,1,0:T(8,128)(2,1)}, u32[]{:S(2)}, u32[]{:S(2)}) %all-to-all-start.1) | async-done | bytes 10485792 | tf_op jit(solution)/shard_map/all_to_all | solution.py:160
  325.6 6.9 %fusion.7 = f32[128,2560]{1,0:T(8,128)S(1)} fusion(bf16[32,64,2560]{2,1,0:T(8,128)(2,1)} %all-to-all-done.1, bf16[1,128,32,64]{1,3,2,0:T(8,128)(2,1)S(1)} %bitcast.38, bf16[1,128,32,64]{1,3,2,0:T(8,128)(2,1)S(1)} %bitcast.37), kind=kOutput, calls=%fused_computation.11 | convolution fusion | flops 2685206528 | bytes 12845056 | tf_op jit(solution)/shard_map/ptes,esd->ptd/dot_general | solution.py:175
  332.5 1.0 add_convert_fusion
  (4 shorter events, 0.0 us)
Async XLA Ops:
  0.0 3.8 %copy-start = (bf16[128,2560]{1,0:T(8,128)(2,1)S(1)}, bf16[128,2560]{1,0:T(8,128)(2,1)}, u32[]{:S(2)}) copy-start(bf16[128,2560]{1,0:T(8,128)(2,1)} %param.6) | copy-start | bytes 1966084
  187.8 5.2 %copy-start.2 = (f32[128,6]{0,1:T(8,128)S(1)}, f32[128,6]{0,1:T(8,128)}, u32[]{:S(2)}) copy-start(f32[128,6]{0,1:T(8,128)} %param.8) | copy-start | bytes 9220
  187.8 137.8 %all-to-all-start.1 = ((bf16[32,64,2560]{2,1,0:T(8,128)(2,1)}), bf16[32,64,2560]{2,1,0:T(8,128)(2,1)}, u32[]{:S(2)}, u32[]{:S(2)}) async-start(bf16[32,64,2560]{2,1,0:T(8,128)(2,1)} %get-tuple-element.8), calls=%async_computation.1 | async-start | bytes 20971520 | tf_op jit(solution)/shard_map/all_to_all | solution.py:160
  193.0 1.5 copy-start.1

commit v12 on v11

--- a/solution.py
+++ b/solution.py
@@ -18,8 +18,8 @@
 
 
 def ffn_kernel(
-    n, small_ref, large_ref, gate_ref, up_ref, down_ref, large_out, small_out,
-    held, send_sem, recv_sem, local_sem,
+    n, small_ref, large_ref, gate_hbm, up_hbm, down_hbm, large_out, small_out,
+    held, gate_ref, up_ref, down_ref, send_sem, recv_sem, local_sem, weight_sem,
 ):
     step = pl.program_id(0)
     me = lax.axis_index("expert")
@@ -44,8 +44,17 @@
         remote(k).wait()
         return carry
 
+    fetches = [
+        pltpu.make_async_copy(source, target, weight_sem.at[index])
+        for index, (source, target) in enumerate(
+            ((gate_hbm, gate_ref), (up_hbm, up_ref), (down_hbm, down_ref))
+        )
+    ]
+
     @pl.when(step == 0)
     def _():
+        for fetch in fetches:
+            fetch.start()
         barrier = pltpu.get_barrier_semaphore()
 
         def greet(k, carry):
@@ -58,8 +67,16 @@
         pl.semaphore_wait(barrier, n - 1)
         sources, slots, features = small_ref.shape
         rows = small_ref[...].reshape(sources * slots, features)
-        held[...] = expert_apply(rows, gate_ref[...], up_ref[...], down_ref[...]).reshape(
-            sources, slots, features
+        fetches[0].wait()
+        gate_part = jnp.dot(rows, gate_ref[...], preferred_element_type=jnp.float32)
+        fetches[1].wait()
+        up_part = jnp.dot(rows, up_ref[...], preferred_element_type=jnp.float32)
+        hidden = (jax.nn.silu(gate_part) * up_part).astype(jnp.bfloat16)
+        fetches[2].wait()
+        held[...] = (
+            jnp.dot(hidden, down_ref[...], preferred_element_type=jnp.float32)
+            .astype(jnp.bfloat16)
+            .reshape(sources, slots, features)
         )
         local.start()
         lax.fori_loop(1, n, start, 0)
@@ -91,9 +108,9 @@
         in_specs=[
             pl.BlockSpec((sources, small, features), lambda i: (0, large // small, 0)),
             pl.BlockSpec((per_step, large, features), lambda i: (i, 0, 0)),
-            pl.BlockSpec((features, hidden), lambda i: (0, 0)),
-            pl.BlockSpec((features, hidden), lambda i: (0, 0)),
-            pl.BlockSpec((hidden, features), lambda i: (0, 0)),
+            pl.BlockSpec(memory_space=pl.ANY),
+            pl.BlockSpec(memory_space=pl.ANY),
+            pl.BlockSpec(memory_space=pl.ANY),
         ],
         out_specs=(
             pl.BlockSpec((per_step, large, features), lambda i: (i, 0, 0)),
@@ -101,9 +118,13 @@
         ),
         scratch_shapes=[
             pltpu.VMEM((sources, small, features), received.dtype),
+            pltpu.VMEM(gate_matrix.shape, gate_matrix.dtype),
+            pltpu.VMEM(up_matrix.shape, up_matrix.dtype),
+            pltpu.VMEM(down_matrix.shape, down_matrix.dtype),
             pltpu.SemaphoreType.DMA((n,)),
             pltpu.SemaphoreType.DMA((n,)),
             pltpu.SemaphoreType.DMA,
+            pltpu.SemaphoreType.DMA((3,)),
         ],
         compiler_params=pltpu.CompilerParams(
             collective_id=0, has_side_effects=True, vmem_limit_bytes=60 * 1024 * 1024

time: 334 us -> 331 us (level)
  no operation moved by 1% of the time
where the time goes in v12:
time: 331 us
  blocking collectives  140 us (42%)
  waiting for transfers between devices  130 us (39%)
  Pallas kernels  38.4 us (12%)
  matrix products  11.3 us (3%)
  starting transfers between devices  5.18 us (2%)
  other arithmetic  4.63 us (1%)
    all_to_all x1, blocking collectives, shards(): lax.all_to_all(outgoing, 'expert', split_axis=0, concat_axis=0, tiled=True)  140 us
    all_to_all x1, waiting for transfers between devices, shards(): lax.all_to_all(answered, 'expert', split_axis=0, concat_axis=0, tiled=True)  130 us
    pallas_call x1, Pallas kernels, expert_blocks(): pl.pallas_call(functools.partial(ffn_kernel, n), out_shape=(jax.ShapeDtyp...  38.4 us
    dot_general x2, matrix products, shards(): jnp.einsum('ptes,esd->ptd', stacked, returned, preferred_element_type=jnp...  7.56 us
  transfers between devices with their start and end apart: 1, of which 1 were waited for; matrix products, arithmetic and copies ran while one was open for 1% of the time, Pallas kernels for 0%

profile of v12, /device:TPU:0, one launch (start us, length us, event | category | flops | bytes accessed | tf_op | source)
XLA Modules:
  0.0 331.2 jit_solution(5629989432860547438)
XLA Ops:
  0.0 0.0 copy-start
  0.0 0.9 copy.28
  0.9 0.1 eq.35
  1.0 0.4 fusion.13
  1.4 0.1 convert_element_type.41
  1.5 0.1 copy.29
  1.6 0.7 multiply_add_fusion.1
  2.3 1.5 broadcast_compare_fusion
  3.8 0.0 copy-done
  3.8 3.4 %convolution_convert_fusion = bf16[32,72,2560]{2,1,0:T(8,128)(2,1)S(1)} fusion(pred[128,32,72]{0,2,1:T(8,128)(4,1)S(1)} %get-tuple-element.14, bf16[128,2560]{1,0:T(8,128)(2,1)S(1)} %copy-done), kind=kOutput, calls=%fused_computation.2 | convolution fusion | flops 1515847680 | bytes 12746752 | tf_op jit(solution)/shard_map/tes,td->esd/dot_general | solution.py:174
  7.2 139.8 %all_to_all.10.small_ref.large_ref = bf16[32,72,2560]{2,1,0:T(8,128)(2,1)} all-to-all(bf16[32,72,2560]{2,1,0:T(8,128)(2,1)S(1)} %convolution_convert_fusion), channel_id=1, replica_groups=mesh['dp'=4,'expert'=32] {'expert'}, dimensions={0} | all-to-all | bytes 23592960 | tf_op jit(solution)/shard_map/all_to_all | solution.py:177
  147.0 38.4 %shard_map.64 = (bf16[32,64,2560]{2,1,0:T(8,128)(2,1)}, bf16[32,8,2560]{2,1,0:T(8,128)(2,1)}) custom-call(bf16[32,72,2560]{2,1,0:T(8,128)(2,1)} %all_to_all.10.small_ref.large_ref, bf16[32,72,2560]{2,1,0:T(8,128)(2,1)} %all_to_all.10.small_ref.large_ref, bf16[2560,768]{1,0:T(8,128)(2,1)} %bitcast.39, bf16[2560,768]{1,0:T(8,128)(2,1)} %bitcast.40, ...), custom_call_target="tpu_custom_call" | custom-call | flops 27179089920 | bytes 35389440 | tf_op jit(solution)/shard_map/pallas_call | solution.py:101
  185.4 0.0 copy-start.2
  185.4 5.2 %all-to-all-start.1 = ((bf16[32,64,2560]{2,1,0:T(8,128)(2,1)}), bf16[32,64,2560]{2,1,0:T(8,128)(2,1)}, u32[]{:S(2)}, u32[]{:S(2)}) async-start(bf16[32,64,2560]{2,1,0:T(8,128)(2,1)} %get-tuple-element.8), calls=%async_computation.1 | async-start | bytes 20971520 | tf_op jit(solution)/shard_map/all_to_all | solution.py:181
  190.6 0.0 copy-done.2
  190.6 0.0 copy-start.1
  190.6 0.2 select_reduce_fusion.3
  190.8 1.3 select_reduce_fusion.1
  192.1 0.0 copy-done.1
  192.1 0.6 fusion.6
  192.7 130.5 %all-to-all-done.1 = bf16[32,64,2560]{2,1,0:T(8,128)(2,1)} async-done(((bf16[32,64,2560]{2,1,0:T(8,128)(2,1)}), bf16[32,64,2560]{2,1,0:T(8,128)(2,1)}, u32[]{:S(2)}, u32[]{:S(2)}) %all-to-all-start.1) | async-done | bytes 10485792 | tf_op jit(solution)/shard_map/all_to_all | solution.py:181
  323.2 6.9 %fusion.7 = f32[128,2560]{1,0:T(8,128)S(1)} fusion(bf16[32,64,2560]{2,1,0:T(8,128)(2,1)} %all-to-all-done.1, bf16[1,128,32,64]{1,3,2,0:T(8,128)(2,1)S(1)} %bitcast.38, bf16[1,128,32,64]{1,3,2,0:T(8,128)(2,1)S(1)} %bitcast.37), kind=kOutput, calls=%fused_computation.11 | convolution fusion | flops 2685206528 | bytes 12845056 | tf_op jit(solution)/shard_map/ptes,esd->ptd/dot_general | solution.py:196
  330.2 1.0 add_convert_fusion
  (4 shorter events, 0.0 us)
Async XLA Ops:
  0.0 3.8 %copy-start = (bf16[128,2560]{1,0:T(8,128)(2,1)S(1)}, bf16[128,2560]{1,0:T(8,128)(2,1)}, u32[]{:S(2)}) copy-start(bf16[128,2560]{1,0:T(8,128)(2,1)} %param.6) | copy-start | bytes 1966084
  185.4 5.2 %copy-start.2 = (f32[128,6]{0,1:T(8,128)S(1)}, f32[128,6]{0,1:T(8,128)}, u32[]{:S(2)}) copy-start(f32[128,6]{0,1:T(8,128)} %param.8) | copy-start | bytes 9220
  185.4 137.8 %all-to-all-start.1 = ((bf16[32,64,2560]{2,1,0:T(8,128)(2,1)}), bf16[32,64,2560]{2,1,0:T(8,128)(2,1)}, u32[]{:S(2)}, u32[]{:S(2)}) async-start(bf16[32,64,2560]{2,1,0:T(8,128)(2,1)} %get-tuple-element.8), calls=%async_computation.1 | async-start | bytes 20971520 | tf_op jit(solution)/shard_map/all_to_all | solution.py:181
  190.6 1.5 copy-start.1

commit v13 on v12

--- a/solution.py
+++ b/solution.py
@@ -177,7 +177,7 @@
     received = lax.all_to_all(outgoing, "expert", split_axis=0, concat_axis=0, tiled=True)
 
     large = slot_bound - slot_bound // 9
-    answered, returned_small = expert_blocks(received, w_gate[0], w_up[0], w_down[0], large, 4)
+    answered, returned_small = expert_blocks(received, w_gate[0], w_up[0], w_down[0], large, 8)
     returned_large = lax.all_to_all(answered, "expert", split_axis=0, concat_axis=0, tiled=True)
     weight_parts = split_bf16(gate_values)
     summed = None

time: 331 us -> 332 us (level)
  no operation moved by 1% of the time
where the time goes in v13:
time: 332 us; the launch traced here: 331 us
  blocking collectives  140 us (42%)
  waiting for transfers between devices  130 us (39%)
  Pallas kernels  38.5 us (12%)
  matrix products  11.3 us (3%)
  starting transfers between devices  5.18 us (2%)
  other arithmetic  4.63 us (1%)
    all_to_all x1, blocking collectives, shards(): lax.all_to_all(outgoing, 'expert', split_axis=0, concat_axis=0, tiled=True)  140 us
    all_to_all x1, waiting for transfers between devices, shards(): lax.all_to_all(answered, 'expert', split_axis=0, concat_axis=0, tiled=True)  130 us
    pallas_call x1, Pallas kernels, expert_blocks(): pl.pallas_call(functools.partial(ffn_kernel, n), out_shape=(jax.ShapeDtyp...  38.5 us
    dot_general x2, matrix products, shards(): jnp.einsum('ptes,esd->ptd', stacked, returned, preferred_element_type=jnp...  7.56 us
  transfers between devices with their start and end apart: 1, of which 1 were waited for; matrix products, arithmetic and copies ran while one was open for 1% of the time, Pallas kernels for 0%

profile of v13, /device:TPU:0, one launch (start us, length us, event | category | flops | bytes accessed | tf_op | source)
XLA Modules:
  0.0 331.2 jit_solution(2149633481778193372)
XLA Ops:
  0.0 0.0 copy-start
  0.0 0.9 copy.28
  0.9 0.1 eq.35
  1.0 0.4 fusion.13
  1.4 0.1 convert_element_type.41
  1.5 0.1 copy.29
  1.6 0.7 multiply_add_fusion.1
  2.3 1.5 broadcast_compare_fusion
  3.8 0.0 copy-done
  3.8 3.4 %convolution_convert_fusion = bf16[32,72,2560]{2,1,0:T(8,128)(2,1)S(1)} fusion(pred[128,32,72]{0,2,1:T(8,128)(4,1)S(1)} %get-tuple-element.14, bf16[128,2560]{1,0:T(8,128)(2,1)S(1)} %copy-done), kind=kOutput, calls=%fused_computation.2 | convolution fusion | flops 1515847680 | bytes 12746752 | tf_op jit(solution)/shard_map/tes,td->esd/dot_general | solution.py:174
  7.2 139.8 %all_to_all.10.small_ref.large_ref = bf16[32,72,2560]{2,1,0:T(8,128)(2,1)} all-to-all(bf16[32,72,2560]{2,1,0:T(8,128)(2,1)S(1)} %convolution_convert_fusion), channel_id=1, replica_groups=mesh['dp'=4,'expert'=32] {'expert'}, dimensions={0} | all-to-all | bytes 23592960 | tf_op jit(solution)/shard_map/all_to_all | solution.py:177
  147.0 38.5 %shard_map.64 = (bf16[32,64,2560]{2,1,0:T(8,128)(2,1)}, bf16[32,8,2560]{2,1,0:T(8,128)(2,1)}) custom-call(bf16[32,72,2560]{2,1,0:T(8,128)(2,1)} %all_to_all.10.small_ref.large_ref, bf16[32,72,2560]{2,1,0:T(8,128)(2,1)} %all_to_all.10.small_ref.large_ref, bf16[2560,768]{1,0:T(8,128)(2,1)} %bitcast.39, bf16[2560,768]{1,0:T(8,128)(2,1)} %bitcast.40, ...), custom_call_target="tpu_custom_call" | custom-call | flops 27179089920 | bytes 35389440 | tf_op jit(solution)/shard_map/pallas_call | solution.py:101
  185.4 0.0 copy-start.2
  185.5 5.2 %all-to-all-start.1 = ((bf16[32,64,2560]{2,1,0:T(8,128)(2,1)}), bf16[32,64,2560]{2,1,0:T(8,128)(2,1)}, u32[]{:S(2)}, u32[]{:S(2)}) async-start(bf16[32,64,2560]{2,1,0:T(8,128)(2,1)} %get-tuple-element.8), calls=%async_computation.1 | async-start | bytes 20971520 | tf_op jit(solution)/shard_map/all_to_all | solution.py:181
  190.7 0.0 copy-done.2
  190.7 0.0 copy-start.1
  190.7 0.2 select_reduce_fusion.3
  190.9 1.3 select_reduce_fusion.1
  192.1 0.0 copy-done.1
  192.2 0.6 fusion.6
  192.8 130.5 %all-to-all-done.1 = bf16[32,64,2560]{2,1,0:T(8,128)(2,1)} async-done(((bf16[32,64,2560]{2,1,0:T(8,128)(2,1)}), bf16[32,64,2560]{2,1,0:T(8,128)(2,1)}, u32[]{:S(2)}, u32[]{:S(2)}) %all-to-all-start.1) | async-done | bytes 10485792 | tf_op jit(solution)/shard_map/all_to_all | solution.py:181
  323.3 6.9 %fusion.7 = f32[128,2560]{1,0:T(8,128)S(1)} fusion(bf16[32,64,2560]{2,1,0:T(8,128)(2,1)} %all-to-all-done.1, bf16[1,128,32,64]{1,3,2,0:T(8,128)(2,1)S(1)} %bitcast.38, bf16[1,128,32,64]{1,3,2,0:T(8,128)(2,1)S(1)} %bitcast.37), kind=kOutput, calls=%fused_computation.11 | convolution fusion | flops 2685206528 | bytes 12845056 | tf_op jit(solution)/shard_map/ptes,esd->ptd/dot_general | solution.py:196
  330.2 1.0 add_convert_fusion
  (4 shorter events, 0.0 us)
Async XLA Ops:
  0.0 3.8 %copy-start = (bf16[128,2560]{1,0:T(8,128)(2,1)S(1)}, bf16[128,2560]{1,0:T(8,128)(2,1)}, u32[]{:S(2)}) copy-start(bf16[128,2560]{1,0:T(8,128)(2,1)} %param.6) | copy-start | bytes 1966084
  185.4 5.2 %copy-start.2 = (f32[128,6]{0,1:T(8,128)S(1)}, f32[128,6]{0,1:T(8,128)}, u32[]{:S(2)}) copy-start(f32[128,6]{0,1:T(8,128)} %param.8) | copy-start | bytes 9220
  185.5 137.8 %all-to-all-start.1 = ((bf16[32,64,2560]{2,1,0:T(8,128)(2,1)}), bf16[32,64,2560]{2,1,0:T(8,128)(2,1)}, u32[]{:S(2)}, u32[]{:S(2)}) async-start(bf16[32,64,2560]{2,1,0:T(8,128)(2,1)} %get-tuple-element.8), calls=%async_computation.1 | async-start | bytes 20971520 | tf_op jit(solution)/shard_map/all_to_all | solution.py:181
  190.7 1.5 copy-start.1

commit v14 on v12

--- a/solution.py
+++ b/solution.py
@@ -176,7 +176,7 @@
     ).astype(jnp.bfloat16)
     received = lax.all_to_all(outgoing, "expert", split_axis=0, concat_axis=0, tiled=True)
 
-    large = slot_bound - slot_bound // 9
+    large = slot_bound - slot_bound // 3
     answered, returned_small = expert_blocks(received, w_gate[0], w_up[0], w_down[0], large, 4)
     returned_large = lax.all_to_all(answered, "expert", split_axis=0, concat_axis=0, tiled=True)
     weight_parts = split_bf16(gate_values)

time: 331 us -> 340 us (1.027)
  Pallas kernels: 38.4 us -> 81.8 us
  waiting for transfers between devices: 130 us -> 93.7 us
    pallas_call x1, Pallas kernels: 38.4 us -> 81.8 us  [expert_blocks(): pl.pallas_call(functools.partial(ffn_kernel, n), out_shape=(jax.ShapeDtyp...]
    all_to_all x1, waiting for transfers between devices: 130 us -> 93.7 us  [shards(): lax.all_to_all(answered, 'expert', split_axis=0, concat_axis=0, tiled=True)]
where the time goes in v14:
time: 340 us
  blocking collectives  140 us (41%)
  waiting for transfers between devices  93.7 us (28%)
  Pallas kernels  81.8 us (24%)
  matrix products  12.8 us (4%)
  starting transfers between devices  6.03 us (2%)
  other arithmetic  4.58 us (1%)
    all_to_all x1, blocking collectives, shards(): lax.all_to_all(outgoing, 'expert', split_axis=0, concat_axis=0, tiled=True)  140 us
    all_to_all x1, waiting for transfers between devices, shards(): lax.all_to_all(answered, 'expert', split_axis=0, concat_axis=0, tiled=True)  93.7 us
    pallas_call x1, Pallas kernels, expert_blocks(): pl.pallas_call(functools.partial(ffn_kernel, n), out_shape=(jax.ShapeDtyp...  81.8 us
    dot_general x2, matrix products, shards(): jnp.einsum('ptes,esd->ptd', stacked, returned, preferred_element_type=jnp...  9.11 us
  transfers between devices with their start and end apart: 1, of which 1 were waited for; matrix products, arithmetic and copies ran while one was open for 1% of the time, Pallas kernels for 0%

profile of v14, /device:TPU:0, one launch (start us, length us, event | category | flops | bytes accessed | tf_op | source)
XLA Modules:
  0.0 340.2 jit_solution(4061556406583298040)
XLA Ops:
  0.0 0.0 copy-start
  0.0 0.9 copy.28
  0.9 0.1 eq.35
  1.0 0.4 fusion.15
  1.4 0.1 convert_element_type.41
  1.5 0.1 copy.29
  1.6 0.7 multiply_add_fusion.1
  2.3 1.5 broadcast_compare_fusion
  3.8 0.0 copy-done
  3.8 3.4 convolution_convert_fusion
  7.2 139.8 %all_to_all.10.small_ref.large_ref = bf16[32,72,2560]{2,1,0:T(8,128)(2,1)} all-to-all(bf16[32,72,2560]{2,1,0:T(8,128)(2,1)S(1)} %convolution_convert_fusion), channel_id=1, replica_groups=mesh['dp'=4,'expert'=32] {'expert'}, dimensions={0} | all-to-all | bytes 23592960 | tf_op jit(solution)/shard_map/all_to_all | solution.py:177
  147.0 81.8 %shard_map.64 = (bf16[32,48,2560]{2,1,0:T(8,128)(2,1)}, bf16[32,24,2560]{2,1,0:T(8,128)(2,1)}) custom-call(bf16[32,72,2560]{2,1,0:T(8,128)(2,1)} %all_to_all.10.small_ref.large_ref, bf16[32,72,2560]{2,1,0:T(8,128)(2,1)} %all_to_all.10.small_ref.large_ref, bf16[2560,768]{1,0:T(8,128)(2,1)} %bitcast.41, bf16[2560,768]{1,0:T(8,128)(2,1)} %bitcast.42, ...), custom_call_target="tpu_custom_call" | custom-call | flops 27179089920 | bytes 35389440 | tf_op jit(solution)/shard_map/pallas_call | solution.py:101
  228.8 0.0 copy-start.1
  228.8 6.0 %all-to-all-start.1 = ((bf16[32,48,2560]{2,1,0:T(8,128)(2,1)}), bf16[32,48,2560]{2,1,0:T(8,128)(2,1)}, u32[]{:S(2)}, u32[]{:S(2)}) async-start(bf16[32,48,2560]{2,1,0:T(8,128)(2,1)} %get-tuple-element.8), calls=%async_computation.1 | async-start | bytes 15728640 | tf_op jit(solution)/shard_map/all_to_all | solution.py:181
  234.8 0.0 copy-done.1
  234.9 0.5 select_reduce_fusion.3
  235.3 0.1 fusion.23
  235.4 0.9 select_reduce_fusion.1
  236.3 3.6 %fusion.11 = f32[128,2560]{1,0:T(8,128)S(1)} fusion(bf16[32,24,2560]{2,1,0:T(8,128)(2,1)} %get-tuple-element.7, bf16[1,128,32,24]{1,2,3,0:T(8,128)(2,1)S(1)} %get-tuple-element.18, bf16[1,128,32,24]{1,2,3,0:T(8,128)(2,1)S(1)} %get-tuple-element.17), kind=kOutput, calls=%fused_computation.15 | convolution fusion | flops 1007157248 | bytes 5636096 | tf_op jit(solution)/shard_map/ptes,esd->ptd/dot_general | solution.py:196
  239.9 93.7 %all-to-all-done.1 = bf16[32,48,2560]{2,1,0:T(8,128)(2,1)} async-done(((bf16[32,48,2560]{2,1,0:T(8,128)(2,1)}), bf16[32,48,2560]{2,1,0:T(8,128)(2,1)}, u32[]{:S(2)}, u32[]{:S(2)}) %all-to-all-start.1) | async-done | bytes 7864352 | tf_op jit(solution)/shard_map/all_to_all | solution.py:181
  333.7 5.5 %fusion.8 = f32[128,2560]{1,0:T(8,128)S(1)} fusion(bf16[32,48,2560]{2,1,0:T(8,128)(2,1)} %all-to-all-done.1, bf16[1,128,32,48]{1,3,2,0:T(8,128)(2,1)S(1)} %bitcast.40, bf16[1,128,32,48]{1,3,2,0:T(8,128)(2,1)S(1)} %bitcast.39), kind=kOutput, calls=%fused_computation.14 | convolution fusion | flops 2013986816 | bytes 9961472 | tf_op jit(solution)/shard_map/ptes,esd->ptd/dot_general | solution.py:196
  339.2 1.0 add_convert_fusion
  (3 shorter events, 0.0 us)
Async XLA Ops:
  0.0 3.8 %copy-start = (bf16[128,2560]{1,0:T(8,128)(2,1)S(1)}, bf16[128,2560]{1,0:T(8,128)(2,1)}, u32[]{:S(2)}) copy-start(bf16[128,2560]{1,0:T(8,128)(2,1)} %param.6) | copy-start | bytes 1966084
  228.8 6.0 %copy-start.1 = (f32[128,6]{0,1:T(8,128)S(1)}, f32[128,6]{0,1:T(8,128)}, u32[]{:S(2)}) copy-start(f32[128,6]{0,1:T(8,128)} %param.8) | copy-start | bytes 9220
  228.8 104.9 %all-to-all-start.1 = ((bf16[32,48,2560]{2,1,0:T(8,128)(2,1)}), bf16[32,48,2560]{2,1,0:T(8,128)(2,1)}, u32[]{:S(2)}, u32[]{:S(2)}) async-start(bf16[32,48,2560]{2,1,0:T(8,128)(2,1)} %get-tuple-element.8), calls=%async_computation.1 | async-start | bytes 15728640 | tf_op jit(solution)/shard_map/all_to_all | solution.py:181

commit v15 on v12

--- a/solution.py
+++ b/solution.py
@@ -55,16 +55,6 @@
     def _():
         for fetch in fetches:
             fetch.start()
-        barrier = pltpu.get_barrier_semaphore()
-
-        def greet(k, carry):
-            pl.semaphore_signal(
-                barrier, inc=1, device_id={"expert": lax.rem(me + k, n)}, device_id_type=MESH
-            )
-            return carry
-
-        lax.fori_loop(1, n, greet, 0)
-        pl.semaphore_wait(barrier, n - 1)
         sources, slots, features = small_ref.shape
         rows = small_ref[...].reshape(sources * slots, features)
         fetches[0].wait()
@@ -79,6 +69,16 @@
             .reshape(sources, slots, features)
         )
         local.start()
+        barrier = pltpu.get_barrier_semaphore()
+
+        def greet(k, carry):
+            pl.semaphore_signal(
+                barrier, inc=1, device_id={"expert": lax.rem(me + k, n)}, device_id_type=MESH
+            )
+            return carry
+
+        lax.fori_loop(1, n, greet, 0)
+        pl.semaphore_wait(barrier, n - 1)
         lax.fori_loop(1, n, start, 0)
 
     sources, slots, features = large_ref.shape

time: 331 us -> 333 us (level)
  no operation moved by 1% of the time
where the time goes in v15:
time: 333 us
  blocking collectives  140 us (42%)
  waiting for transfers between devices  130 us (39%)
  Pallas kernels  40.3 us (12%)
  matrix products  11.3 us (3%)
  starting transfers between devices  5.18 us (2%)
  other arithmetic  4.63 us (1%)
    all_to_all x1, blocking collectives, shards(): lax.all_to_all(outgoing, 'expert', split_axis=0, concat_axis=0, tiled=True)  140 us
    all_to_all x1, waiting for transfers between devices, shards(): lax.all_to_all(answered, 'expert', split_axis=0, concat_axis=0, tiled=True)  130 us
    pallas_call x1, Pallas kernels, expert_blocks(): pl.pallas_call(functools.partial(ffn_kernel, n), out_shape=(jax.ShapeDtyp...  40.3 us
    dot_general x2, matrix products, shards(): jnp.einsum('ptes,esd->ptd', stacked, returned, preferred_element_type=jnp...  7.56 us
  transfers between devices with their start and end apart: 1, of which 1 were waited for; matrix products, arithmetic and copies ran while one was open for 1% of the time, Pallas kernels for 0%

profile of v15, /device:TPU:0, one launch (start us, length us, event | category | flops | bytes accessed | tf_op | source)
XLA Modules:
  0.0 333.0 jit_solution(10202103687572357511)
XLA Ops:
  0.0 0.0 copy-start
  0.0 0.9 copy.28
  0.9 0.1 eq.35
  1.0 0.4 fusion.13
  1.4 0.1 convert_element_type.41
  1.5 0.1 copy.29
  1.6 0.7 multiply_add_fusion.1
  2.3 1.5 broadcast_compare_fusion
  3.8 0.0 copy-done
  3.8 3.4 %convolution_convert_fusion = bf16[32,72,2560]{2,1,0:T(8,128)(2,1)S(1)} fusion(pred[128,32,72]{0,2,1:T(8,128)(4,1)S(1)} %get-tuple-element.14, bf16[128,2560]{1,0:T(8,128)(2,1)S(1)} %copy-done), kind=kOutput, calls=%fused_computation.2 | convolution fusion | flops 1515847680 | bytes 12746752 | tf_op jit(solution)/shard_map/tes,td->esd/dot_general | solution.py:174
  7.2 139.8 %all_to_all.10.small_ref.large_ref = bf16[32,72,2560]{2,1,0:T(8,128)(2,1)} all-to-all(bf16[32,72,2560]{2,1,0:T(8,128)(2,1)S(1)} %convolution_convert_fusion), channel_id=1, replica_groups=mesh['dp'=4,'expert'=32] {'expert'}, dimensions={0} | all-to-all | bytes 23592960 | tf_op jit(solution)/shard_map/all_to_all | solution.py:177
  147.0 40.3 %shard_map.64 = (bf16[32,64,2560]{2,1,0:T(8,128)(2,1)}, bf16[32,8,2560]{2,1,0:T(8,128)(2,1)}) custom-call(bf16[32,72,2560]{2,1,0:T(8,128)(2,1)} %all_to_all.10.small_ref.large_ref, bf16[32,72,2560]{2,1,0:T(8,128)(2,1)} %all_to_all.10.small_ref.large_ref, bf16[2560,768]{1,0:T(8,128)(2,1)} %bitcast.39, bf16[2560,768]{1,0:T(8,128)(2,1)} %bitcast.40, ...), custom_call_target="tpu_custom_call" | custom-call | flops 27179089920 | bytes 35389440 | tf_op jit(solution)/shard_map/pallas_call | solution.py:101
  187.2 0.0 copy-start.2
  187.3 5.2 %all-to-all-start.1 = ((bf16[32,64,2560]{2,1,0:T(8,128)(2,1)}), bf16[32,64,2560]{2,1,0:T(8,128)(2,1)}, u32[]{:S(2)}, u32[]{:S(2)}) async-start(bf16[32,64,2560]{2,1,0:T(8,128)(2,1)} %get-tuple-element.8), calls=%async_computation.1 | async-start | bytes 20971520 | tf_op jit(solution)/shard_map/all_to_all | solution.py:181
  192.4 0.0 copy-done.2
  192.5 0.0 copy-start.1
  192.5 0.2 select_reduce_fusion.3
  192.7 1.3 select_reduce_fusion.1
  193.9 0.0 copy-done.1
  193.9 0.6 fusion.6
  194.6 130.5 %all-to-all-done.1 = bf16[32,64,2560]{2,1,0:T(8,128)(2,1)} async-done(((bf16[32,64,2560]{2,1,0:T(8,128)(2,1)}), bf16[32,64,2560]{2,1,0:T(8,128)(2,1)}, u32[]{:S(2)}, u32[]{:S(2)}) %all-to-all-start.1) | async-done | bytes 10485792 | tf_op jit(solution)/shard_map/all_to_all | solution.py:181
  325.1 6.9 %fusion.7 = f32[128,2560]{1,0:T(8,128)S(1)} fusion(bf16[32,64,2560]{2,1,0:T(8,128)(2,1)} %all-to-all-done.1, bf16[1,128,32,64]{1,3,2,0:T(8,128)(2,1)S(1)} %bitcast.38, bf16[1,128,32,64]{1,3,2,0:T(8,128)(2,1)S(1)} %bitcast.37), kind=kOutput, calls=%fused_computation.11 | convolution fusion | flops 2685206528 | bytes 12845056 | tf_op jit(solution)/shard_map/ptes,esd->ptd/dot_general | solution.py:196
  332.0 1.0 add_convert_fusion
  (4 shorter events, 0.0 us)
Async XLA Ops:
  0.0 3.8 %copy-start = (bf16[128,2560]{1,0:T(8,128)(2,1)S(1)}, bf16[128,2560]{1,0:T(8,128)(2,1)}, u32[]{:S(2)}) copy-start(bf16[128,2560]{1,0:T(8,128)(2,1)} %param.6) | copy-start | bytes 1966084
  187.2 5.2 %copy-start.2 = (f32[128,6]{0,1:T(8,128)S(1)}, f32[128,6]{0,1:T(8,128)}, u32[]{:S(2)}) copy-start(f32[128,6]{0,1:T(8,128)} %param.8) | copy-start | bytes 9220
  187.3 137.8 %all-to-all-start.1 = ((bf16[32,64,2560]{2,1,0:T(8,128)(2,1)}), bf16[32,64,2560]{2,1,0:T(8,128)(2,1)}, u32[]{:S(2)}, u32[]{:S(2)}) async-start(bf16[32,64,2560]{2,1,0:T(8,128)(2,1)} %get-tuple-element.8), calls=%async_computation.1 | async-start | bytes 20971520 | tf_op jit(solution)/shard_map/all_to_all | solution.py:181
  192.5 1.5 copy-start.1

commit v16 on v12

--- a/solution.py
+++ b/solution.py
@@ -19,7 +19,7 @@
 
 def ffn_kernel(
     n, small_ref, large_ref, gate_hbm, up_hbm, down_hbm, large_out, small_out,
-    held, gate_ref, up_ref, down_ref, send_sem, recv_sem, local_sem, weight_sem,
+    held, gate_up_ref, down_ref, send_sem, recv_sem, local_sem, weight_sem,
 ):
     step = pl.program_id(0)
     me = lax.axis_index("expert")
@@ -44,12 +44,25 @@
         remote(k).wait()
         return carry
 
+    hidden = down_ref.shape[0]
     fetches = [
         pltpu.make_async_copy(source, target, weight_sem.at[index])
         for index, (source, target) in enumerate(
-            ((gate_hbm, gate_ref), (up_hbm, up_ref), (down_hbm, down_ref))
+            (
+                (gate_hbm, gate_up_ref.at[:, pl.ds(0, hidden)]),
+                (up_hbm, gate_up_ref.at[:, pl.ds(hidden, hidden)]),
+                (down_hbm, down_ref),
+            )
         )
     ]
+
+    def apply(rows):
+        both = jnp.dot(rows, gate_up_ref[...], preferred_element_type=jnp.float32)
+        gate_part, up_part = both[:, :hidden], both[:, hidden:]
+        mixed = (jax.nn.silu(gate_part) * up_part).astype(jnp.bfloat16)
+        return jnp.dot(mixed, down_ref[...], preferred_element_type=jnp.float32).astype(
+            jnp.bfloat16
+        )
 
     @pl.when(step == 0)
     def _():
@@ -67,25 +80,15 @@
         pl.semaphore_wait(barrier, n - 1)
         sources, slots, features = small_ref.shape
         rows = small_ref[...].reshape(sources * slots, features)
-        fetches[0].wait()
-        gate_part = jnp.dot(rows, gate_ref[...], preferred_element_type=jnp.float32)
-        fetches[1].wait()
-        up_part = jnp.dot(rows, up_ref[...], preferred_element_type=jnp.float32)
-        hidden = (jax.nn.silu(gate_part) * up_part).astype(jnp.bfloat16)
-        fetches[2].wait()
-        held[...] = (
-            jnp.dot(hidden, down_ref[...], preferred_element_type=jnp.float32)
-            .astype(jnp.bfloat16)
-            .reshape(sources, slots, features)
-        )
+        for fetch in fetches:
+            fetch.wait()
+        held[...] = apply(rows).reshape(sources, slots, features)
         local.start()
         lax.fori_loop(1, n, start, 0)
 
     sources, slots, features = large_ref.shape
     rows = large_ref[...].reshape(sources * slots, features)
-    large_out[...] = expert_apply(rows, gate_ref[...], up_ref[...], down_ref[...]).reshape(
-        sources, slots, features
-    )
+    large_out[...] = apply(rows).reshape(sources, slots, features)
 
     @pl.when(step == pl.num_programs(0) - 1)
     def _():
@@ -118,8 +121,7 @@
         ),
         scratch_shapes=[
             pltpu.VMEM((sources, small, features), received.dtype),
-            pltpu.VMEM(gate_matrix.shape, gate_matrix.dtype),
-            pltpu.VMEM(up_matrix.shape, up_matrix.dtype),
+            pltpu.VMEM((features, 2 * hidden), gate_matrix.dtype),
             pltpu.VMEM(down_matrix.shape, down_matrix.dtype),
             pltpu.SemaphoreType.DMA((n,)),
             pltpu.SemaphoreType.DMA((n,)),

time: 331 us -> 332 us (level)
  no operation moved by 1% of the time
where the time goes in v16:
time: 332 us; the launch traced here: 331 us
  blocking collectives  140 us (42%)
  waiting for transfers between devices  130 us (39%)
  Pallas kernels  37.7 us (11%)
  matrix products  11.3 us (3%)
  starting transfers between devices  6.05 us (2%)
  other arithmetic  4.63 us (1%)
    all_to_all x1, blocking collectives, shards(): lax.all_to_all(outgoing, 'expert', split_axis=0, concat_axis=0, tiled=True)  140 us
    all_to_all x1, waiting for transfers between devices, shards(): lax.all_to_all(answered, 'expert', split_axis=0, concat_axis=0, tiled=True)  130 us
    pallas_call x1, Pallas kernels, expert_blocks(): pl.pallas_call(functools.partial(ffn_kernel, n), out_shape=(jax.ShapeDtyp...  37.7 us
    dot_general x2, matrix products, shards(): jnp.einsum('ptes,esd->ptd', stacked, returned, preferred_element_type=jnp...  7.56 us
  transfers between devices with their start and end apart: 1, of which 1 were waited for; matrix products, arithmetic and copies ran while one was open for 1% of the time, Pallas kernels for 0%

profile of v16, /device:TPU:0, one launch (start us, length us, event | category | flops | bytes accessed | tf_op | source)
XLA Modules:
  0.0 331.3 jit_solution(4241477151410829900)
XLA Ops:
  0.0 0.0 copy-start
  0.0 0.9 copy.28
  0.9 0.1 eq.35
  1.0 0.4 fusion.13
  1.4 0.1 convert_element_type.41
  1.5 0.1 copy.29
  1.6 0.7 multiply_add_fusion.1
  2.3 1.5 broadcast_compare_fusion
  3.8 0.0 copy-done
  3.8 3.4 %convolution_convert_fusion = bf16[32,72,2560]{2,1,0:T(8,128)(2,1)S(1)} fusion(pred[128,32,72]{0,2,1:T(8,128)(4,1)S(1)} %get-tuple-element.14, bf16[128,2560]{1,0:T(8,128)(2,1)S(1)} %copy-done), kind=kOutput, calls=%fused_computation.2 | convolution fusion | flops 1515847680 | bytes 12746752 | tf_op jit(solution)/shard_map/tes,td->esd/dot_general | solution.py:176
  7.2 139.8 %all_to_all.10.small_ref.large_ref = bf16[32,72,2560]{2,1,0:T(8,128)(2,1)} all-to-all(bf16[32,72,2560]{2,1,0:T(8,128)(2,1)S(1)} %convolution_convert_fusion), channel_id=1, replica_groups=mesh['dp'=4,'expert'=32] {'expert'}, dimensions={0} | all-to-all | bytes 23592960 | tf_op jit(solution)/shard_map/all_to_all | solution.py:179
  147.0 37.7 %shard_map.64 = (bf16[32,64,2560]{2,1,0:T(8,128)(2,1)}, bf16[32,8,2560]{2,1,0:T(8,128)(2,1)}) custom-call(bf16[32,72,2560]{2,1,0:T(8,128)(2,1)} %all_to_all.10.small_ref.large_ref, bf16[32,72,2560]{2,1,0:T(8,128)(2,1)} %all_to_all.10.small_ref.large_ref, bf16[2560,768]{1,0:T(8,128)(2,1)} %bitcast.39, bf16[2560,768]{1,0:T(8,128)(2,1)} %bitcast.40, ...), custom_call_target="tpu_custom_call" | custom-call | flops 27179089920 | bytes 35389440 | tf_op jit(solution)/shard_map/pallas_call | solution.py:104
  184.7 0.0 copy-start.2
  184.7 6.1 %all-to-all-start.1 = ((bf16[32,64,2560]{2,1,0:T(8,128)(2,1)}), bf16[32,64,2560]{2,1,0:T(8,128)(2,1)}, u32[]{:S(2)}, u32[]{:S(2)}) async-start(bf16[32,64,2560]{2,1,0:T(8,128)(2,1)} %get-tuple-element.8), calls=%async_computation.1 | async-start | bytes 20971520 | tf_op jit(solution)/shard_map/all_to_all | solution.py:183
  190.7 0.0 copy-done.2
  190.7 0.0 copy-start.1
  190.8 0.2 select_reduce_fusion.3
  191.0 1.3 select_reduce_fusion.1
  192.2 0.0 copy-done.1
  192.2 0.6 fusion.6
  192.9 130.4 %all-to-all-done.1 = bf16[32,64,2560]{2,1,0:T(8,128)(2,1)} async-done(((bf16[32,64,2560]{2,1,0:T(8,128)(2,1)}), bf16[32,64,2560]{2,1,0:T(8,128)(2,1)}, u32[]{:S(2)}, u32[]{:S(2)}) %all-to-all-start.1) | async-done | bytes 10485792 | tf_op jit(solution)/shard_map/all_to_all | solution.py:183
  323.3 6.9 %fusion.7 = f32[128,2560]{1,0:T(8,128)S(1)} fusion(bf16[32,64,2560]{2,1,0:T(8,128)(2,1)} %all-to-all-done.1, bf16[1,128,32,64]{1,3,2,0:T(8,128)(2,1)S(1)} %bitcast.38, bf16[1,128,32,64]{1,3,2,0:T(8,128)(2,1)S(1)} %bitcast.37), kind=kOutput, calls=%fused_computation.11 | convolution fusion | flops 2685206528 | bytes 12845056 | tf_op jit(solution)/shard_map/ptes,esd->ptd/dot_general | solution.py:198
  330.3 1.0 add_convert_fusion
  (4 shorter events, 0.0 us)
Async XLA Ops:
  0.0 3.8 %copy-start = (bf16[128,2560]{1,0:T(8,128)(2,1)S(1)}, bf16[128,2560]{1,0:T(8,128)(2,1)}, u32[]{:S(2)}) copy-start(bf16[128,2560]{1,0:T(8,128)(2,1)} %param.6) | copy-start | bytes 1966084
  184.7 6.1 %copy-start.2 = (f32[128,6]{0,1:T(8,128)S(1)}, f32[128,6]{0,1:T(8,128)}, u32[]{:S(2)}) copy-start(f32[128,6]{0,1:T(8,128)} %param.8) | copy-start | bytes 9220
  184.7 138.6 %all-to-all-start.1 = ((bf16[32,64,2560]{2,1,0:T(8,128)(2,1)}), bf16[32,64,2560]{2,1,0:T(8,128)(2,1)}, u32[]{:S(2)}, u32[]{:S(2)}) async-start(bf16[32,64,2560]{2,1,0:T(8,128)(2,1)} %get-tuple-element.8), calls=%async_computation.1 | async-start | bytes 20971520 | tf_op jit(solution)/shard_map/all_to_all | solution.py:183
  190.7 1.5 copy-start.1

commit v17 on v16

--- a/solution.py
+++ b/solution.py
@@ -182,13 +182,18 @@
     answered, returned_small = expert_blocks(received, w_gate[0], w_up[0], w_down[0], large, 4)
     returned_large = lax.all_to_all(answered, "expert", split_axis=0, concat_axis=0, tiled=True)
     weight_parts = split_bf16(gate_values)
+    experts = jnp.arange(experts_all, dtype=jnp.int32)
+    slots = slot_of.reshape(token_count, topk_width)
     summed = None
     for begin, end, returned in ((large, slot_bound, returned_small), (0, large, returned_large)):
         stacked = jnp.stack(
             [
                 jnp.sum(
                     jnp.where(
-                        hit[:, :, :, begin:end], part.astype(jnp.float32)[:, :, None, None], 0.0
+                        (expert_ids[:, :, None, None] == experts[None, None, :, None])
+                        & (slots[:, :, None, None] == jnp.arange(begin, end)[None, None, None, :]),
+                        part.astype(jnp.float32)[:, :, None, None],
+                        0.0,
                     ),
                     axis=1,
                 )

time: 332 us -> 331 us (level)
  no operation moved by 1% of the time
where the time goes in v17:
time: 331 us
  blocking collectives  140 us (42%)
  waiting for transfers between devices  129 us (39%)
  Pallas kernels  37.7 us (11%)
  matrix products  12.7 us (4%)
  starting transfers between devices  6.05 us (2%)
  other arithmetic  4.49 us (1%)
    all_to_all x1, blocking collectives, shards(): lax.all_to_all(outgoing, 'expert', split_axis=0, concat_axis=0, tiled=True)  140 us
    all_to_all x1, waiting for transfers between devices, shards(): lax.all_to_all(answered, 'expert', split_axis=0, concat_axis=0, tiled=True)  129 us
    pallas_call x1, Pallas kernels, expert_blocks(): pl.pallas_call(functools.partial(ffn_kernel, n), out_shape=(jax.ShapeDtyp...  37.7 us
    dot_general x2, matrix products, shards(): jnp.einsum('ptes,esd->ptd', stacked, returned, preferred_element_type=jnp...  8.98 us
  transfers between devices with their start and end apart: 1, of which 1 were waited for; matrix products, arithmetic and copies ran while one was open for 1% of the time, Pallas kernels for 0%

profile of v17, /device:TPU:0, one launch (start us, length us, event | category | flops | bytes accessed | tf_op | source)
XLA Modules:
  0.0 330.9 jit_solution(17659544515430158984)
XLA Ops:
  0.0 0.0 copy-start
  0.0 0.9 copy.34
  0.9 0.1 eq.57
  1.0 0.4 fusion.15
  1.4 0.1 convert_element_type.45
  1.5 0.1 copy.35
  1.6 0.7 multiply_add_fusion.1
  2.3 1.1 compare_reduce_fusion
  3.4 0.0 copy-done
  3.4 3.4 %convolution_convert_fusion = bf16[32,72,2560]{2,1,0:T(8,128)(2,1)S(1)} fusion(pred[128,32,72]{0,2,1:T(8,128)(4,1)S(1)} %compare_reduce_fusion, bf16[128,2560]{1,0:T(8,128)(2,1)S(1)} %copy-done), kind=kOutput, calls=%fused_computation.2 | convolution fusion | flops 1515847680 | bytes 12746752 | tf_op jit(solution)/shard_map/tes,td->esd/dot_general | solution.py:176
  6.8 139.8 %all_to_all.10.small_ref.large_ref = bf16[32,72,2560]{2,1,0:T(8,128)(2,1)} all-to-all(bf16[32,72,2560]{2,1,0:T(8,128)(2,1)S(1)} %convolution_convert_fusion), channel_id=1, replica_groups=mesh['dp'=4,'expert'=32] {'expert'}, dimensions={0} | all-to-all | bytes 23592960 | tf_op jit(solution)/shard_map/all_to_all | solution.py:179
  146.6 37.7 %shard_map.64 = (bf16[32,64,2560]{2,1,0:T(8,128)(2,1)}, bf16[32,8,2560]{2,1,0:T(8,128)(2,1)}) custom-call(bf16[32,72,2560]{2,1,0:T(8,128)(2,1)} %all_to_all.10.small_ref.large_ref, bf16[32,72,2560]{2,1,0:T(8,128)(2,1)} %all_to_all.10.small_ref.large_ref, bf16[2560,768]{1,0:T(8,128)(2,1)} %bitcast.39, bf16[2560,768]{1,0:T(8,128)(2,1)} %bitcast.40, ...), custom_call_target="tpu_custom_call" | custom-call | flops 27179089920 | bytes 35389440 | tf_op jit(solution)/shard_map/pallas_call | solution.py:104
  184.3 0.0 copy-start.2
  184.3 0.0 copy-start.1
  184.3 6.1 %all-to-all-start.1 = ((bf16[32,64,2560]{2,1,0:T(8,128)(2,1)}), bf16[32,64,2560]{2,1,0:T(8,128)(2,1)}, u32[]{:S(2)}, u32[]{:S(2)}) async-start(bf16[32,64,2560]{2,1,0:T(8,128)(2,1)} %get-tuple-element.8), calls=%async_computation.1 | async-start | bytes 20971520 | tf_op jit(solution)/shard_map/all_to_all | solution.py:183
  190.4 0.1 broadcast_compare_fusion
  190.4 0.0 copy-done.2
  190.4 0.0 copy-done.1
  190.5 0.2 fusion.19
  190.8 1.3 fusion.2
  192.1 2.0 fusion.8
  194.1 128.8 %all-to-all-done.1 = bf16[32,64,2560]{2,1,0:T(8,128)(2,1)} async-done(((bf16[32,64,2560]{2,1,0:T(8,128)(2,1)}), bf16[32,64,2560]{2,1,0:T(8,128)(2,1)}, u32[]{:S(2)}, u32[]{:S(2)}) %all-to-all-start.1) | async-done | bytes 10485792 | tf_op jit(solution)/shard_map/all_to_all | solution.py:183
  322.9 6.9 %fusion.9 = f32[128,2560]{1,0:T(8,128)S(1)} fusion(bf16[32,64,2560]{2,1,0:T(8,128)(2,1)} %all-to-all-done.1, bf16[1,128,32,64]{1,3,2,0:T(8,128)(2,1)S(1)} %bitcast.38, bf16[1,128,32,64]{1,3,2,0:T(8,128)(2,1)S(1)} %bitcast.37), kind=kOutput, calls=%fused_computation.13 | convolution fusion | flops 2685206528 | bytes 12845056 | tf_op jit(solution)/shard_map/ptes,esd->ptd/dot_general | solution.py:203
  329.9 1.0 add_convert_fusion
  (7 shorter events, 0.1 us)
Async XLA Ops:
  0.0 3.4 %copy-start = (bf16[128,2560]{1,0:T(8,128)(2,1)S(1)}, bf16[128,2560]{1,0:T(8,128)(2,1)}, u32[]{:S(2)}) copy-start(bf16[128,2560]{1,0:T(8,128)(2,1)} %param.6) | copy-start | bytes 1966084
  184.3 6.2 %copy-start.2 = (f32[128,6]{0,1:T(8,128)S(1)}, f32[128,6]{0,1:T(8,128)}, u32[]{:S(2)}) copy-start(f32[128,6]{0,1:T(8,128)} %param.8) | copy-start | bytes 9220
  184.3 6.2 %copy-start.1 = (s32[128,6]{0,1:T(8,128)S(1)}, s32[128,6]{0,1:T(8,128)}, u32[]{:S(2)}) copy-start(s32[128,6]{0,1:T(8,128)} %param.7) | copy-start | bytes 9220
  184.3 138.6 %all-to-all-start.1 = ((bf16[32,64,2560]{2,1,0:T(8,128)(2,1)}), bf16[32,64,2560]{2,1,0:T(8,128)(2,1)}, u32[]{:S(2)}, u32[]{:S(2)}) async-start(bf16[32,64,2560]{2,1,0:T(8,128)(2,1)} %get-tuple-element.8), calls=%async_computation.1 | async-start | bytes 20971520 | tf_op jit(solution)/shard_map/all_to_all | solution.py:183

commit v18 on v17

--- a/solution.py
+++ b/solution.py
@@ -158,7 +158,7 @@
     slot_bound = max(favoured_bound, other_bound)
     buffer_rows = experts_all * slot_bound
 
-    flat_ids = expert_ids.reshape(-1)
+    flat_ids = expert_ids.T.reshape(-1)
     one_hot = (flat_ids[:, None] == jnp.arange(experts_all, dtype=jnp.int32)[None, :]).astype(
         jnp.bfloat16
     )
@@ -167,7 +167,8 @@
     before = (pair_index[:, None] > pair_index[None, :]).astype(jnp.bfloat16)
     earlier = jnp.dot(before, one_hot, preferred_element_type=jnp.float32)
     slot_of = jnp.sum(earlier * one_hot.astype(jnp.float32), axis=1).astype(jnp.int32)
-    places = (flat_ids * slot_bound + slot_of).reshape(token_count, topk_width)
+    places = (flat_ids * slot_bound + slot_of).reshape(topk_width, token_count).T
+    slot_of = slot_of.reshape(topk_width, token_count).T
 
     hit = (
         places[:, :, None] == jnp.arange(buffer_rows, dtype=jnp.int32)[None, None, :]
@@ -183,7 +184,7 @@
     returned_large = lax.all_to_all(answered, "expert", split_axis=0, concat_axis=0, tiled=True)
     weight_parts = split_bf16(gate_values)
     experts = jnp.arange(experts_all, dtype=jnp.int32)
-    slots = slot_of.reshape(token_count, topk_width)
+    slots = slot_of
     summed = None
     for begin, end, returned in ((large, slot_bound, returned_small), (0, large, returned_large)):
         stacked = jnp.stack(

time: 331 us -> 331 us (level)
  no operation moved by 1% of the time
where the time goes in v18:
time: 331 us; the launch traced here: 330 us
  blocking collectives  140 us (42%)
  waiting for transfers between devices  129 us (39%)
  Pallas kernels  37.7 us (11%)
  matrix products  13.5 us (4%)
  starting transfers between devices  5.87 us (2%)
  other arithmetic  4.47 us (1%)
    all_to_all x1, blocking collectives, shards(): lax.all_to_all(outgoing, 'expert', split_axis=0, concat_axis=0, tiled=True)  140 us
    all_to_all x1, waiting for transfers between devices, shards(): lax.all_to_all(answered, 'expert', split_axis=0, concat_axis=0, tiled=True)  129 us
    pallas_call x1, Pallas kernels, expert_blocks(): pl.pallas_call(functools.partial(ffn_kernel, n), out_shape=(jax.ShapeDtyp...  37.7 us
    dot_general x2, matrix products, shards(): jnp.einsum('ptes,esd->ptd', stacked, returned, preferred_element_type=jnp...  8.98 us
  transfers between devices with their start and end apart: 1, of which 1 were waited for; matrix products, arithmetic and copies ran while one was open for 1% of the time, Pallas kernels for 0%

profile of v18, /device:TPU:0, one launch (start us, length us, event | category | flops | bytes accessed | tf_op | source)
XLA Modules:
  0.0 330.4 jit_solution(1963537576066346893)
XLA Ops:
  0.0 0.0 copy-start
  0.0 1.1 fusion.15
  1.1 0.7 fusion.30
  1.8 1.1 compare_reduce_fusion
  2.9 0.0 copy-done
  2.9 3.4 %convolution_convert_fusion = bf16[32,72,2560]{2,1,0:T(8,128)(2,1)S(1)} fusion(pred[128,32,72]{0,2,1:T(8,128)(4,1)S(1)} %compare_reduce_fusion, bf16[128,2560]{1,0:T(8,128)(2,1)S(1)} %copy-done), kind=kOutput, calls=%fused_computation.2 | convolution fusion | flops 1515847680 | bytes 12746752 | tf_op jit(solution)/shard_map/tes,td->esd/dot_general | solution.py:177
  6.3 139.8 %all_to_all.10.small_ref.large_ref = bf16[32,72,2560]{2,1,0:T(8,128)(2,1)} all-to-all(bf16[32,72,2560]{2,1,0:T(8,128)(2,1)S(1)} %convolution_convert_fusion), channel_id=1, replica_groups=mesh['dp'=4,'expert'=32] {'expert'}, dimensions={0} | all-to-all | bytes 23592960 | tf_op jit(solution)/shard_map/all_to_all | solution.py:180
  146.1 37.7 %shard_map.64 = (bf16[32,64,2560]{2,1,0:T(8,128)(2,1)}, bf16[32,8,2560]{2,1,0:T(8,128)(2,1)}) custom-call(bf16[32,72,2560]{2,1,0:T(8,128)(2,1)} %all_to_all.10.small_ref.large_ref, bf16[32,72,2560]{2,1,0:T(8,128)(2,1)} %all_to_all.10.small_ref.large_ref, bf16[2560,768]{1,0:T(8,128)(2,1)} %bitcast.55, bf16[2560,768]{1,0:T(8,128)(2,1)} %bitcast.56, ...), custom_call_target="tpu_custom_call" | custom-call | flops 27179089920 | bytes 35389440 | tf_op jit(solution)/shard_map/pallas_call | solution.py:104
  183.8 0.0 copy-start.2
  183.8 0.0 copy-start.1
  183.8 5.9 %all-to-all-start.1 = ((bf16[32,64,2560]{2,1,0:T(8,128)(2,1)}), bf16[32,64,2560]{2,1,0:T(8,128)(2,1)}, u32[]{:S(2)}, u32[]{:S(2)}) async-start(bf16[32,64,2560]{2,1,0:T(8,128)(2,1)} %get-tuple-element.8), calls=%async_computation.1 | async-start | bytes 20971520 | tf_op jit(solution)/shard_map/all_to_all | solution.py:184
  189.7 0.1 broadcast_compare_fusion
  189.8 0.0 copy-done.2
  189.8 0.0 copy-done.1
  189.8 0.2 fusion.19
  190.1 1.3 fusion.2
  191.5 2.0 fusion.8
  193.5 128.9 %all-to-all-done.1 = bf16[32,64,2560]{2,1,0:T(8,128)(2,1)} async-done(((bf16[32,64,2560]{2,1,0:T(8,128)(2,1)}), bf16[32,64,2560]{2,1,0:T(8,128)(2,1)}, u32[]{:S(2)}, u32[]{:S(2)}) %all-to-all-start.1) | async-done | bytes 10485792 | tf_op jit(solution)/shard_map/all_to_all | solution.py:184
  322.4 6.9 %fusion.9 = f32[128,2560]{1,0:T(8,128)S(1)} fusion(bf16[32,64,2560]{2,1,0:T(8,128)(2,1)} %all-to-all-done.1, bf16[1,128,32,64]{1,3,2,0:T(8,128)(2,1)S(1)} %bitcast.53, bf16[1,128,32,64]{1,3,2,0:T(8,128)(2,1)S(1)} %bitcast.52), kind=kOutput, calls=%fused_computation.13 | convolution fusion | flops 2685206528 | bytes 12845056 | tf_op jit(solution)/shard_map/ptes,esd->ptd/dot_general | solution.py:204
  329.4 1.0 add_convert_fusion
  (7 shorter events, 0.1 us)
Async XLA Ops:
  0.0 2.9 copy-start
  183.8 6.0 %copy-start.2 = (f32[128,6]{0,1:T(8,128)S(1)}, f32[128,6]{0,1:T(8,128)}, u32[]{:S(2)}) copy-start(f32[128,6]{0,1:T(8,128)} %param.8) | copy-start | bytes 9220
  183.8 6.0 %copy-start.1 = (s32[128,6]{0,1:T(8,128)S(1)}, s32[128,6]{0,1:T(8,128)}, u32[]{:S(2)}) copy-start(s32[128,6]{0,1:T(8,128)} %param.7) | copy-start | bytes 9220
  183.8 138.6 %all-to-all-start.1 = ((bf16[32,64,2560]{2,1,0:T(8,128)(2,1)}), bf16[32,64,2560]{2,1,0:T(8,128)(2,1)}, u32[]{:S(2)}, u32[]{:S(2)}) async-start(bf16[32,64,2560]{2,1,0:T(8,128)(2,1)} %get-tuple-element.8), calls=%async_computation.1 | async-start | bytes 20971520 | tf_op jit(solution)/shard_map/all_to_all | solution.py:184

commit v19 on v18

--- a/solution.py
+++ b/solution.py
@@ -180,7 +180,7 @@
     received = lax.all_to_all(outgoing, "expert", split_axis=0, concat_axis=0, tiled=True)
 
     large = slot_bound - slot_bound // 9
-    answered, returned_small = expert_blocks(received, w_gate[0], w_up[0], w_down[0], large, 4)
+    answered, returned_small = expert_blocks(received, w_gate[0], w_up[0], w_down[0], large, 8)
     returned_large = lax.all_to_all(answered, "expert", split_axis=0, concat_axis=0, tiled=True)
     weight_parts = split_bf16(gate_values)
     experts = jnp.arange(experts_all, dtype=jnp.int32)

time: 331 us -> 331 us (level)
  no operation moved by 1% of the time
where the time goes in v19:
time: 331 us
  blocking collectives  140 us (42%)
  waiting for transfers between devices  129 us (39%)
  Pallas kernels  37.8 us (11%)
  matrix products  13.5 us (4%)
  starting transfers between devices  6.05 us (2%)
  other arithmetic  4.47 us (1%)
    all_to_all x1, blocking collectives, shards(): lax.all_to_all(outgoing, 'expert', split_axis=0, concat_axis=0, tiled=True)  140 us
    all_to_all x1, waiting for transfers between devices, shards(): lax.all_to_all(answered, 'expert', split_axis=0, concat_axis=0, tiled=True)  129 us
    pallas_call x1, Pallas kernels, expert_blocks(): pl.pallas_call(functools.partial(ffn_kernel, n), out_shape=(jax.ShapeDtyp...  37.8 us
    dot_general x2, matrix products, shards(): jnp.einsum('ptes,esd->ptd', stacked, returned, preferred_element_type=jnp...  8.98 us
  transfers between devices with their start and end apart: 1, of which 1 were waited for; matrix products, arithmetic and copies ran while one was open for 1% of the time, Pallas kernels for 0%

profile of v19, /device:TPU:0, one launch (start us, length us, event | category | flops | bytes accessed | tf_op | source)
XLA Modules:
  0.0 330.5 jit_solution(17831857971492565723)
XLA Ops:
  0.0 0.0 copy-start
  0.0 1.1 fusion.15
  1.1 0.7 fusion.30
  1.8 1.1 compare_reduce_fusion
  2.9 0.0 copy-done
  2.9 3.4 %convolution_convert_fusion = bf16[32,72,2560]{2,1,0:T(8,128)(2,1)S(1)} fusion(pred[128,32,72]{0,2,1:T(8,128)(4,1)S(1)} %compare_reduce_fusion, bf16[128,2560]{1,0:T(8,128)(2,1)S(1)} %copy-done), kind=kOutput, calls=%fused_computation.2 | convolution fusion | flops 1515847680 | bytes 12746752 | tf_op jit(solution)/shard_map/tes,td->esd/dot_general | solution.py:177
  6.3 139.8 %all_to_all.10.small_ref.large_ref = bf16[32,72,2560]{2,1,0:T(8,128)(2,1)} all-to-all(bf16[32,72,2560]{2,1,0:T(8,128)(2,1)S(1)} %convolution_convert_fusion), channel_id=1, replica_groups=mesh['dp'=4,'expert'=32] {'expert'}, dimensions={0} | all-to-all | bytes 23592960 | tf_op jit(solution)/shard_map/all_to_all | solution.py:180
  146.1 37.8 %shard_map.64 = (bf16[32,64,2560]{2,1,0:T(8,128)(2,1)}, bf16[32,8,2560]{2,1,0:T(8,128)(2,1)}) custom-call(bf16[32,72,2560]{2,1,0:T(8,128)(2,1)} %all_to_all.10.small_ref.large_ref, bf16[32,72,2560]{2,1,0:T(8,128)(2,1)} %all_to_all.10.small_ref.large_ref, bf16[2560,768]{1,0:T(8,128)(2,1)} %bitcast.55, bf16[2560,768]{1,0:T(8,128)(2,1)} %bitcast.56, ...), custom_call_target="tpu_custom_call" | custom-call | flops 27179089920 | bytes 35389440 | tf_op jit(solution)/shard_map/pallas_call | solution.py:104
  183.9 0.0 copy-start.2
  183.9 0.0 copy-start.1
  183.9 6.0 %all-to-all-start.1 = ((bf16[32,64,2560]{2,1,0:T(8,128)(2,1)}), bf16[32,64,2560]{2,1,0:T(8,128)(2,1)}, u32[]{:S(2)}, u32[]{:S(2)}) async-start(bf16[32,64,2560]{2,1,0:T(8,128)(2,1)} %get-tuple-element.8), calls=%async_computation.1 | async-start | bytes 20971520 | tf_op jit(solution)/shard_map/all_to_all | solution.py:184
  190.0 0.1 broadcast_compare_fusion
  190.1 0.0 copy-done.2
  190.1 0.0 copy-done.1
  190.1 0.2 fusion.19
  190.4 1.3 fusion.2
  191.7 2.0 fusion.8
  193.8 128.8 %all-to-all-done.1 = bf16[32,64,2560]{2,1,0:T(8,128)(2,1)} async-done(((bf16[32,64,2560]{2,1,0:T(8,128)(2,1)}), bf16[32,64,2560]{2,1,0:T(8,128)(2,1)}, u32[]{:S(2)}, u32[]{:S(2)}) %all-to-all-start.1) | async-done | bytes 10485792 | tf_op jit(solution)/shard_map/all_to_all | solution.py:184
  322.5 6.9 %fusion.9 = f32[128,2560]{1,0:T(8,128)S(1)} fusion(bf16[32,64,2560]{2,1,0:T(8,128)(2,1)} %all-to-all-done.1, bf16[1,128,32,64]{1,3,2,0:T(8,128)(2,1)S(1)} %bitcast.53, bf16[1,128,32,64]{1,3,2,0:T(8,128)(2,1)S(1)} %bitcast.52), kind=kOutput, calls=%fused_computation.13 | convolution fusion | flops 2685206528 | bytes 12845056 | tf_op jit(solution)/shard_map/ptes,esd->ptd/dot_general | solution.py:204
  329.5 1.0 add_convert_fusion
  (7 shorter events, 0.1 us)
Async XLA Ops:
  0.0 2.9 copy-start
  183.9 6.2 %copy-start.2 = (f32[128,6]{0,1:T(8,128)S(1)}, f32[128,6]{0,1:T(8,128)}, u32[]{:S(2)}) copy-start(f32[128,6]{0,1:T(8,128)} %param.8) | copy-start | bytes 9220
  183.9 6.2 %copy-start.1 = (s32[128,6]{0,1:T(8,128)S(1)}, s32[128,6]{0,1:T(8,128)}, u32[]{:S(2)}) copy-start(s32[128,6]{0,1:T(8,128)} %param.7) | copy-start | bytes 9220
  183.9 138.6 %all-to-all-start.1 = ((bf16[32,64,2560]{2,1,0:T(8,128)(2,1)}), bf16[32,64,2560]{2,1,0:T(8,128)(2,1)}, u32[]{:S(2)}, u32[]{:S(2)}) async-start(bf16[32,64,2560]{2,1,0:T(8,128)(2,1)} %get-tuple-element.8), calls=%async_computation.1 | async-start | bytes 20971520 | tf_op jit(solution)/shard_map/all_to_all | solution.py:184

commit v20 on v18

--- a/solution.py
+++ b/solution.py
@@ -56,10 +56,11 @@
         )
     ]
 
-    def apply(rows):
+    def apply(rows, before_down=lambda: None):
         both = jnp.dot(rows, gate_up_ref[...], preferred_element_type=jnp.float32)
         gate_part, up_part = both[:, :hidden], both[:, hidden:]
         mixed = (jax.nn.silu(gate_part) * up_part).astype(jnp.bfloat16)
+        before_down()
         return jnp.dot(mixed, down_ref[...], preferred_element_type=jnp.float32).astype(
             jnp.bfloat16
         )
@@ -80,9 +81,9 @@
         pl.semaphore_wait(barrier, n - 1)
         sources, slots, features = small_ref.shape
         rows = small_ref[...].reshape(sources * slots, features)
-        for fetch in fetches:
-            fetch.wait()
-        held[...] = apply(rows).reshape(sources, slots, features)
+        fetches[0].wait()
+        fetches[1].wait()
+        held[...] = apply(rows, fetches[2].wait).reshape(sources, slots, features)
         local.start()
         lax.fori_loop(1, n, start, 0)
 

time: 331 us -> 330 us (level)
  no operation moved by 1% of the time
where the time goes in v20:
time: 330 us; the launch traced here: 329 us
  blocking collectives  140 us (42%)
  waiting for transfers between devices  129 us (39%)
  Pallas kernels  37.5 us (11%)
  matrix products  13.5 us (4%)
  starting transfers between devices  5.08 us (2%)
  other arithmetic  4.47 us (1%)
    all_to_all x1, blocking collectives, shards(): lax.all_to_all(outgoing, 'expert', split_axis=0, concat_axis=0, tiled=True)  140 us
    all_to_all x1, waiting for transfers between devices, shards(): lax.all_to_all(answered, 'expert', split_axis=0, concat_axis=0, tiled=True)  129 us
    pallas_call x1, Pallas kernels, expert_blocks(): pl.pallas_call(functools.partial(ffn_kernel, n), out_shape=(jax.ShapeDtyp...  37.5 us
    dot_general x2, matrix products, shards(): jnp.einsum('ptes,esd->ptd', stacked, returned, preferred_element_type=jnp...  8.98 us
  transfers between devices with their start and end apart: 1, of which 1 were waited for; matrix products, arithmetic and copies ran while one was open for 1% of the time, Pallas kernels for 0%

profile of v20, /device:TPU:0, one launch (start us, length us, event | category | flops | bytes accessed | tf_op | source)
XLA Modules:
  0.0 329.5 jit_solution(575766286953602239)
XLA Ops:
  0.0 0.0 copy-start
  0.0 1.1 fusion.15
  1.1 0.7 fusion.30
  1.8 1.1 compare_reduce_fusion
  2.9 0.0 copy-done
  2.9 3.4 %convolution_convert_fusion = bf16[32,72,2560]{2,1,0:T(8,128)(2,1)S(1)} fusion(pred[128,32,72]{0,2,1:T(8,128)(4,1)S(1)} %compare_reduce_fusion, bf16[128,2560]{1,0:T(8,128)(2,1)S(1)} %copy-done), kind=kOutput, calls=%fused_computation.2 | convolution fusion | flops 1515847680 | bytes 12746752 | tf_op jit(solution)/shard_map/tes,td->esd/dot_general | solution.py:178
  6.3 139.8 %all_to_all.10.small_ref.large_ref = bf16[32,72,2560]{2,1,0:T(8,128)(2,1)} all-to-all(bf16[32,72,2560]{2,1,0:T(8,128)(2,1)S(1)} %convolution_convert_fusion), channel_id=1, replica_groups=mesh['dp'=4,'expert'=32] {'expert'}, dimensions={0} | all-to-all | bytes 23592960 | tf_op jit(solution)/shard_map/all_to_all | solution.py:181
  146.1 37.5 %shard_map.64 = (bf16[32,64,2560]{2,1,0:T(8,128)(2,1)}, bf16[32,8,2560]{2,1,0:T(8,128)(2,1)}) custom-call(bf16[32,72,2560]{2,1,0:T(8,128)(2,1)} %all_to_all.10.small_ref.large_ref, bf16[32,72,2560]{2,1,0:T(8,128)(2,1)} %all_to_all.10.small_ref.large_ref, bf16[2560,768]{1,0:T(8,128)(2,1)} %bitcast.55, bf16[2560,768]{1,0:T(8,128)(2,1)} %bitcast.56, ...), custom_call_target="tpu_custom_call" | custom-call | flops 27179089920 | bytes 35389440 | tf_op jit(solution)/shard_map/pallas_call | solution.py:105
  183.6 0.0 copy-start.2
  183.6 0.0 copy-start.1
  183.7 5.1 %all-to-all-start.1 = ((bf16[32,64,2560]{2,1,0:T(8,128)(2,1)}), bf16[32,64,2560]{2,1,0:T(8,128)(2,1)}, u32[]{:S(2)}, u32[]{:S(2)}) async-start(bf16[32,64,2560]{2,1,0:T(8,128)(2,1)} %get-tuple-element.8), calls=%async_computation.1 | async-start | bytes 20971520 | tf_op jit(solution)/shard_map/all_to_all | solution.py:185
  188.8 0.1 broadcast_compare_fusion
  188.8 0.0 copy-done.2
  188.9 0.0 copy-done.1
  188.9 0.2 fusion.19
  189.2 1.3 fusion.2
  190.5 2.0 fusion.8
  192.5 128.9 %all-to-all-done.1 = bf16[32,64,2560]{2,1,0:T(8,128)(2,1)} async-done(((bf16[32,64,2560]{2,1,0:T(8,128)(2,1)}), bf16[32,64,2560]{2,1,0:T(8,128)(2,1)}, u32[]{:S(2)}, u32[]{:S(2)}) %all-to-all-start.1) | async-done | bytes 10485792 | tf_op jit(solution)/shard_map/all_to_all | solution.py:185
  321.5 6.9 %fusion.9 = f32[128,2560]{1,0:T(8,128)S(1)} fusion(bf16[32,64,2560]{2,1,0:T(8,128)(2,1)} %all-to-all-done.1, bf16[1,128,32,64]{1,3,2,0:T(8,128)(2,1)S(1)} %bitcast.53, bf16[1,128,32,64]{1,3,2,0:T(8,128)(2,1)S(1)} %bitcast.52), kind=kOutput, calls=%fused_computation.13 | convolution fusion | flops 2685206528 | bytes 12845056 | tf_op jit(solution)/shard_map/ptes,esd->ptd/dot_general | solution.py:205
  328.4 1.0 add_convert_fusion
  (7 shorter events, 0.1 us)
Async XLA Ops:
  0.0 2.9 copy-start
  183.6 5.2 %copy-start.2 = (f32[128,6]{0,1:T(8,128)S(1)}, f32[128,6]{0,1:T(8,128)}, u32[]{:S(2)}) copy-start(f32[128,6]{0,1:T(8,128)} %param.8) | copy-start | bytes 9220
  183.6 5.2 %copy-start.1 = (s32[128,6]{0,1:T(8,128)S(1)}, s32[128,6]{0,1:T(8,128)}, u32[]{:S(2)}) copy-start(s32[128,6]{0,1:T(8,128)} %param.7) | copy-start | bytes 9220
  183.7 137.8 %all-to-all-start.1 = ((bf16[32,64,2560]{2,1,0:T(8,128)(2,1)}), bf16[32,64,2560]{2,1,0:T(8,128)(2,1)}, u32[]{:S(2)}, u32[]{:S(2)}) async-start(bf16[32,64,2560]{2,1,0:T(8,128)(2,1)} %get-tuple-element.8), calls=%async_computation.1 | async-start | bytes 20971520 | tf_op jit(solution)/shard_map/all_to_all | solution.py:185
